TPU v7x, 512 devices: a whole 4x4x16 slice. The times are simulated.
512 devices in a mesh: grp: 16 (over y_lo, x, core), ep: 32 (over z, y_hi).
Axes of the slice: x: 4, y: 4 (y_hi: 2, y_lo: 2; y = y_hi * 2 + y_lo), z: 16, core: 2. Of those that a mesh axis runs over, the one named last changes fastest.
Arguments:
- tokens: bfloat16 [16, 512, 5120], P('grp', 'ep'), may hold values from -6 to 6
- cotangent: bfloat16 [16, 512, 5120], P('grp', 'ep'), may hold values from -1.5 to 1.5
- counts: int32 [16, 32, 4], P('grp', 'ep'), may hold values from 0 to 4, as said below
- destination: int32 [16, 32, 16], P('grp', 'ep'), may hold values from 0 to 15, each once within a row
- placement: int32 [32], replicated, may hold values from 0 to 31, each once
- gate_up_weight: bfloat16 [32, 2, 5120, 128], P('ep', None, 'grp'), may hold values from -0.078125 to 0.078125
- down_weight: bfloat16 [32, 5120, 128], P('ep', 'grp'), may hold values from -0.1875 to 0.1875
Outputs:
- layer_out: bfloat16 [16, 512, 5120], P('grp', 'ep')
- input_grad: bfloat16 [16, 512, 5120], P('grp', 'ep')
- gate_up_grad: float32 [32, 2, 5120, 128], P('ep', None, 'grp')
- down_grad: float32 [32, 5120, 128], P('ep', 'grp')
Inputs may be any that keep to these rules, and one draw needn't show every extreme that they name: counts[g, j, e] is the number of kept slots of expert e on device (g, j) after reassignment; some device has all 4 slots of an expert kept in every draw. `destination`: the 16 blocks of one device go to 16 different groups. `placement`: each expert slice is served by exactly one owner.
All inputs are finite; a program needn't handle non-finite values.
Results may differ from a plain program's by a relative error of at most 0.017.
Values may be sent and summed in bfloat16 or wider, within the bound.
No kernel may reach another device: no remote copies, remote signals or barrier semaphores. Data moves between devices by JAX's collectives and lax.ppermute only.
A program may use at most 64 MiB of HBM per device.

v0:
```python
import jax
import jax.numpy as jnp
from jax import lax
from jax.sharding import PartitionSpec as P


def swiglu_backward(gate_up, hidden_grad):
    gate_part = gate_up[0]
    up_part = gate_up[1]
    sigmoid_gate = jax.nn.sigmoid(gate_part)
    activated = gate_part * sigmoid_gate
    hidden = (activated * up_part).astype(jnp.bfloat16)
    gate_grad = hidden_grad * up_part * sigmoid_gate * (1.0 + gate_part * (1.0 - sigmoid_gate))
    up_grad = hidden_grad * activated
    return (hidden, jnp.stack([gate_grad, up_grad]).astype(jnp.bfloat16))


def body(tokens, cotangent, counts, destination, placement, gate_up_weight, down_weight):
    groups = lax.axis_size("grp")
    owners = lax.axis_size("ep")
    tok_dev = tokens.shape[1]
    model_width = tokens.shape[2]
    experts = counts.shape[2]
    capacity = tok_dev // experts
    block_rows = tok_dev // groups
    split_count = owners // experts
    row_count = owners * capacity
    order = jnp.argsort(destination[0, 0])
    send_tokens = jnp.take(tokens[0].reshape(groups, block_rows, model_width), order, axis=0)
    send_cotangent = jnp.take(cotangent[0].reshape(groups, block_rows, model_width), order, axis=0)
    here_tokens, here_cotangent = (
        lax.all_to_all(send_tokens, "grp", split_axis=0, concat_axis=0, tiled=True),
        lax.all_to_all(send_cotangent, "grp", split_axis=0, concat_axis=0, tiled=True),
    )
    slot_ids = lax.broadcasted_iota(jnp.int32, (experts, capacity), 1)
    keep = (slot_ids < counts[0, 0][:, None])[:, :, None]
    nothing = jnp.zeros((), jnp.bfloat16)
    kept_tokens = jnp.where(keep, here_tokens.reshape(experts, capacity, model_width), nothing)
    kept_cotangent = jnp.where(
        keep, here_cotangent.reshape(experts, capacity, model_width), nothing
    )
    expert_of = placement // split_count
    routed_tokens, routed_cotangent = (
        lax.all_to_all(
            jnp.take(kept_tokens, expert_of, axis=0), "ep", split_axis=0, concat_axis=0, tiled=True
        ),
        lax.all_to_all(
            jnp.take(kept_cotangent, expert_of, axis=0),
            "ep",
            split_axis=0,
            concat_axis=0,
            tiled=True,
        ),
    )
    routed_tokens = routed_tokens.reshape(row_count, model_width)
    routed_cotangent = routed_cotangent.reshape(row_count, model_width)
    stacked_down = down_weight[:, None]
    full_gate_up, full_down = (
        lax.all_gather(gate_up_weight, "grp", axis=2, tiled=True),
        lax.all_gather(stacked_down, "grp", axis=2, tiled=True),
    )
    full_gate_up = full_gate_up[0]
    full_down = full_down[0, 0]
    gate_up = jnp.einsum(
        "rd,kds->krs", routed_tokens, full_gate_up, preferred_element_type=jnp.float32
    )
    hidden_grad = jnp.dot(routed_cotangent, full_down, preferred_element_type=jnp.float32)
    hidden, grad_rows = swiglu_backward(gate_up, hidden_grad)
    forward_part = (
        jnp.einsum("rs,ds->rd", hidden, full_down, preferred_element_type=jnp.float32)
        .astype(jnp.bfloat16)
        .reshape(owners, capacity, model_width)
    )
    backward_part = (
        jnp.einsum("krs,kds->rd", grad_rows, full_gate_up, preferred_element_type=jnp.float32)
        .astype(jnp.bfloat16)
        .reshape(owners, capacity, model_width)
    )
    owner_table = (
        expert_of[:, None] == lax.broadcasted_iota(jnp.int32, (owners, experts), 1)
    ).astype(jnp.bfloat16)

    def combine(returned):
        summed = jnp.einsum(
            "jcd,je->ecd", returned, owner_table, preferred_element_type=jnp.float32
        )
        return summed.astype(jnp.bfloat16).reshape(1, tok_dev, model_width)

    layer_out = combine(lax.all_to_all(forward_part, "ep", split_axis=0, concat_axis=0, tiled=True))
    input_grad = combine(
        lax.all_to_all(backward_part, "ep", split_axis=0, concat_axis=0, tiled=True)
    )
    gate_up_term = jnp.einsum(
        "rd,krs->kds", routed_tokens, grad_rows, preferred_element_type=jnp.float32
    )
    down_term = jnp.einsum(
        "rd,rs->ds", routed_cotangent, hidden, preferred_element_type=jnp.float32
    )
    gate_up_grad, down_grad = (
        lax.psum_scatter(
            gate_up_term[None].astype(jnp.bfloat16), "grp", scatter_dimension=2, tiled=True
        ).astype(jnp.float32),
        lax.psum_scatter(
            down_term[None, None].astype(jnp.bfloat16), "grp", scatter_dimension=2, tiled=True
        ).astype(jnp.float32),
    )
    return (layer_out, input_grad, gate_up_grad, down_grad[:, 0])


def solution(mesh):
    return jax.shard_map(
        body,
        mesh=mesh,
        in_specs=(
            P("grp", "ep", None),
            P("grp", "ep", None),
            P("grp", "ep", None),
            P("grp", "ep", None),
            P(),
            P("ep", None, "grp", None),
            P("ep", "grp", None),
        ),
        out_specs=(
            P("grp", "ep", None),
            P("grp", "ep", None),
            P("ep", None, "grp", None),
            P("ep", "grp", None),
        ),
        check_vma=False,
    )
```

profile of v0, /device:TPU:32, one launch (start us, length us, event | category | flops | bytes accessed | tf_op | source)
XLA Modules:
  0.0 448.4 jit_solution(12998677638847090264)
XLA Ops:
  7.2 1.9 sort.17
  9.2 0.6 gather_fusion.2
  9.8 0.6 gather_fusion
  10.5 0.1 bitcast_select_fusion
  10.6 0.5 broadcast.114
  11.1 0.7 reduce.3
  11.8 0.8 reshape.164
  12.6 5.4 %all-to-all-start = ((bf16[16,2,2560]{2,1,0:T(2,128)(2,1)}), bf16[16,2,2560]{2,1,0:T(2,128)(2,1)S(1)}, u32[]{:S(2)}, u32[]{:S(2)}) async-start(bf16[16,2,2560]{2,1,0:T(2,128)(2,1)} %reshape.164), calls=%async_computation | async-start | bytes 327680 | tf_op jit(solution)/shard_map/all_to_all | solution.py:32
  18.1 0.7 reduce.2
  18.8 0.8 reshape.166
  19.6 0.1 iota_compare_fusion
  19.6 5.2 %all-to-all-done = bf16[16,2,2560]{2,1,0:T(2,128)(2,1)S(1)} async-done(((bf16[16,2,2560]{2,1,0:T(2,128)(2,1)}), bf16[16,2,2560]{2,1,0:T(2,128)(2,1)S(1)}, u32[]{:S(2)}, u32[]{:S(2)}) %all-to-all-start) | async-done | bytes 163872 | tf_op jit(solution)/shard_map/all_to_all | solution.py:32
  24.8 3.5 all-to-all-start.3
  28.3 0.1 reshape.165
  28.5 0.9 reduce
  29.4 0.1 reshape.94
  29.5 5.5 %all-to-all-done.3 = bf16[16,2,2560]{2,1,0:T(2,128)(2,1)S(1)} async-done(((bf16[16,2,2560]{2,1,0:T(2,128)(2,1)}), bf16[16,2,2560]{2,1,0:T(2,128)(2,1)S(1)}, u32[]{:S(2)}, u32[]{:S(2)}) %all-to-all-start.3) | async-done | bytes 163872 | tf_op jit(solution)/shard_map/all_to_all | solution.py:33
  35.0 0.1 reshape.167
  35.2 0.9 reduce.1
  36.1 0.1 reshape.98
  36.2 0.2 broadcast_select_fusion.2
  36.4 1.7 gather_fusion.3
  38.1 1.7 gather_fusion.1
  39.8 2.7 broadcast_select_fusion
  42.5 17.7 %all-to-all-start.1 = ((bf16[32,4,5120]{2,1,0:T(4,128)(2,1)}), bf16[32,4,5120]{2,1,0:T(4,128)(2,1)S(1)}, u32[]{:S(2)}, u32[]{:S(2)}) async-start(bf16[32,4,5120]{2,1,0:T(4,128)(2,1)} %get-tuple-element.29), calls=%async_computation.1 | async-start | bytes 2621440 | tf_op jit(solution)/shard_map/all_to_all | solution.py:44
  60.2 0.0 all-gather.4.cloned.1.call-start
  60.2 0.7 all-gather.4.cloned.1.call-update
  60.9 64.1 %all-to-all-done.1 = bf16[32,4,5120]{2,1,0:T(4,128)(2,1)S(1)} async-done(((bf16[32,4,5120]{2,1,0:T(4,128)(2,1)}), bf16[32,4,5120]{2,1,0:T(4,128)(2,1)S(1)}, u32[]{:S(2)}, u32[]{:S(2)}) %all-to-all-start.1) | async-done | bytes 1310752 | tf_op jit(solution)/shard_map/all_to_all | solution.py:44
  125.0 1.1 copy-done.3
  126.1 6.9 %all-to-all-start.4 = ((bf16[32,4,5120]{2,1,0:T(4,128)(2,1)}), bf16[32,4,5120]{2,1,0:T(4,128)(2,1)S(1)}, u32[]{:S(2)}, u32[]{:S(2)}) async-start(bf16[32,4,5120]{2,1,0:T(4,128)(2,1)} %get-tuple-element.28), calls=%async_computation.4 | async-start | bytes 2621440 | tf_op jit(solution)/shard_map/all_to_all | solution.py:47
  133.0 0.0 all-gather.6.cloned.1.call-start
  133.1 0.7 all-gather.6.cloned.1.call-update
  133.8 2.5 reshape.157
  136.3 0.0 all-gather.4.cloned.1.call-done
  136.3 2.3 fusion.11
  138.6 37.2 %all-gather.6.cloned.1.call-done = bf16[1,5120,128]{2,1,0:T(8,128)(2,1)} async-done(((bf16[1,320,128]{2,1,0:T(8,128)(2,1)}), bf16[1,5120,128]{2,1,0:T(8,128)(2,1)}) %all-gather.6.cloned.1.call-update) | async-done | bytes 1310736 | tf_op jit(solution)/shard_map/all_gather | solution.py:60
  175.8 2.9 convolution_convert_fusion.2
  178.7 3.4 reshape.96
  182.1 15.2 %all-to-all-done.4 = bf16[32,4,5120]{2,1,0:T(4,128)(2,1)S(1)} async-done(((bf16[32,4,5120]{2,1,0:T(4,128)(2,1)}), bf16[32,4,5120]{2,1,0:T(4,128)(2,1)S(1)}, u32[]{:S(2)}, u32[]{:S(2)}) %all-to-all-start.4) | async-done | bytes 1310752 | tf_op jit(solution)/shard_map/all_to_all | solution.py:47
  197.3 1.0 copy-done.2
  198.3 7.1 %all-to-all-start.2 = ((bf16[32,4,5120]{2,1,0:T(4,128)(2,1)}), bf16[32,4,5120]{2,1,0:T(4,128)(2,1)}, u32[]{:S(2)}, u32[]{:S(2)}) async-start(bf16[32,4,5120]{2,1,0:T(4,128)(2,1)} %reshape.96), calls=%async_computation.2 | async-start | bytes 2621440 | tf_op jit(solution)/shard_map/all_to_all | solution.py:89
  205.4 0.2 all-reduce.3.cloned.1.call-start
  205.6 2.5 reshape.99
  208.1 1.8 fusion.26
  209.9 2.3 fusion
  212.3 7.4 %copy.37 = bf16[1,2,5120,128]{3,1,0,2:T(2,128)(2,1)} copy(bf16[1,2,5120,128]{2,3,1,0:T(8,128)(2,1)} %fusion) | data formatting | bytes 5242880 | tf_op jit(solution)/shard_map/convert_element_type | solution.py:101
  219.7 2.7 fusion.1
  222.4 1.4 reshape.100
  223.8 46.0 %all-to-all-done.2 = bf16[32,4,5120]{2,1,0:T(4,128)(2,1)} async-done(((bf16[32,4,5120]{2,1,0:T(4,128)(2,1)}), bf16[32,4,5120]{2,1,0:T(4,128)(2,1)}, u32[]{:S(2)}, u32[]{:S(2)}) %all-to-all-start.2) | async-done | bytes 1310752 | tf_op jit(solution)/shard_map/all_to_all | solution.py:89
  269.8 7.0 %all-to-all-start.5 = ((bf16[32,4,5120]{2,1,0:T(4,128)(2,1)}), bf16[32,4,5120]{2,1,0:T(4,128)(2,1)S(1)}, u32[]{:S(2)}, u32[]{:S(2)}) async-start(bf16[32,4,5120]{2,1,0:T(4,128)(2,1)} %reshape.100), calls=%async_computation.5 | async-start | bytes 2621440 | tf_op jit(solution)/shard_map/all_to_all | solution.py:91
  276.8 0.0 reduce-scatter.2.cloned.1.call-start
  276.9 1.6 fusion.2
  278.5 1.3 dynamic-slice
  280.4 81.8 %all-reduce.3.cloned.1.call-done = bf16[1,2,5120,128]{3,1,0,2:T(2,128)(2,1)} async-done(((bf16[1,2,5120,128]{3,1,0,2:T(2,128)(2,1)}), bf16[1,2,5120,128]{3,1,0,2:T(2,128)(2,1)}) %all-reduce.3.cloned.1.call-update) | async-done | bytes 2621456
  362.2 1.0 dynamic-slice_convert_fusion
  363.2 0.7 copy.38
  364.0 71.8 %reduce-scatter.2.cloned.1.call-done = bf16[1,1,320,128]{3,2,1,0:T(8,128)(2,1)} async-done(((bf16[1,1,5120,128]{3,2,1,0:T(8,128)(2,1)}), bf16[1,1,320,128]{3,2,1,0:T(8,128)(2,1)}) %reduce-scatter.2.cloned.1.call-update) | async-done | bytes 81936 | tf_op jit(solution)/shard_map/reduce_scatter | solution.py:103
  435.7 1.6 bitcast_convert_fusion
  437.3 2.1 convolution_convert_fusion.4
  439.4 0.1 copy.32
  439.5 0.7 reshape.97
  440.2 0.8 convolution_convert_fusion.3
  441.0 0.1 copy.35
  441.1 0.7 reshape.101
  (21 shorter events, 0.1 us)
Async XLA Ops:
  7.2 2.0 copy-start
  7.2 2.7 copy-start.1
  9.8 8.2 %copy-start.4 = (s32[32]{0:T(128)S(1)}, s32[32]{0:T(128)}, u32[]{:S(2)}) copy-start(s32[32]{0:T(128)} %param.15) | copy-start | bytes 388
  10.5 9.1 %copy-start.5 = (s32[1,1,4]{2,1,0:T(1,128)S(1)}, s32[1,1,4]{2,1,0:T(1,128)}, u32[]{:S(2)}) copy-start(s32[1,1,4]{2,1,0:T(1,128)} %param.13) | copy-start | bytes 52
  12.6 12.2 %all-to-all-start = ((bf16[16,2,2560]{2,1,0:T(2,128)(2,1)}), bf16[16,2,2560]{2,1,0:T(2,128)(2,1)S(1)}, u32[]{:S(2)}, u32[]{:S(2)}) async-start(bf16[16,2,2560]{2,1,0:T(2,128)(2,1)} %reshape.164), calls=%async_computation | async-start | bytes 327680 | tf_op jit(solution)/shard_map/all_to_all | solution.py:32
  24.8 10.2 %all-to-all-start.3 = ((bf16[16,2,2560]{2,1,0:T(2,128)(2,1)}), bf16[16,2,2560]{2,1,0:T(2,128)(2,1)S(1)}, u32[]{:S(2)}, u32[]{:S(2)}) async-start(bf16[16,2,2560]{2,1,0:T(2,128)(2,1)} %reshape.166), calls=%async_computation.3 | async-start | bytes 327680 | tf_op jit(solution)/shard_map/all_to_all | solution.py:33
  42.5 82.5 %all-to-all-start.1 = ((bf16[32,4,5120]{2,1,0:T(4,128)(2,1)}), bf16[32,4,5120]{2,1,0:T(4,128)(2,1)S(1)}, u32[]{:S(2)}, u32[]{:S(2)}) async-start(bf16[32,4,5120]{2,1,0:T(4,128)(2,1)} %get-tuple-element.29), calls=%async_computation.1 | async-start | bytes 2621440 | tf_op jit(solution)/shard_map/all_to_all | solution.py:44
  60.2 76.1 %all-gather.4.cloned.1.call-start = ((), (), s32[]{:S(2)}) async-start(), calls=%async_computation.7 | async-start | bytes 2785280 | tf_op jit(solution)/shard_map/all_gather | solution.py:59
  125.0 1.1 copy-start.3
  126.1 71.2 %all-to-all-start.4 = ((bf16[32,4,5120]{2,1,0:T(4,128)(2,1)}), bf16[32,4,5120]{2,1,0:T(4,128)(2,1)S(1)}, u32[]{:S(2)}, u32[]{:S(2)}) async-start(bf16[32,4,5120]{2,1,0:T(4,128)(2,1)} %get-tuple-element.28), calls=%async_computation.4 | async-start | bytes 2621440 | tf_op jit(solution)/shard_map/all_to_all | solution.py:47
  133.0 42.7 %all-gather.6.cloned.1.call-start = ((), (), s32[]{:S(2)}) async-start(), calls=%async_computation.9 | async-start | bytes 1392640 | tf_op jit(solution)/shard_map/all_gather | solution.py:60
  197.3 1.0 copy-start.2
  198.3 71.5 %all-to-all-start.2 = ((bf16[32,4,5120]{2,1,0:T(4,128)(2,1)}), bf16[32,4,5120]{2,1,0:T(4,128)(2,1)}, u32[]{:S(2)}, u32[]{:S(2)}) async-start(bf16[32,4,5120]{2,1,0:T(4,128)(2,1)} %reshape.96), calls=%async_computation.2 | async-start | bytes 2621440 | tf_op jit(solution)/shard_map/all_to_all | solution.py:89
  205.4 156.8 %all-reduce.3.cloned.1.call-start = ((), (), s32[]{:S(2)}) async-start(), calls=%async_computation.10 | async-start | bytes 5242880
  269.8 170.4 %all-to-all-start.5 = ((bf16[32,4,5120]{2,1,0:T(4,128)(2,1)}), bf16[32,4,5120]{2,1,0:T(4,128)(2,1)S(1)}, u32[]{:S(2)}, u32[]{:S(2)}) async-start(bf16[32,4,5120]{2,1,0:T(4,128)(2,1)} %reshape.100), calls=%async_computation.5 | async-start | bytes 2621440 | tf_op jit(solution)/shard_map/all_to_all | solution.py:91
  276.8 158.9 %reduce-scatter.2.cloned.1.call-start = ((), (), s32[]{:S(2)}) async-start(), calls=%async_computation.8 | async-start | bytes 1392640 | tf_op jit(solution)/shard_map/reduce_scatter | solution.py:103
Sparse Core Ops, SparseCore 0:
  63.1 41.9 all-gather.3
  136.0 39.7 all-gather.5
  219.8 142.3 all-reduce.2
  364.9 70.8 reduce-scatter.1
where the time goes:
time: 450 us; the launch traced here: 448 us
  waiting for transfers between devices  328 us (73%)
  starting transfers between devices  48 us (11%)
  local copies, waits for them, and re-layouts  30 us (7%)
  matrix products  16.6 us (4%)
  between operations  14.7 us (3%)
  other arithmetic  11 us (2%)
    unnamed x5, waiting for transfers between devices  83.2 us
    reduce_scatter x1, waiting for transfers between devices, body(): lax.psum_scatter(down_term[None, None].astype(jnp.bfloat16), 'grp', scatt...  71.8 us
    all_to_all x1, waiting for transfers between devices, body(): lax.all_to_all(jnp.take(kept_tokens, expert_of, axis=0), 'ep', split_axis...  64.1 us
    all_to_all x1, waiting for transfers between devices, body(): lax.all_to_all(forward_part, 'ep', split_axis=0, concat_axis=0, tiled=True)  46 us
    all_gather x1, waiting for transfers between devices, body(): lax.all_gather(stacked_down, 'grp', axis=2, tiled=True)  37.2 us
    all_to_all x1, starting transfers between devices, body(): lax.all_to_all(jnp.take(kept_tokens, expert_of, axis=0), 'ep', split_axis...  17.7 us
    all_to_all x1, waiting for transfers between devices, body(): lax.all_to_all(jnp.take(kept_cotangent, expert_of, axis=0), 'ep', split_a...  15.2 us
  transfers between devices with their start and end apart: 10, of which 8 were waited for; matrix products, arithmetic and copies ran while one was open for 9% of the time, Pallas kernels for 0%

commit v1 on v0

v1 whole, which is shorter than its diff:
```python
import functools

import jax
import jax.numpy as jnp
from jax import lax
from jax.experimental import pallas as pl
from jax.experimental.pallas import tpu as pltpu
from jax.sharding import Mesh, PartitionSpec as P

AXES = ("y_lo", "x", "core", "z", "y_hi")
SIZES = (2, 4, 2, 16, 2)
GRP = ("y_lo", "x", "core")
EP = ("z", "y_hi")
PLANE = ("y_hi", "y_lo", "x", "core")

G = 16
Z = 16
Y = 2
E = 4
C = 4
D = 5120
W = D // G
WP = 384
S = 128
R = Y * C * G
BF = jnp.bfloat16
F32 = jnp.float32


def dot(a, b, dims=((1,), (0,))):
    return lax.dot_general(a, b, (dims, ((), ())), preferred_element_type=F32)


def pack_kernel(me_ref, counts_ref, dest_ref, tok_ref, cot_ref, out_ref):
    me = me_ref[0]
    rows = lax.broadcasted_iota(jnp.int32, (G, G), 0)
    pick = (rows == dest_ref[...]).astype(F32).astype(BF)
    lane = lax.broadcasted_iota(jnp.int32, (G, WP), 1)
    row = lax.broadcasted_iota(jnp.int32, (G, WP), 0)
    extra = jnp.zeros((G, WP), F32)
    for e in range(E):
        extra = jnp.where((lane == W + e) & (row == me), counts_ref[e].astype(F32), extra)
    for d in range(G):
        start = d * W // 128 * 128
        for t, ref in enumerate((tok_ref, cot_ref)):
            moved = dot(pick, ref[:, start : start + WP])
            if start != d * W:
                moved = pltpu.roll(moved, WP - (d * W - start), 1)
            moved = jnp.where(lane < W, moved, extra).astype(BF)
            for y in range(Y):
                out_ref[y * G + d, t * G : (t + 1) * G, :] = moved


def pack(me, counts, dest, tokens, cotangent):
    vmem = pl.BlockSpec(memory_space=pltpu.VMEM)
    smem = pl.BlockSpec(memory_space=pltpu.SMEM)
    return pl.pallas_call(
        pack_kernel,
        out_shape=jax.ShapeDtypeStruct((Y * G, 2 * G, WP), BF),
        in_specs=[smem, smem, vmem, vmem, vmem],
        out_specs=vmem,
        name="pack",
    )(me, counts, dest, tokens, cotangent)


def load_rows(recv_ref, x_ref):
    lane = lax.broadcasted_iota(jnp.int32, (G, 128), 1)
    for y in range(Y):
        table = jnp.zeros((G, 128), F32)
        for g in range(G):
            table = table + recv_ref[y * G + g, 0:G, WP - 128 : WP].astype(F32)
        for e in range(E):
            kept = jnp.sum(jnp.where(lane == 128 - (WP - W) + e, table, 0.0), axis=1, keepdims=True)
            for c in range(C):
                keep = jnp.broadcast_to(kept, (G, W)) > c + 0.5
                at = (y * C + c) * G
                for t in range(2):
                    block = recv_ref[y * G + e * C + c, t * G : (t + 1) * G, 0:W].astype(F32)
                    x_ref[t, e, at : at + G, :] = jnp.where(keep, block, 0.0).astype(BF)


def first_kernel(expert_ref, recv_ref, weight_ref, out_ref, x_ref):
    load_rows(recv_ref, x_ref)

    def step(z, carry):
        e = expert_ref[z]
        tok = x_ref[0, e]
        cot = x_ref[1, e]
        out_ref[z, :, 0:S] = dot(tok, weight_ref[z, 0]).astype(BF)
        out_ref[z, :, S : 2 * S] = dot(tok, weight_ref[z, 1]).astype(BF)
        out_ref[z, :, 2 * S : 3 * S] = dot(cot, weight_ref[z, 2]).astype(BF)
        return carry

    lax.fori_loop(0, Z, step, 0)


def first(expert, recv, weight):
    vmem = pl.BlockSpec(memory_space=pltpu.VMEM)
    smem = pl.BlockSpec(memory_space=pltpu.SMEM)
    return pl.pallas_call(
        first_kernel,
        out_shape=jax.ShapeDtypeStruct((Z, R, 3 * S), BF),
        in_specs=[smem, vmem, vmem],
        out_specs=vmem,
        scratch_shapes=[pltpu.VMEM((2, E, R, W), BF)],
        name="first",
    )(expert, recv, weight)


def middle_kernel(part_ref, out_ref):
    total = part_ref[0].astype(F32)
    for d in range(1, G):
        total = total + part_ref[d].astype(F32)
    gate = total[:, 0:S]
    up = total[:, S : 2 * S]
    hidden_grad = total[:, 2 * S : 3 * S]
    sigmoid = jax.nn.sigmoid(gate)
    activated = gate * sigmoid
    out_ref[:, 0:S] = (activated * up).astype(BF)
    grad = hidden_grad * up * sigmoid * (1.0 + gate * (1.0 - sigmoid))
    out_ref[:, S : 2 * S] = grad.astype(BF)
    out_ref[:, 2 * S : 3 * S] = (hidden_grad * activated).astype(BF)


def middle(parts):
    vmem = pl.BlockSpec(memory_space=pltpu.VMEM)
    return pl.pallas_call(
        middle_kernel,
        out_shape=jax.ShapeDtypeStruct((R, 3 * S), BF),
        in_specs=[vmem],
        out_specs=vmem,
        name="middle",
    )(parts)


def last_kernel(expert_ref, recv_ref, weight_ref, act_ref, out_ref, grad_ref, x_ref, acc_ref):
    load_rows(recv_ref, x_ref)
    acc_ref[...] = jnp.zeros_like(acc_ref)
    tail = ((1,), (1,))
    head = ((0,), (0,))

    def step(z, carry):
        e = expert_ref[z]
        hidden = act_ref[z, :, 0:S]
        gate_grad = act_ref[z, :, S : 2 * S]
        up_grad = act_ref[z, :, 2 * S : 3 * S]
        acc_ref[0, e] += dot(hidden, weight_ref[z, 2], tail)
        acc_ref[1, e] += dot(gate_grad, weight_ref[z, 0], tail) + dot(up_grad, weight_ref[z, 1], tail)
        tok = x_ref[0, e]
        cot = x_ref[1, e]
        grad_ref[z, 0] = dot(tok, gate_grad, head).astype(BF)
        grad_ref[z, 1] = dot(tok, up_grad, head).astype(BF)
        grad_ref[z, 2] = dot(cot, hidden, head).astype(BF)
        return carry

    lax.fori_loop(0, Z, step, 0)
    n = E * C * G
    i = lax.broadcasted_iota(jnp.int32, (n, n), 0)
    j = lax.broadcasted_iota(jnp.int32, (n, n), 1)
    swap = ((i // (E * C) == j % G) & (i % (E * C) == j // G)).astype(F32).astype(BF)
    for y in range(Y):
        for t in range(2):
            rows = jnp.concatenate(
                [acc_ref[t, e, y * C * G : (y + 1) * C * G, :].astype(BF) for e in range(E)], axis=0
            )
            moved = dot(swap, rows).astype(BF)
            for h in range(G):
                out_ref[y * G + h, t * G : (t + 1) * G, 0:W] = moved[h * E * C : (h + 1) * E * C, :]
                out_ref[y * G + h, t * G : (t + 1) * G, W:WP] = jnp.zeros((E * C, WP - W), BF)


def last(expert, recv, weight, act):
    vmem = pl.BlockSpec(memory_space=pltpu.VMEM)
    smem = pl.BlockSpec(memory_space=pltpu.SMEM)
    return pl.pallas_call(
        last_kernel,
        out_shape=(
            jax.ShapeDtypeStruct((Y * G, 2 * G, WP), BF),
            jax.ShapeDtypeStruct((Z, 3, W, S), BF),
        ),
        in_specs=[smem, vmem, vmem, vmem],
        out_specs=(vmem, vmem),
        scratch_shapes=[pltpu.VMEM((2, E, R, W), BF), pltpu.VMEM((2, E, R, W), F32)],
        name="last",
    )(expert, recv, weight, act)


def unpack_kernel(recv_ref, layer_ref, grad_ref):
    lane = lax.broadcasted_iota(jnp.int32, (G, WP), 1)
    for t, ref in enumerate((layer_ref, grad_ref)):
        for d in range(0, G, 2):
            rows = slice(t * G, (t + 1) * G)
            left = recv_ref[d, rows, :].astype(F32) + recv_ref[G + d, rows, :].astype(F32)
            right = recv_ref[d + 1, rows, :].astype(F32) + recv_ref[G + d + 1, rows, :].astype(F32)
            right = pltpu.roll(right, W - 256, 1)
            low = lane[:, 0:128] < W - 256
            at = d * W
            ref[:, at : at + 256] = left[:, 0:256].astype(BF)
            ref[:, at + 256 : at + 384] = jnp.where(low, left[:, 256:384], right[:, 0:128]).astype(BF)
            ref[:, at + 384 : at + 640] = right[:, 128:384].astype(BF)


def unpack(recv):
    vmem = pl.BlockSpec(memory_space=pltpu.VMEM)
    shape = jax.ShapeDtypeStruct((E * C, D), BF)
    return pl.pallas_call(
        unpack_kernel,
        out_shape=(shape, shape),
        in_specs=[vmem],
        out_specs=(vmem, vmem),
        name="unpack",
    )(recv)


def exchange(x, axes):
    return lax.all_to_all(x, axes, split_axis=0, concat_axis=0, tiled=True)


def body(tokens, cotangent, counts, destination, placement, gate_up_weight, down_weight):
    me = lax.axis_index(GRP).reshape(1).astype(jnp.int32)
    local = jnp.concatenate([gate_up_weight[0], down_weight], axis=0)
    weight = lax.all_gather(local[None], "z", axis=0, tiled=True)
    sent = pack(me, counts[0, 0], destination[0], tokens[0], cotangent[0])
    recv = exchange(sent, PLANE)
    near = lax.dynamic_index_in_dim(placement.reshape(Z, Y), lax.axis_index("y_hi"), 1, keepdims=False)
    expert = near // (Z * Y // E)
    parts = exchange(first(expert, recv, weight), GRP)
    act = lax.all_gather(middle(parts)[None], GRP, axis=0, tiled=True)
    returned, grads = last(expert, recv, weight, act)
    layer_out, input_grad = unpack(exchange(returned, PLANE))
    own = lax.psum_scatter(grads, "z", scatter_dimension=0, tiled=True).astype(F32)
    return (layer_out[None], input_grad[None], own[:, 0:2], own[:, 2])


def solution(mesh):
    fine = Mesh(mesh.devices.reshape(SIZES), AXES)
    return jax.shard_map(
        body,
        mesh=fine,
        in_specs=(
            P(GRP, EP, None),
            P(GRP, EP, None),
            P(GRP, EP, None),
            P(GRP, EP, None),
            P(),
            P(EP, None, GRP, None),
            P(EP, GRP, None),
        ),
        out_specs=(
            P(GRP, EP, None),
            P(GRP, EP, None),
            P(EP, None, GRP, None),
            P(EP, GRP, None),
        ),
        check_vma=False,
    )
```

time: 450 us -> 266 us (0.59)
  the two profiles are of different devices: /device:TPU:32 before, /device:TPU:4 now
where the time goes in v1:
time: 266 us; the launch traced here: 265 us
  waiting for transfers between devices  167 us (63%)
  blocking collectives  44.1 us (17%)
  Pallas kernels  24.1 us (9%)
  between operations  13.8 us (5%)
  starting transfers between devices  9.55 us (4%)
  local copies, waits for them, and re-layouts  3.72 us (1%)
  other arithmetic  3.18 us (1%)
    all_gather x1, waiting for transfers between devices, body(): weight = lax.all_gather(local[None], 'z', axis=0, tiled=True)  59.5 us
    reduce_scatter x1, waiting for transfers between devices, body(): lax.psum_scatter(grads, 'z', scatter_dimension=0, tiled=True).astype(F32)  59 us
    all_to_all x2, blocking collectives, exchange(): return lax.all_to_all(x, axes, split_axis=0, concat_axis=0, tiled=True)  44.1 us
    all_gather x1, waiting for transfers between devices, body(): act = lax.all_gather(middle(parts)[None], GRP, axis=0, tiled=True)  36.8 us
    all_to_all x1, waiting for transfers between devices, exchange(): return lax.all_to_all(x, axes, split_axis=0, concat_axis=0, tiled=True)  11.7 us
    pallas_call x1, Pallas kernels, last(): pl.pallas_call(last_kernel, out_shape=(jax.ShapeDtypeStruct((Y * G, 2 * G...  10.2 us
    all_to_all x1, starting transfers between devices, exchange(): return lax.all_to_all(x, axes, split_axis=0, concat_axis=0, tiled=True)  9.43 us
    pallas_call x1, Pallas kernels, first(): pl.pallas_call(first_kernel, out_shape=jax.ShapeDtypeStruct((Z, R, 3 * S)...  7.41 us
  transfers between devices with their start and end apart: 4, of which 4 were waited for; matrix products, arithmetic and copies ran while one was open for 0% of the time, Pallas kernels for 2%

profile of v1, /device:TPU:4, one launch (start us, length us, event | category | flops | bytes accessed | tf_op | source)
XLA Modules:
  0.0 265.5 jit_solution(6290727680760478180)
XLA Ops:
  7.2 0.0 all-gather.5.cloned.1.call-start
  7.2 1.7 pad_maximum_fusion
  8.9 0.0 copy-start.2
  8.9 0.0 all-gather.5.cloned.1.call-update
  8.9 2.3 pack.1
  11.2 9.4 %all-to-all-start = ((bf16[32,32,384]{2,1,0:T(8,128)(2,1)}), bf16[32,32,384]{2,1,0:T(8,128)(2,1)S(1)}, u32[]{:S(2)}, u32[]{:S(2)}) async-start(bf16[32,32,384]{2,1,0:T(8,128)(2,1)} %pack.1), calls=%async_computation | async-start | bytes 1572864 | tf_op jit(solution)/shard_map/all_to_all | solution.py:216
  20.6 0.0 all-gather.7.cloned.1.call-start
  20.7 0.0 copy-done.2
  20.7 0.1 reshape.14
  20.8 0.2 dynamic-slice_reduce_fusion
  20.9 0.5 and_select_fusion.expert_ref
  21.5 11.7 %all-to-all-done.recv_ref = bf16[32,32,384]{2,1,0:T(8,128)(2,1)S(1)} async-done(((bf16[32,32,384]{2,1,0:T(8,128)(2,1)}), bf16[32,32,384]{2,1,0:T(8,128)(2,1)S(1)}, u32[]{:S(2)}, u32[]{:S(2)}) %all-to-all-start) | async-done | bytes 786464 | tf_op jit(solution)/shard_map/all_to_all | solution.py:216
  33.2 0.0 copy-start
  33.2 59.5 %all-gather.5.cloned.1.call-done = bf16[48,320,128]{2,1,0:T(8,128)(2,1)} async-done(((bf16[3,320,128]{2,1,0:T(8,128)(2,1)}), bf16[48,320,128]{2,1,0:T(8,128)(2,1)}) %all-gather.5.cloned.1.call-update) | async-done | bytes 3932176 | tf_op jit(solution)/shard_map/all_gather | solution.py:222
  92.7 0.0 copy-done
  92.7 7.4 %first.1 = bf16[16,128,384]{2,1,0:T(8,128)(2,1)} custom-call(s32[16]{0:T(128)} %and_select_fusion.expert_ref, bf16[32,32,384]{2,1,0:T(8,128)(2,1)} %copy-done, bf16[16,3,320,128]{3,2,1,0:T(8,128)(2,1)} %bitcast.12), custom_call_target="tpu_custom_call" | custom-call | tf_op jit(solution)/shard_map/first/pallas_call | solution.py:100
  100.1 24.5 %all_to_all.15.part_ref = bf16[16,128,384]{2,1,0:T(8,128)(2,1)} all-to-all(bf16[16,128,384]{2,1,0:T(8,128)(2,1)} %first.1), channel_id=1, replica_groups=mesh['y_lo'=2,'x'=4,'core'=2,'z'=16,'y_hi'=2] {'y_lo','x','core'}, dimensions={0} | all-to-all | bytes 3145728 | tf_op jit(solution)/shard_map/all_to_all | solution.py:216
  124.6 2.3 middle.1
  126.8 0.0 all-gather.7.cloned.1.call-update
  126.9 0.0 reduce-scatter.2.cloned.1.call-start
  126.9 36.8 %all-gather.7.cloned.1.call-done = bf16[2048,384]{1,0:T(8,128)(2,1)} async-done(((bf16[128,384]{1,0:T(8,128)(2,1)}), bf16[2048,384]{1,0:T(8,128)(2,1)}) %all-gather.7.cloned.1.call-update) | async-done | bytes 1572880 | tf_op jit(solution)/shard_map/all_gather | solution.py:228
  163.7 10.2 %last.1 = (bf16[32,32,384]{2,1,0:T(8,128)(2,1)}, bf16[16,3,320,128]{3,2,1,0:T(8,128)(2,1)}) custom-call(s32[16]{0:T(128)} %and_select_fusion.expert_ref, bf16[32,32,384]{2,1,0:T(8,128)(2,1)} %copy-done, bf16[16,3,320,128]{3,2,1,0:T(8,128)(2,1)} %bitcast.13, bf16[16,128,384]{2,1,0:T(8,128)(2,1)} %bitcast.14), custom_call_target="tpu_custom_call" | custom-call | tf_op jit(solution)/shard_map/last/pallas_call | solution.py:175
  173.9 0.0 copy-start.1
  173.9 0.0 reduce-scatter.2.cloned.1.call-update
  173.9 1.1 copy-done.1
  175.0 19.6 %all_to_all.16.recv_ref = bf16[32,32,384]{2,1,0:T(8,128)(2,1)} all-to-all(bf16[32,32,384]{2,1,0:T(8,128)(2,1)S(1)} %copy-done.1), channel_id=1, replica_groups=mesh['y_lo'=2,'x'=4,'core'=2,'z'=16,'y_hi'=2] {'y_hi','y_lo','x','core'}, dimensions={0} | all-to-all | bytes 1572864 | tf_op jit(solution)/shard_map/all_to_all | solution.py:216
  194.7 2.0 unpack.1
  196.6 59.0 %reduce-scatter.2.cloned.1.call-done = bf16[1,3,320,128]{3,2,1,0:T(8,128)(2,1)} async-done(((bf16[16,3,320,128]{3,2,1,0:T(8,128)(2,1)}), bf16[1,3,320,128]{3,2,1,0:T(8,128)(2,1)}) %reduce-scatter.2.cloned.1.call-update) | async-done | bytes 245776 | tf_op jit(solution)/shard_map/reduce_scatter | solution.py:231
  255.6 1.0 convert_element_type.3
  256.6 0.7 slice_bitcast_fusion
  257.3 1.7 slice.8
Async XLA Ops:
  7.2 85.5 %all-gather.5.cloned.1.call-start = ((), (), s32[]{:S(2)}) async-start(), calls=%async_computation.5 | async-start | bytes 4177920 | tf_op jit(solution)/shard_map/all_gather | solution.py:222
  8.9 11.8 %copy-start.2 = (s32[32]{0:T(128)S(1)}, s32[32]{0:T(128)}, u32[]{:S(2)}) copy-start(s32[32]{0:T(128)} %param.11) | copy-start | bytes 388
  11.2 22.0 %all-to-all-start = ((bf16[32,32,384]{2,1,0:T(8,128)(2,1)}), bf16[32,32,384]{2,1,0:T(8,128)(2,1)S(1)}, u32[]{:S(2)}, u32[]{:S(2)}) async-start(bf16[32,32,384]{2,1,0:T(8,128)(2,1)} %pack.1), calls=%async_computation | async-start | bytes 1572864 | tf_op jit(solution)/shard_map/all_to_all | solution.py:216
  20.6 143.1 %all-gather.7.cloned.1.call-start = ((), (), s32[]{:S(2)}) async-start(), calls=%async_computation.6 | async-start | bytes 1671168 | tf_op jit(solution)/shard_map/all_gather | solution.py:228
  33.2 59.5 %copy-start = (bf16[32,32,384]{2,1,0:T(8,128)(2,1)}, bf16[32,32,384]{2,1,0:T(8,128)(2,1)S(1)}, u32[]{:S(2)}) copy-start(bf16[32,32,384]{2,1,0:T(8,128)(2,1)S(1)} %all-to-all-done.recv_ref) | copy-start | bytes 2359300
  126.9 128.8 %reduce-scatter.2.cloned.1.call-start = ((), (), s32[]{:S(2)}) async-start(), calls=%async_computation.4 | async-start | bytes 4177920 | tf_op jit(solution)/shard_map/reduce_scatter | solution.py:231
  173.9 1.1 copy-start.1
Sparse Core Ops, SparseCore 0:
  10.6 82.0 all-gather.4
  127.0 36.6 all-gather.6
  174.0 81.5 reduce-scatter.1

commit v2 on v1

v2 whole, which is shorter than its diff:
```python
import jax
import jax.numpy as jnp
from jax import lax
from jax.experimental import pallas as pl
from jax.experimental.pallas import tpu as pltpu
from jax.sharding import Mesh, PartitionSpec as P

AXES = ("y_lo", "x", "core", "z_hi", "z_lo", "y_hi")
SIZES = (2, 4, 2, 8, 2, 2)
GRP = ("y_lo", "x", "core")
EP = ("z_hi", "z_lo", "y_hi")
NEAR = ("z_lo", "y_hi")
PLANE = NEAR + GRP

G = 16
Z = 8
N = 4
E = 4
C = 4
D = 5120
W = D // G
WP = 384
S = 128
Q = C * G
R = N * Q
H = Z * R // G
BF = jnp.bfloat16
F32 = jnp.float32
VMEM = pl.BlockSpec(memory_space=pltpu.VMEM)
SMEM = pl.BlockSpec(memory_space=pltpu.SMEM)
ANY = pl.BlockSpec(memory_space=pl.ANY)


def dot(a, b, dims=((1,), (0,))):
    return lax.dot_general(a, b, (dims, ((), ())), preferred_element_type=F32)


def pack_kernel(me_ref, counts_ref, dest_ref, tok_ref, cot_ref, out_ref):
    me = me_ref[0]
    rows = lax.broadcasted_iota(jnp.int32, (G, G), 0)
    pick = (rows == dest_ref[...]).astype(F32).astype(BF)
    lane = lax.broadcasted_iota(jnp.int32, (G, WP), 1)
    row = lax.broadcasted_iota(jnp.int32, (G, WP), 0)
    extra = jnp.zeros((G, WP), F32)
    for e in range(E):
        extra = jnp.where((lane == W + e) & (row == me), counts_ref[e].astype(F32), extra)
    for d in range(G):
        start = d * W // 128 * 128
        for t, ref in enumerate((tok_ref, cot_ref)):
            moved = dot(pick, ref[:, start : start + WP])
            if start != d * W:
                moved = pltpu.roll(moved, WP - (d * W - start), 1)
            moved = jnp.where(lane < W, moved, extra).astype(BF)
            for n in range(N):
                out_ref[n * G + d, t * G : (t + 1) * G, :] = moved


def pack(me, counts, dest, tokens, cotangent):
    return pl.pallas_call(
        pack_kernel,
        out_shape=jax.ShapeDtypeStruct((N * G, 2 * G, WP), BF),
        in_specs=[SMEM, SMEM, VMEM, VMEM, VMEM],
        out_specs=VMEM,
        name="pack",
    )(me, counts, dest, tokens, cotangent)


def rows_kernel(recv_ref, x_ref, xt_ref):
    lane = lax.broadcasted_iota(jnp.int32, (G, 128), 1)
    for n in range(N):
        table = jnp.zeros((G, 128), F32)
        for g in range(G):
            table = table + recv_ref[n * G + g, 0:G, WP - 128 : WP].astype(F32)
        for e in range(E):
            kept = jnp.sum(jnp.where(lane == 128 - (WP - W) + e, table, 0.0), axis=1, keepdims=True)
            kept = jnp.broadcast_to(kept, (G, W))
            for c in range(C):
                at = n * Q + c * G
                for t in range(2):
                    block = recv_ref[n * G + e * C + c, t * G : (t + 1) * G, 0:W].astype(F32)
                    x_ref[t, e, at : at + G, :] = jnp.where(kept > c + 0.5, block, 0.0).astype(BF)
    for t in range(2):
        for e in range(E):
            xt_ref[t, e] = x_ref[t, e].astype(F32).T.astype(BF)


def prepare(recv):
    return pl.pallas_call(
        rows_kernel,
        out_shape=(jax.ShapeDtypeStruct((2, E, R, W), BF), jax.ShapeDtypeStruct((2, E, W, R), BF)),
        in_specs=[VMEM],
        out_specs=(VMEM, VMEM),
        name="prepare",
    )(recv)


def first_kernel(expert_ref, x_ref, weight_ref, out_ref):
    for i in range(2):
        e = expert_ref[2 * pl.program_id(0) + i]
        tok = x_ref[0, e]
        out_ref[i, :, 0 : 2 * S] = dot(tok, jnp.concatenate([weight_ref[i, 0], weight_ref[i, 1]], axis=1)).astype(BF)
        out_ref[i, :, 2 * S : 3 * S] = dot(x_ref[1, e], weight_ref[i, 2]).astype(BF)


def first(expert, x, weight):
    return pl.pallas_call(
        first_kernel,
        grid=(Z // 2,),
        out_shape=jax.ShapeDtypeStruct((Z, R, 3 * S), BF),
        in_specs=[
            SMEM,
            pl.BlockSpec((2, E, R, W), lambda i: (0, 0, 0, 0)),
            pl.BlockSpec((2, 3, W, S), lambda i: (i, 0, 0, 0)),
        ],
        out_specs=pl.BlockSpec((2, R, 3 * S), lambda i: (i, 0, 0)),
        name="first",
    )(expert, x, weight)


def middle_kernel(part_ref, out_ref):
    total = part_ref[0].astype(F32)
    for d in range(1, G):
        total = total + part_ref[d].astype(F32)
    gate = total[:, 0:S]
    up = total[:, S : 2 * S]
    hidden_grad = total[:, 2 * S : 3 * S]
    sigmoid = jax.nn.sigmoid(gate)
    activated = gate * sigmoid
    hidden = (activated * up).astype(BF)
    gate_grad = (hidden_grad * up * sigmoid * (1.0 + gate * (1.0 - sigmoid))).astype(BF)
    up_grad = (hidden_grad * activated).astype(BF)
    for d in range(G):
        out_ref[d, :, 0:S] = hidden
        out_ref[d, :, S : 2 * S] = gate_grad
        out_ref[d, :, 2 * S : 3 * S] = up_grad


def middle(parts):
    block = pl.BlockSpec((G, H // 4, 3 * S), lambda i: (0, i, 0))
    return pl.pallas_call(
        middle_kernel,
        grid=(4,),
        out_shape=jax.ShapeDtypeStruct((G, H, 3 * S), BF),
        in_specs=[block],
        out_specs=block,
        name="middle",
    )(parts)


def weigh_kernel(expert_ref, xt_ref, act_ref, grad_ref, mark_ref):
    for i in range(2):
        e = expert_ref[2 * pl.program_id(0) + i]
        both = dot(xt_ref[0, e], act_ref[i, :, S : 3 * S])
        grad_ref[i, 0] = both[:, 0:S].astype(BF)
        grad_ref[i, 1] = both[:, S : 2 * S].astype(BF)
        grad_ref[i, 2] = dot(xt_ref[1, e], act_ref[i, :, 0:S]).astype(BF)
    mark_ref[...] = jnp.zeros_like(mark_ref)


def weigh(expert, xt, act):
    return pl.pallas_call(
        weigh_kernel,
        grid=(Z // 2,),
        out_shape=(jax.ShapeDtypeStruct((Z, 3, W, S), BF), jax.ShapeDtypeStruct((8, 128), F32)),
        in_specs=[
            SMEM,
            pl.BlockSpec((2, E, W, R), lambda i: (0, 0, 0, 0)),
            pl.BlockSpec((2, R, 3 * S), lambda i: (i, 0, 0)),
        ],
        out_specs=(pl.BlockSpec((2, 3, W, S), lambda i: (i, 0, 0, 0)), pl.BlockSpec((8, 128), lambda i: (0, 0))),
        name="weigh",
    )(expert, xt, act)


def last_kernel(expert_ref, weight_ref, act_ref, mark_ref, out_ref, acc_ref):
    acc_ref[...] = jnp.zeros_like(acc_ref)
    tail = ((1,), (1,))

    def step(z, carry):
        e = expert_ref[z]
        acc_ref[0, e] += dot(act_ref[z, :, 0:S], weight_ref[z, 2], tail)
        both = jnp.concatenate([weight_ref[z, 0], weight_ref[z, 1]], axis=1)
        acc_ref[1, e] += dot(act_ref[z, :, S : 3 * S], both, tail)
        return carry

    lax.fori_loop(0, Z, step, 0)
    size = E * Q
    i = lax.broadcasted_iota(jnp.int32, (size, size), 0)
    j = lax.broadcasted_iota(jnp.int32, (size, size), 1)
    swap = ((i // (E * C) == j % G) & (i % (E * C) == j // G)).astype(F32).astype(BF)
    for n in range(N):
        for t in range(2):
            rows = jnp.concatenate([acc_ref[t, e, n * Q : (n + 1) * Q, :].astype(BF) for e in range(E)], axis=0)
            moved = dot(swap, rows).astype(BF)
            for h in range(G):
                out_ref[n * G + h, t * G : (t + 1) * G, 0:W] = moved[h * E * C : (h + 1) * E * C, :]
                out_ref[n * G + h, t * G : (t + 1) * G, W:WP] = jnp.zeros((E * C, WP - W), BF)


def last(expert, weight, act, mark):
    return pl.pallas_call(
        last_kernel,
        out_shape=jax.ShapeDtypeStruct((N * G, 2 * G, WP), BF),
        in_specs=[SMEM, VMEM, VMEM, ANY],
        out_specs=VMEM,
        scratch_shapes=[pltpu.VMEM((2, E, R, W), F32)],
        name="last",
    )(expert, weight, act, mark)


def unpack_kernel(recv_ref, layer_ref, grad_ref):
    low = lax.broadcasted_iota(jnp.int32, (G, 128), 1) < W - 256
    for t, ref in enumerate((layer_ref, grad_ref)):
        rows = slice(t * G, (t + 1) * G)
        for d in range(0, G, 2):
            left = recv_ref[d, rows, :].astype(F32)
            right = recv_ref[d + 1, rows, :].astype(F32)
            for n in range(1, N):
                left = left + recv_ref[n * G + d, rows, :].astype(F32)
                right = right + recv_ref[n * G + d + 1, rows, :].astype(F32)
            right = pltpu.roll(right, W - 256, 1)
            at = d * W
            ref[:, at : at + 256] = left[:, 0:256].astype(BF)
            ref[:, at + 256 : at + 384] = jnp.where(low, left[:, 256:384], right[:, 0:128]).astype(BF)
            ref[:, at + 384 : at + 640] = right[:, 128:384].astype(BF)


def unpack(recv):
    shape = jax.ShapeDtypeStruct((E * C, D), BF)
    return pl.pallas_call(
        unpack_kernel, out_shape=(shape, shape), in_specs=[VMEM], out_specs=(VMEM, VMEM), name="unpack"
    )(recv)


def widen_kernel(own_ref, gate_up_ref, down_ref):
    gate_up_ref[0] = own_ref[0, 0:2].astype(F32)
    down_ref[0] = own_ref[0, 2].astype(F32)


def widen(own):
    return pl.pallas_call(
        widen_kernel,
        out_shape=(jax.ShapeDtypeStruct((1, 2, W, S), F32), jax.ShapeDtypeStruct((1, W, S), F32)),
        in_specs=[VMEM],
        out_specs=(VMEM, VMEM),
        name="widen",
    )(own)


def exchange(x, axes):
    return lax.all_to_all(x, axes, split_axis=0, concat_axis=0, tiled=True)


def body(tokens, cotangent, counts, destination, placement, gate_up_weight, down_weight):
    me = lax.axis_index(GRP).reshape(1).astype(jnp.int32)
    local = jnp.concatenate([gate_up_weight[0], down_weight], axis=0)
    weight = lax.all_gather(local[None], "z_hi", axis=0, tiled=True)
    x, xt = prepare(exchange(pack(me, counts[0, 0], destination[0], tokens[0], cotangent[0]), PLANE))
    near = lax.dynamic_index_in_dim(placement.reshape(Z, N), lax.axis_index(NEAR), 1, keepdims=False)
    expert = near // (Z * N // E)
    parts = exchange(first(expert, x, weight).reshape(G, H, 3 * S), GRP)
    act = exchange(middle(parts), GRP).reshape(Z, R, 3 * S)
    grads, mark = weigh(expert, xt, act)
    own = lax.psum_scatter(grads, "z_hi", scatter_dimension=0, tiled=True)
    layer_out, input_grad = unpack(exchange(last(expert, weight, act, mark), PLANE))
    gate_up_grad, down_grad = widen(own)
    return (layer_out[None], input_grad[None], gate_up_grad, down_grad)


def solution(mesh):
    fine = Mesh(mesh.devices.reshape(SIZES), AXES)
    return jax.shard_map(
        body,
        mesh=fine,
        in_specs=(
            P(GRP, EP, None),
            P(GRP, EP, None),
            P(GRP, EP, None),
            P(GRP, EP, None),
            P(),
            P(EP, None, GRP, None),
            P(EP, GRP, None),
        ),
        out_specs=(
            P(GRP, EP, None),
            P(GRP, EP, None),
            P(EP, None, GRP, None),
            P(EP, GRP, None),
        ),
        check_vma=False,
    )
```

time: 266 us -> 246 us (0.925)
  the two profiles are of different devices: /device:TPU:4 before, /device:TPU:8 now
where the time goes in v2:
time: 246 us; the launch traced here: 245 us
  waiting for transfers between devices  126 us (51%)
  blocking collectives  54.4 us (22%)
  Pallas kernels  29.7 us (12%)
  starting transfers between devices  17.1 us (7%)
  between operations  14.1 us (6%)
  local copies, waits for them, and re-layouts  2.58 us (1%)
    reduce_scatter x1, waiting for transfers between devices, body(): own = lax.psum_scatter(grads, 'z_hi', scatter_dimension=0, tiled=True)  63.5 us
    all_to_all x2, blocking collectives, exchange(): return lax.all_to_all(x, axes, split_axis=0, concat_axis=0, tiled=True)  54.4 us
    all_gather x1, waiting for transfers between devices, body(): weight = lax.all_gather(local[None], 'z_hi', axis=0, tiled=True)  41.5 us
    all_to_all x2, waiting for transfers between devices, exchange(): return lax.all_to_all(x, axes, split_axis=0, concat_axis=0, tiled=True)  20.2 us
    all_to_all x2, starting transfers between devices, exchange(): return lax.all_to_all(x, axes, split_axis=0, concat_axis=0, tiled=True)  17 us
    pallas_call x1, Pallas kernels, last(): pl.pallas_call(last_kernel, out_shape=jax.ShapeDtypeStruct((N * G, 2 * G,...  6.36 us
    pallas_call x1, Pallas kernels, first(): pl.pallas_call(first_kernel, grid=(Z // 2,), out_shape=jax.ShapeDtypeStru...  4.95 us
  transfers between devices with their start and end apart: 4, of which 3 were waited for; matrix products, arithmetic and copies ran while one was open for 1% of the time, Pallas kernels for 2%

profile of v2, /device:TPU:8, one launch (start us, length us, event | category | flops | bytes accessed | tf_op | source)
XLA Modules:
  0.0 245.2 jit_solution(12726782691178734548)
XLA Ops:
  7.2 2.5 %pack.1 = bf16[64,32,384]{2,1,0:T(8,128)(2,1)} custom-call(s32[1]{0:T(128)} %bitcast.2.me_ref, s32[4]{0:T(128)} %bitcast.19, s32[1,16]{1,0:T(1,128)} %bitcast.20, bf16[16,5120]{1,0:T(8,128)(2,1)} %bitcast.17, bf16[16,5120]{1,0:T(8,128)(2,1)} %bitcast.18), custom_call_target="tpu_custom_call" | custom-call | tf_op jit(solution)/shard_map/pack/pallas_call | solution.py:59
  9.7 0.0 copy-start.2
  9.7 0.0 copy-start.3
  9.7 0.0 copy-start.4
  9.7 10.1 %all-to-all-start = ((bf16[64,32,384]{2,1,0:T(8,128)(2,1)}), bf16[64,32,384]{2,1,0:T(8,128)(2,1)S(1)}, u32[]{:S(2)}, u32[]{:S(2)}) async-start(bf16[64,32,384]{2,1,0:T(8,128)(2,1)} %pack.1), calls=%async_computation | async-start | bytes 3145728 | tf_op jit(solution)/shard_map/all_to_all | solution.py:251
  19.8 0.0 all-gather.3.cloned.1.call-start
  19.9 0.0 copy-done.2
  19.9 0.0 copy-done.3
  19.9 0.7 pad_maximum_fusion
  20.6 0.0 all-gather.3.cloned.1.call-update
  20.6 0.0 copy-done.4
  20.6 0.1 reshape.20
  20.7 0.2 dynamic-slice_reduce_fusion
  20.9 0.5 and_select_fusion.expert_ref
  21.4 20.2 %all-to-all-done.recv_ref = bf16[64,32,384]{2,1,0:T(8,128)(2,1)S(1)} async-done(((bf16[64,32,384]{2,1,0:T(8,128)(2,1)}), bf16[64,32,384]{2,1,0:T(8,128)(2,1)S(1)}, u32[]{:S(2)}, u32[]{:S(2)}) %all-to-all-start) | async-done | bytes 1572896 | tf_op jit(solution)/shard_map/all_to_all | solution.py:251
  41.7 0.0 copy-start
  41.7 1.1 copy-done
  42.8 3.4 %prepare.1 = (bf16[2,4,256,320]{3,2,1,0:T(8,128)(2,1)}, bf16[2,4,320,256]{3,2,1,0:T(8,128)(2,1)}) custom-call(bf16[64,32,384]{2,1,0:T(8,128)(2,1)} %copy-done), custom_call_target="tpu_custom_call" | custom-call | tf_op jit(solution)/shard_map/prepare/pallas_call | solution.py:88
  46.2 41.5 %all-gather.3.cloned.1.call-done = bf16[24,320,128]{2,1,0:T(8,128)(2,1)} async-done(((bf16[3,320,128]{2,1,0:T(8,128)(2,1)}), bf16[24,320,128]{2,1,0:T(8,128)(2,1)}) %all-gather.3.cloned.1.call-update) | async-done | bytes 1966096 | tf_op jit(solution)/shard_map/all_gather | solution.py:257
  87.7 4.9 %first.1 = bf16[8,256,384]{2,1,0:T(8,128)(2,1)} custom-call(s32[8]{0:T(128)} %and_select_fusion.expert_ref, bf16[2,4,256,320]{3,2,1,0:T(8,128)(2,1)} %get-tuple-element.12.x_ref, bf16[8,3,320,128]{3,2,1,0:T(8,128)(2,1)} %bitcast.13), custom_call_target="tpu_custom_call" | custom-call | tf_op jit(solution)/shard_map/first/pallas_call | solution.py:106
  92.7 28.0 %all_to_all.20.part_ref = bf16[16,128,384]{2,1,0:T(8,128)(2,1)} all-to-all(bf16[16,128,384]{2,1,0:T(8,128)(2,1)} %bitcast.15), channel_id=1, replica_groups=mesh['y_lo'=2,'x'=4,'core'=2,'z_hi'=8,'z_lo'=2,'y_hi'=2] {'y_lo','x','co..., dimensions={0} | all-to-all | bytes 3145728 | tf_op jit(solution)/shard_map/all_to_all | solution.py:251
  120.7 3.7 %middle.1 = bf16[16,128,384]{2,1,0:T(8,128)(2,1)} custom-call(bf16[16,128,384]{2,1,0:T(8,128)(2,1)} %all_to_all.20.part_ref), custom_call_target="tpu_custom_call" | custom-call | tf_op jit(solution)/shard_map/middle/pallas_call | solution.py:140
  124.4 26.4 %all_to_all.21 = bf16[16,128,384]{2,1,0:T(8,128)(2,1)} all-to-all(bf16[16,128,384]{2,1,0:T(8,128)(2,1)} %middle.1), channel_id=1, replica_groups=mesh['y_lo'=2,'x'=4,'core'=2,'z_hi'=8,'z_lo'=2,'y_hi'=2] {'y_lo','x','co..., dimensions={0} | all-to-all | bytes 3145728 | tf_op jit(solution)/shard_map/all_to_all | solution.py:251
  150.8 4.7 %weigh.1 = (bf16[8,3,320,128]{3,2,1,0:T(8,128)(2,1)}, f32[8,128]{1,0:T(8,128)}) custom-call(s32[8]{0:T(128)} %and_select_fusion.expert_ref, bf16[2,4,320,256]{3,2,1,0:T(8,128)(2,1)} %get-tuple-element.13.xt_ref, bf16[8,256,384]{2,1,0:T(8,128)(2,1)} %bitcast.11), custom_call_target="tpu_custom_call" | custom-call | tf_op jit(solution)/shard_map/weigh/pallas_call | solution.py:161
  155.5 6.4 %last.1 = bf16[64,32,384]{2,1,0:T(8,128)(2,1)} custom-call(s32[8]{0:T(128)} %and_select_fusion.expert_ref, bf16[8,3,320,128]{3,2,1,0:T(8,128)(2,1)} %bitcast.14, bf16[8,256,384]{2,1,0:T(8,128)(2,1)} %bitcast.12, f32[8,128]{1,0:T(8,128)} %get-tuple-element.14.mark_ref), custom_call_target="tpu_custom_call" | custom-call | tf_op jit(solution)/shard_map/last/pallas_call | solution.py:201
  161.9 6.9 %all-to-all-start.3 = ((bf16[64,32,384]{2,1,0:T(8,128)(2,1)}), bf16[64,32,384]{2,1,0:T(8,128)(2,1)S(1)}, u32[]{:S(2)}, u32[]{:S(2)}) async-start(bf16[64,32,384]{2,1,0:T(8,128)(2,1)} %last.1), calls=%async_computation.3 | async-start | bytes 3145728 | tf_op jit(solution)/shard_map/all_to_all | solution.py:251
  168.8 0.0 reduce-scatter.2.cloned.1.call-start
  168.9 0.7 reduce-scatter.2.cloned.1.call-update
  169.6 63.5 %reduce-scatter.2.cloned.1.call-done.own_ref = bf16[1,3,320,128]{3,2,1,0:T(8,128)(2,1)} async-done(((bf16[8,3,320,128]{3,2,1,0:T(8,128)(2,1)}), bf16[1,3,320,128]{3,2,1,0:T(8,128)(2,1)}) %reduce-scatter.2.cloned.1.call-update) | async-done | bytes 245776 | tf_op jit(solution)/shard_map/reduce_scatter | solution.py:264
  233.1 1.7 widen.1
  234.9 0.0 all-to-all-done.3.recv_ref
  234.9 0.0 copy-start.1
  234.9 1.2 copy-done.1
  236.0 2.3 unpack.1
Async XLA Ops:
  9.7 10.2 %copy-start.2 = (bf16[1,2,320,128]{3,2,1,0:T(8,128)(2,1)S(1)}, bf16[1,2,320,128]{3,2,1,0:T(8,128)(2,1)}, u32[]{:S(2)}) copy-start(bf16[1,2,320,128]{3,2,1,0:T(8,128)(2,1)} %param.12) | copy-start | bytes 491524
  9.7 10.2 %copy-start.3 = (bf16[1,320,128]{2,1,0:T(8,128)(2,1)S(1)}, bf16[1,320,128]{2,1,0:T(8,128)(2,1)}, u32[]{:S(2)}) copy-start(bf16[1,320,128]{2,1,0:T(8,128)(2,1)} %param.13) | copy-start | bytes 245764
  9.7 10.9 %copy-start.4 = (s32[32]{0:T(128)S(1)}, s32[32]{0:T(128)}, u32[]{:S(2)}) copy-start(s32[32]{0:T(128)} %param.11) | copy-start | bytes 388
  9.7 32.0 %all-to-all-start = ((bf16[64,32,384]{2,1,0:T(8,128)(2,1)}), bf16[64,32,384]{2,1,0:T(8,128)(2,1)S(1)}, u32[]{:S(2)}, u32[]{:S(2)}) async-start(bf16[64,32,384]{2,1,0:T(8,128)(2,1)} %pack.1), calls=%async_computation | async-start | bytes 3145728 | tf_op jit(solution)/shard_map/all_to_all | solution.py:251
  19.8 67.9 %all-gather.3.cloned.1.call-start = ((), (), s32[]{:S(2)}) async-start(), calls=%async_computation.6 | async-start | bytes 2211840 | tf_op jit(solution)/shard_map/all_gather | solution.py:257
  41.7 1.1 copy-start
  161.9 73.0 %all-to-all-start.3 = ((bf16[64,32,384]{2,1,0:T(8,128)(2,1)}), bf16[64,32,384]{2,1,0:T(8,128)(2,1)S(1)}, u32[]{:S(2)}, u32[]{:S(2)}) async-start(bf16[64,32,384]{2,1,0:T(8,128)(2,1)} %last.1), calls=%async_computation.3 | async-start | bytes 3145728 | tf_op jit(solution)/shard_map/all_to_all | solution.py:251
  168.8 64.3 %reduce-scatter.2.cloned.1.call-start = ((), (), s32[]{:S(2)}) async-start(), calls=%async_computation.5 | async-start | bytes 2211840 | tf_op jit(solution)/shard_map/reduce_scatter | solution.py:264
  234.9 1.2 copy-start.1
Sparse Core Ops, SparseCore 0:
  23.3 64.4 all-gather.2
  172.5 60.5 reduce-scatter.1

commit v3 on v2

--- a/solution.py
+++ b/solution.py
@@ -4,6 +4,7 @@
 from jax.experimental import pallas as pl
 from jax.experimental.pallas import tpu as pltpu
 from jax.sharding import Mesh, PartitionSpec as P
+
 
 AXES = ("y_lo", "x", "core", "z_hi", "z_lo", "y_hi")
 SIZES = (2, 4, 2, 8, 2, 2)
@@ -28,7 +29,6 @@
 F32 = jnp.float32
 VMEM = pl.BlockSpec(memory_space=pltpu.VMEM)
 SMEM = pl.BlockSpec(memory_space=pltpu.SMEM)
-ANY = pl.BlockSpec(memory_space=pl.ANY)
 
 
 def dot(a, b, dims=((1,), (0,))):
@@ -94,15 +94,15 @@
     )(recv)
 
 
-def first_kernel(expert_ref, x_ref, weight_ref, out_ref):
+def first_kernel(expert_ref, x_ref, gate_up_ref, down_ref, out_ref):
     for i in range(2):
         e = expert_ref[2 * pl.program_id(0) + i]
-        tok = x_ref[0, e]
-        out_ref[i, :, 0 : 2 * S] = dot(tok, jnp.concatenate([weight_ref[i, 0], weight_ref[i, 1]], axis=1)).astype(BF)
-        out_ref[i, :, 2 * S : 3 * S] = dot(x_ref[1, e], weight_ref[i, 2]).astype(BF)
-
-
-def first(expert, x, weight):
+        both = jnp.concatenate([gate_up_ref[i, 0], gate_up_ref[i, 1]], axis=1)
+        out_ref[i, :, 0 : 2 * S] = dot(x_ref[0, e], both).astype(BF)
+        out_ref[i, :, 2 * S : 3 * S] = dot(x_ref[1, e], down_ref[i]).astype(BF)
+
+
+def first(expert, x, gate_up, down):
     return pl.pallas_call(
         first_kernel,
         grid=(Z // 2,),
@@ -110,11 +110,12 @@
         in_specs=[
             SMEM,
             pl.BlockSpec((2, E, R, W), lambda i: (0, 0, 0, 0)),
-            pl.BlockSpec((2, 3, W, S), lambda i: (i, 0, 0, 0)),
+            pl.BlockSpec((2, 2, W, S), lambda i: (i, 0, 0, 0)),
+            pl.BlockSpec((2, W, S), lambda i: (i, 0, 0)),
         ],
         out_specs=pl.BlockSpec((2, R, 3 * S), lambda i: (i, 0, 0)),
         name="first",
-    )(expert, x, weight)
+    )(expert, x, gate_up, down)
 
 
 def middle_kernel(part_ref, out_ref):
@@ -147,39 +148,38 @@
     )(parts)
 
 
-def weigh_kernel(expert_ref, xt_ref, act_ref, grad_ref, mark_ref):
+def weigh_kernel(expert_ref, xt_ref, act_ref, out_ref):
     for i in range(2):
         e = expert_ref[2 * pl.program_id(0) + i]
         both = dot(xt_ref[0, e], act_ref[i, :, S : 3 * S])
-        grad_ref[i, 0] = both[:, 0:S].astype(BF)
-        grad_ref[i, 1] = both[:, S : 2 * S].astype(BF)
-        grad_ref[i, 2] = dot(xt_ref[1, e], act_ref[i, :, 0:S]).astype(BF)
-    mark_ref[...] = jnp.zeros_like(mark_ref)
+        out_ref[i, 0] = both[:, 0:S].astype(BF)
+        out_ref[i, 1] = both[:, S : 2 * S].astype(BF)
+        out_ref[i, 2] = dot(xt_ref[1, e], act_ref[i, :, 0:S]).astype(BF)
 
 
 def weigh(expert, xt, act):
     return pl.pallas_call(
         weigh_kernel,
         grid=(Z // 2,),
-        out_shape=(jax.ShapeDtypeStruct((Z, 3, W, S), BF), jax.ShapeDtypeStruct((8, 128), F32)),
+        out_shape=jax.ShapeDtypeStruct((Z, 3, W, S), BF),
         in_specs=[
             SMEM,
             pl.BlockSpec((2, E, W, R), lambda i: (0, 0, 0, 0)),
             pl.BlockSpec((2, R, 3 * S), lambda i: (i, 0, 0)),
         ],
-        out_specs=(pl.BlockSpec((2, 3, W, S), lambda i: (i, 0, 0, 0)), pl.BlockSpec((8, 128), lambda i: (0, 0))),
+        out_specs=pl.BlockSpec((2, 3, W, S), lambda i: (i, 0, 0, 0)),
         name="weigh",
     )(expert, xt, act)
 
 
-def last_kernel(expert_ref, weight_ref, act_ref, mark_ref, out_ref, acc_ref):
+def last_kernel(expert_ref, gate_up_ref, down_ref, act_ref, out_ref, acc_ref):
     acc_ref[...] = jnp.zeros_like(acc_ref)
     tail = ((1,), (1,))
 
     def step(z, carry):
         e = expert_ref[z]
-        acc_ref[0, e] += dot(act_ref[z, :, 0:S], weight_ref[z, 2], tail)
-        both = jnp.concatenate([weight_ref[z, 0], weight_ref[z, 1]], axis=1)
+        acc_ref[0, e] += dot(act_ref[z, :, 0:S], down_ref[z], tail)
+        both = jnp.concatenate([gate_up_ref[z, 0], gate_up_ref[z, 1]], axis=1)
         acc_ref[1, e] += dot(act_ref[z, :, S : 3 * S], both, tail)
         return carry
 
@@ -197,15 +197,15 @@
                 out_ref[n * G + h, t * G : (t + 1) * G, W:WP] = jnp.zeros((E * C, WP - W), BF)
 
 
-def last(expert, weight, act, mark):
+def last(expert, gate_up, down, act):
     return pl.pallas_call(
         last_kernel,
         out_shape=jax.ShapeDtypeStruct((N * G, 2 * G, WP), BF),
-        in_specs=[SMEM, VMEM, VMEM, ANY],
+        in_specs=[SMEM, VMEM, VMEM, VMEM],
         out_specs=VMEM,
         scratch_shapes=[pltpu.VMEM((2, E, R, W), F32)],
         name="last",
-    )(expert, weight, act, mark)
+    )(expert, gate_up, down, act)
 
 
 def unpack_kernel(recv_ref, layer_ref, grad_ref):
@@ -251,18 +251,28 @@
     return lax.all_to_all(x, axes, split_axis=0, concat_axis=0, tiled=True)
 
 
+def gather(x):
+    return lax.all_gather(x, "z_hi", axis=0, tiled=True)
+
+
+def scatter(x):
+    return lax.psum_scatter(x, "z_hi", scatter_dimension=0, tiled=True)
+
+
 def body(tokens, cotangent, counts, destination, placement, gate_up_weight, down_weight):
+    gate_up = gather(gate_up_weight)
+    down = gather(down_weight)
     me = lax.axis_index(GRP).reshape(1).astype(jnp.int32)
-    local = jnp.concatenate([gate_up_weight[0], down_weight], axis=0)
-    weight = lax.all_gather(local[None], "z_hi", axis=0, tiled=True)
-    x, xt = prepare(exchange(pack(me, counts[0, 0], destination[0], tokens[0], cotangent[0]), PLANE))
     near = lax.dynamic_index_in_dim(placement.reshape(Z, N), lax.axis_index(NEAR), 1, keepdims=False)
     expert = near // (Z * N // E)
-    parts = exchange(first(expert, x, weight).reshape(G, H, 3 * S), GRP)
-    act = exchange(middle(parts), GRP).reshape(Z, R, 3 * S)
-    grads, mark = weigh(expert, xt, act)
-    own = lax.psum_scatter(grads, "z_hi", scatter_dimension=0, tiled=True)
-    layer_out, input_grad = unpack(exchange(last(expert, weight, act, mark), PLANE))
+    sent = pack(me, counts[0, 0], destination[0], tokens[0], cotangent[0])
+    x, xt = prepare(exchange(sent, PLANE))
+    parts = first(expert, x, gate_up, down).reshape(G, H, 3 * S)
+    act = middle(exchange(parts, GRP))
+    act = exchange(act, GRP).reshape(Z, R, 3 * S)
+    own = scatter(weigh(expert, xt, act))
+    out = last(expert, gate_up, down, act)
+    layer_out, input_grad = unpack(exchange(out, PLANE))
     gate_up_grad, down_grad = widen(own)
     return (layer_out[None], input_grad[None], gate_up_grad, down_grad)
 

time: 246 us -> 240 us (0.976)
  the two profiles are of different devices: /device:TPU:8 before, /device:TPU:2 now
where the time goes in v3:
time: 240 us; the launch traced here: 239 us
  blocking collectives  111 us (46%)
  waiting for transfers between devices  62.7 us (26%)
  Pallas kernels  29.6 us (12%)
  starting transfers between devices  19 us (8%)
  between operations  14.1 us (6%)
  local copies, waits for them, and re-layouts  2.63 us (1%)
    reduce_scatter x1, waiting for transfers between devices, scatter(): return lax.psum_scatter(x, 'z_hi', scatter_dimension=0, tiled=True)  59.9 us
    all_gather x1, blocking collectives, gather(): return lax.all_gather(x, 'z_hi', axis=0, tiled=True)  59.1 us
    all_to_all x2, blocking collectives, exchange(): return lax.all_to_all(x, axes, split_axis=0, concat_axis=0, tiled=True)  51.7 us
    all_to_all x2, starting transfers between devices, exchange(): return lax.all_to_all(x, axes, split_axis=0, concat_axis=0, tiled=True)  18.9 us
    pallas_call x1, Pallas kernels, last(): pl.pallas_call(last_kernel, out_shape=jax.ShapeDtypeStruct((N * G, 2 * G,...  6.35 us
    pallas_call x1, Pallas kernels, first(): pl.pallas_call(first_kernel, grid=(Z // 2,), out_shape=jax.ShapeDtypeStru...  4.96 us
  transfers between devices with their start and end apart: 4, of which 2 were waited for; matrix products, arithmetic and copies ran while one was open for 0% of the time, Pallas kernels for 4%

profile of v3, /device:TPU:2, one launch (start us, length us, event | category | flops | bytes accessed | tf_op | source)
XLA Modules:
  0.0 239.3 jit_solution(2694620504568633214)
XLA Ops:
  7.2 2.5 %pack.1 = bf16[64,32,384]{2,1,0:T(8,128)(2,1)} custom-call(s32[1]{0:T(128)} %bitcast.me_ref, s32[4]{0:T(128)} %bitcast.14, s32[1,16]{1,0:T(1,128)} %bitcast.15, bf16[16,5120]{1,0:T(8,128)(2,1)} %bitcast.12, bf16[16,5120]{1,0:T(8,128)(2,1)} %bitcast.13), custom_call_target="tpu_custom_call" | custom-call | tf_op jit(solution)/shard_map/pack/pallas_call | solution.py:59
  9.7 0.0 copy-start.3
  9.7 0.0 copy-start.2
  9.7 10.1 %all-to-all-start = ((bf16[64,32,384]{2,1,0:T(8,128)(2,1)}), bf16[64,32,384]{2,1,0:T(8,128)(2,1)S(1)}, u32[]{:S(2)}, u32[]{:S(2)}) async-start(bf16[64,32,384]{2,1,0:T(8,128)(2,1)} %pack.1), calls=%async_computation | async-start | bytes 3145728 | tf_op jit(solution)/shard_map/all_to_all | solution.py:251
  19.8 0.0 all-gather.2.cloned.1.call-start
  19.9 0.7 all-gather.2.cloned.1.call-update
  20.6 0.0 copy-done.3
  20.6 0.1 reshape.20
  20.7 0.2 dynamic-slice_reduce_fusion
  20.8 0.5 and_select_fusion.expert_ref
  21.4 0.0 copy-done.2
  21.4 59.1 %all_gather.7.down_ref = bf16[8,320,128]{2,1,0:T(8,128)(2,1)} all-gather(bf16[1,320,128]{2,1,0:T(8,128)(2,1)S(1)} %copy-done.2), channel_id=1, replica_groups=mesh['y_lo'=2,'x'=4,'core'=2,'z_hi'=8,'z_lo'=2,'y_hi'=2] {'z_hi'}, dimensions={0}, use_global_device_ids=true | all-gather | bytes 737280 | tf_op jit(solution)/shard_map/all_gather | solution.py:255
  80.5 0.0 all-to-all-done.recv_ref
  80.5 0.0 copy-start
  80.5 1.2 copy-done
  81.7 3.4 %prepare.1 = (bf16[2,4,256,320]{3,2,1,0:T(8,128)(2,1)}, bf16[2,4,320,256]{3,2,1,0:T(8,128)(2,1)}) custom-call(bf16[64,32,384]{2,1,0:T(8,128)(2,1)} %copy-done), custom_call_target="tpu_custom_call" | custom-call | tf_op jit(solution)/shard_map/prepare/pallas_call | solution.py:88
  85.0 2.1 all-gather.2.cloned.1.call-done.gate_up_ref
  87.2 5.0 %first.1 = bf16[8,256,384]{2,1,0:T(8,128)(2,1)} custom-call(s32[8]{0:T(128)} %and_select_fusion.expert_ref, bf16[2,4,256,320]{3,2,1,0:T(8,128)(2,1)} %get-tuple-element.10.x_ref, bf16[8,2,320,128]{3,2,1,0:T(8,128)(2,1)} %all-gather.2.cloned.1.call-done.gate_up_ref, bf16[8,320,128]{2,1,0:T(8,128)(2,1)} %all_gather.7.down_ref), custom_call_target="tpu_custom_call" | custom-call | tf_op jit(solution)/shard_map/first/pallas_call | solution.py:106
  92.1 25.2 %all_to_all.20.part_ref = bf16[16,128,384]{2,1,0:T(8,128)(2,1)} all-to-all(bf16[16,128,384]{2,1,0:T(8,128)(2,1)} %bitcast.11), channel_id=1, replica_groups=mesh['y_lo'=2,'x'=4,'core'=2,'z_hi'=8,'z_lo'=2,'y_hi'=2] {'y_lo','x','co..., dimensions={0} | all-to-all | bytes 3145728 | tf_op jit(solution)/shard_map/all_to_all | solution.py:251
  117.3 3.7 %middle.1 = bf16[16,128,384]{2,1,0:T(8,128)(2,1)} custom-call(bf16[16,128,384]{2,1,0:T(8,128)(2,1)} %all_to_all.20.part_ref), custom_call_target="tpu_custom_call" | custom-call | tf_op jit(solution)/shard_map/middle/pallas_call | solution.py:141
  121.0 26.5 %all_to_all.21 = bf16[16,128,384]{2,1,0:T(8,128)(2,1)} all-to-all(bf16[16,128,384]{2,1,0:T(8,128)(2,1)} %middle.1), channel_id=1, replica_groups=mesh['y_lo'=2,'x'=4,'core'=2,'z_hi'=8,'z_lo'=2,'y_hi'=2] {'y_lo','x','co..., dimensions={0} | all-to-all | bytes 3145728 | tf_op jit(solution)/shard_map/all_to_all | solution.py:251
  147.5 6.3 %last.1 = bf16[64,32,384]{2,1,0:T(8,128)(2,1)} custom-call(s32[8]{0:T(128)} %and_select_fusion.expert_ref, bf16[8,2,320,128]{3,2,1,0:T(8,128)(2,1)} %all-gather.2.cloned.1.call-done.gate_up_ref, bf16[8,320,128]{2,1,0:T(8,128)(2,1)} %all_gather.7.down_ref, bf16[8,256,384]{2,1,0:T(8,128)(2,1)} %bitcast.9), custom_call_target="tpu_custom_call" | custom-call | tf_op jit(solution)/shard_map/last/pallas_call | solution.py:201
  153.8 8.8 %all-to-all-start.3 = ((bf16[64,32,384]{2,1,0:T(8,128)(2,1)}), bf16[64,32,384]{2,1,0:T(8,128)(2,1)S(1)}, u32[]{:S(2)}, u32[]{:S(2)}) async-start(bf16[64,32,384]{2,1,0:T(8,128)(2,1)} %last.1), calls=%async_computation.3 | async-start | bytes 3145728 | tf_op jit(solution)/shard_map/all_to_all | solution.py:251
  162.6 0.0 reduce-scatter.2.cloned.1.call-start
  162.6 4.7 %weigh.1 = bf16[8,3,320,128]{3,2,1,0:T(8,128)(2,1)} custom-call(s32[8]{0:T(128)} %and_select_fusion.expert_ref, bf16[2,4,320,256]{3,2,1,0:T(8,128)(2,1)} %get-tuple-element.13.xt_ref, bf16[8,256,384]{2,1,0:T(8,128)(2,1)} %bitcast.10), custom_call_target="tpu_custom_call" | custom-call | tf_op jit(solution)/shard_map/weigh/pallas_call | solution.py:161
  167.4 0.0 reduce-scatter.2.cloned.1.call-update
  167.4 59.9 %reduce-scatter.2.cloned.1.call-done.own_ref = bf16[1,3,320,128]{3,2,1,0:T(8,128)(2,1)} async-done(((bf16[8,3,320,128]{3,2,1,0:T(8,128)(2,1)}), bf16[1,3,320,128]{3,2,1,0:T(8,128)(2,1)}) %reduce-scatter.2.cloned.1.call-update) | async-done | bytes 245776 | tf_op jit(solution)/shard_map/reduce_scatter | solution.py:259
  227.3 1.7 widen.1
  229.0 0.0 all-to-all-done.3.recv_ref
  229.0 0.0 copy-start.1
  229.0 1.2 copy-done.1
  230.2 2.3 unpack.1
Async XLA Ops:
  9.7 10.9 %copy-start.3 = (s32[32]{0:T(128)S(1)}, s32[32]{0:T(128)}, u32[]{:S(2)}) copy-start(s32[32]{0:T(128)} %param.11) | copy-start | bytes 388
  9.7 11.7 %copy-start.2 = (bf16[1,320,128]{2,1,0:T(8,128)(2,1)S(1)}, bf16[1,320,128]{2,1,0:T(8,128)(2,1)}, u32[]{:S(2)}) copy-start(bf16[1,320,128]{2,1,0:T(8,128)(2,1)} %param.13) | copy-start | bytes 245764
  9.7 70.8 %all-to-all-start = ((bf16[64,32,384]{2,1,0:T(8,128)(2,1)}), bf16[64,32,384]{2,1,0:T(8,128)(2,1)S(1)}, u32[]{:S(2)}, u32[]{:S(2)}) async-start(bf16[64,32,384]{2,1,0:T(8,128)(2,1)} %pack.1), calls=%async_computation | async-start | bytes 3145728 | tf_op jit(solution)/shard_map/all_to_all | solution.py:251
  19.8 67.3 %all-gather.2.cloned.1.call-start = ((), (), s32[]{:S(2)}) async-start(), calls=%async_computation.5 | async-start | bytes 1474560 | tf_op jit(solution)/shard_map/all_gather | solution.py:255
  80.5 1.2 copy-start
  153.8 75.2 %all-to-all-start.3 = ((bf16[64,32,384]{2,1,0:T(8,128)(2,1)}), bf16[64,32,384]{2,1,0:T(8,128)(2,1)S(1)}, u32[]{:S(2)}, u32[]{:S(2)}) async-start(bf16[64,32,384]{2,1,0:T(8,128)(2,1)} %last.1), calls=%async_computation.3 | async-start | bytes 3145728 | tf_op jit(solution)/shard_map/all_to_all | solution.py:251
  162.6 64.7 %reduce-scatter.2.cloned.1.call-start = ((), (), s32[]{:S(2)}) async-start(), calls=%async_computation.6 | async-start | bytes 2211840 | tf_op jit(solution)/shard_map/reduce_scatter | solution.py:259
  229.0 1.2 copy-start.1
Sparse Core Ops, SparseCore 0:
  22.7 64.4 all-gather.1
  167.5 59.7 reduce-scatter.1

commit v4 on v3

--- a/solution.py
+++ b/solution.py
@@ -11,11 +11,12 @@
 GRP = ("y_lo", "x", "core")
 EP = ("z_hi", "z_lo", "y_hi")
 NEAR = ("z_lo", "y_hi")
-PLANE = NEAR + GRP
+PLANE = ("y_hi",) + GRP
 
 G = 16
 Z = 8
-N = 4
+Y = 2
+N = 2 * Y
 E = 4
 C = 4
 D = 5120
@@ -35,7 +36,7 @@
     return lax.dot_general(a, b, (dims, ((), ())), preferred_element_type=F32)
 
 
-def pack_kernel(me_ref, counts_ref, dest_ref, tok_ref, cot_ref, out_ref):
+def pack_kernel(me_ref, counts_ref, dest_ref, tok_ref, cot_ref, out_ref, one_ref):
     me = me_ref[0]
     rows = lax.broadcasted_iota(jnp.int32, (G, G), 0)
     pick = (rows == dest_ref[...]).astype(F32).astype(BF)
@@ -51,58 +52,64 @@
             if start != d * W:
                 moved = pltpu.roll(moved, WP - (d * W - start), 1)
             moved = jnp.where(lane < W, moved, extra).astype(BF)
-            for n in range(N):
-                out_ref[n * G + d, t * G : (t + 1) * G, :] = moved
+            one_ref[d, t * G : (t + 1) * G, :] = moved
+            for y in range(Y):
+                out_ref[y * G + d, t * G : (t + 1) * G, :] = moved
 
 
 def pack(me, counts, dest, tokens, cotangent):
     return pl.pallas_call(
         pack_kernel,
-        out_shape=jax.ShapeDtypeStruct((N * G, 2 * G, WP), BF),
+        out_shape=(
+            jax.ShapeDtypeStruct((Y * G, 2 * G, WP), BF),
+            jax.ShapeDtypeStruct((G, 2 * G, WP), BF),
+        ),
         in_specs=[SMEM, SMEM, VMEM, VMEM, VMEM],
-        out_specs=VMEM,
+        out_specs=(VMEM, VMEM),
         name="pack",
     )(me, counts, dest, tokens, cotangent)
 
 
-def rows_kernel(recv_ref, x_ref, xt_ref):
+def rows_kernel(own_ref, other_ref, x_ref, xt_ref):
     lane = lax.broadcasted_iota(jnp.int32, (G, 128), 1)
     for n in range(N):
+        recv_ref = (own_ref, other_ref)[n // Y]
+        first_block = n % Y * G
         table = jnp.zeros((G, 128), F32)
         for g in range(G):
-            table = table + recv_ref[n * G + g, 0:G, WP - 128 : WP].astype(F32)
+            table = table + recv_ref[first_block + g, 0:G, WP - 128 : WP].astype(F32)
         for e in range(E):
             kept = jnp.sum(jnp.where(lane == 128 - (WP - W) + e, table, 0.0), axis=1, keepdims=True)
             kept = jnp.broadcast_to(kept, (G, W))
             for c in range(C):
                 at = n * Q + c * G
                 for t in range(2):
-                    block = recv_ref[n * G + e * C + c, t * G : (t + 1) * G, 0:W].astype(F32)
+                    block = recv_ref[first_block + e * C + c, t * G : (t + 1) * G, 0:W].astype(F32)
                     x_ref[t, e, at : at + G, :] = jnp.where(kept > c + 0.5, block, 0.0).astype(BF)
     for t in range(2):
         for e in range(E):
             xt_ref[t, e] = x_ref[t, e].astype(F32).T.astype(BF)
 
 
-def prepare(recv):
+def prepare(own, other):
     return pl.pallas_call(
         rows_kernel,
         out_shape=(jax.ShapeDtypeStruct((2, E, R, W), BF), jax.ShapeDtypeStruct((2, E, W, R), BF)),
-        in_specs=[VMEM],
+        in_specs=[VMEM, VMEM],
         out_specs=(VMEM, VMEM),
         name="prepare",
-    )(recv)
-
-
-def first_kernel(expert_ref, x_ref, gate_up_ref, down_ref, out_ref):
+    )(own, other)
+
+
+def first_kernel(expert_ref, x_ref, weight_ref, out_ref):
     for i in range(2):
         e = expert_ref[2 * pl.program_id(0) + i]
-        both = jnp.concatenate([gate_up_ref[i, 0], gate_up_ref[i, 1]], axis=1)
+        both = jnp.concatenate([weight_ref[i, 0], weight_ref[i, 1]], axis=1)
         out_ref[i, :, 0 : 2 * S] = dot(x_ref[0, e], both).astype(BF)
-        out_ref[i, :, 2 * S : 3 * S] = dot(x_ref[1, e], down_ref[i]).astype(BF)
-
-
-def first(expert, x, gate_up, down):
+        out_ref[i, :, 2 * S : 3 * S] = dot(x_ref[1, e], weight_ref[i, 2]).astype(BF)
+
+
+def first(expert, x, weight):
     return pl.pallas_call(
         first_kernel,
         grid=(Z // 2,),
@@ -110,12 +117,11 @@
         in_specs=[
             SMEM,
             pl.BlockSpec((2, E, R, W), lambda i: (0, 0, 0, 0)),
-            pl.BlockSpec((2, 2, W, S), lambda i: (i, 0, 0, 0)),
-            pl.BlockSpec((2, W, S), lambda i: (i, 0, 0)),
+            pl.BlockSpec((2, 3, W, S), lambda i: (i, 0, 0, 0)),
         ],
         out_specs=pl.BlockSpec((2, R, 3 * S), lambda i: (i, 0, 0)),
         name="first",
-    )(expert, x, gate_up, down)
+    )(expert, x, weight)
 
 
 def middle_kernel(part_ref, out_ref):
@@ -172,14 +178,14 @@
     )(expert, xt, act)
 
 
-def last_kernel(expert_ref, gate_up_ref, down_ref, act_ref, out_ref, acc_ref):
+def last_kernel(expert_ref, weight_ref, act_ref, own_ref, other_ref, acc_ref):
     acc_ref[...] = jnp.zeros_like(acc_ref)
     tail = ((1,), (1,))
 
     def step(z, carry):
         e = expert_ref[z]
-        acc_ref[0, e] += dot(act_ref[z, :, 0:S], down_ref[z], tail)
-        both = jnp.concatenate([gate_up_ref[z, 0], gate_up_ref[z, 1]], axis=1)
+        acc_ref[0, e] += dot(act_ref[z, :, 0:S], weight_ref[z, 2], tail)
+        both = jnp.concatenate([weight_ref[z, 0], weight_ref[z, 1]], axis=1)
         acc_ref[1, e] += dot(act_ref[z, :, S : 3 * S], both, tail)
         return carry
 
@@ -189,47 +195,55 @@
     j = lax.broadcasted_iota(jnp.int32, (size, size), 1)
     swap = ((i // (E * C) == j % G) & (i % (E * C) == j // G)).astype(F32).astype(BF)
     for n in range(N):
+        out_ref = (own_ref, other_ref)[n // Y]
+        first_block = n % Y * G
         for t in range(2):
             rows = jnp.concatenate([acc_ref[t, e, n * Q : (n + 1) * Q, :].astype(BF) for e in range(E)], axis=0)
             moved = dot(swap, rows).astype(BF)
             for h in range(G):
-                out_ref[n * G + h, t * G : (t + 1) * G, 0:W] = moved[h * E * C : (h + 1) * E * C, :]
-                out_ref[n * G + h, t * G : (t + 1) * G, W:WP] = jnp.zeros((E * C, WP - W), BF)
-
-
-def last(expert, gate_up, down, act):
+                out_ref[first_block + h, t * G : (t + 1) * G, 0:W] = moved[h * E * C : (h + 1) * E * C, :]
+                out_ref[first_block + h, t * G : (t + 1) * G, W:WP] = jnp.zeros((E * C, WP - W), BF)
+
+
+def last(expert, weight, act):
+    shape = jax.ShapeDtypeStruct((Y * G, 2 * G, WP), BF)
     return pl.pallas_call(
         last_kernel,
-        out_shape=jax.ShapeDtypeStruct((N * G, 2 * G, WP), BF),
-        in_specs=[SMEM, VMEM, VMEM, VMEM],
-        out_specs=VMEM,
+        out_shape=(shape, shape),
+        in_specs=[SMEM, VMEM, VMEM],
+        out_specs=(VMEM, VMEM),
         scratch_shapes=[pltpu.VMEM((2, E, R, W), F32)],
         name="last",
-    )(expert, gate_up, down, act)
-
-
-def unpack_kernel(recv_ref, layer_ref, grad_ref):
+    )(expert, weight, act)
+
+
+def unpack_kernel(*refs):
+    recv_ref, layer_ref, grad_ref = refs[0], refs[-2], refs[-1]
+    add_refs = refs[1:-2]
     low = lax.broadcasted_iota(jnp.int32, (G, 128), 1) < W - 256
     for t, ref in enumerate((layer_ref, grad_ref)):
         rows = slice(t * G, (t + 1) * G)
         for d in range(0, G, 2):
-            left = recv_ref[d, rows, :].astype(F32)
-            right = recv_ref[d + 1, rows, :].astype(F32)
-            for n in range(1, N):
-                left = left + recv_ref[n * G + d, rows, :].astype(F32)
-                right = right + recv_ref[n * G + d + 1, rows, :].astype(F32)
+            left = recv_ref[d, rows, :].astype(F32) + recv_ref[G + d, rows, :].astype(F32)
+            right = recv_ref[d + 1, rows, :].astype(F32) + recv_ref[G + d + 1, rows, :].astype(F32)
             right = pltpu.roll(right, W - 256, 1)
             at = d * W
-            ref[:, at : at + 256] = left[:, 0:256].astype(BF)
-            ref[:, at + 256 : at + 384] = jnp.where(low, left[:, 256:384], right[:, 0:128]).astype(BF)
-            ref[:, at + 384 : at + 640] = right[:, 128:384].astype(BF)
-
-
-def unpack(recv):
+            cut = jnp.where(low, left[:, 256:384], right[:, 0:128])
+            for lo, hi, part in ((0, 256, left[:, 0:256]), (256, 384, cut), (384, 640, right[:, 128:384])):
+                if add_refs:
+                    part = part + add_refs[t][:, at + lo : at + hi].astype(F32)
+                ref[:, at + lo : at + hi] = part.astype(BF)
+
+
+def unpack(recv, *add):
     shape = jax.ShapeDtypeStruct((E * C, D), BF)
     return pl.pallas_call(
-        unpack_kernel, out_shape=(shape, shape), in_specs=[VMEM], out_specs=(VMEM, VMEM), name="unpack"
-    )(recv)
+        unpack_kernel,
+        out_shape=(shape, shape),
+        in_specs=[VMEM] * (1 + len(add)),
+        out_specs=(VMEM, VMEM),
+        name="unpack",
+    )(recv, *add)
 
 
 def widen_kernel(own_ref, gate_up_ref, down_ref):
@@ -259,21 +273,30 @@
     return lax.psum_scatter(x, "z_hi", scatter_dimension=0, tiled=True)
 
 
+def swap(*xs):
+    return [lax.ppermute(x, "z_lo", ((0, 1), (1, 0))) for x in xs]
+
+
 def body(tokens, cotangent, counts, destination, placement, gate_up_weight, down_weight):
-    gate_up = gather(gate_up_weight)
-    down = gather(down_weight)
+    local = jnp.concatenate([gate_up_weight, down_weight[:, None]], axis=1)
+    weight = gather(local)
     me = lax.axis_index(GRP).reshape(1).astype(jnp.int32)
     near = lax.dynamic_index_in_dim(placement.reshape(Z, N), lax.axis_index(NEAR), 1, keepdims=False)
     expert = near // (Z * N // E)
-    sent = pack(me, counts[0, 0], destination[0], tokens[0], cotangent[0])
-    x, xt = prepare(exchange(sent, PLANE))
-    parts = first(expert, x, gate_up, down).reshape(G, H, 3 * S)
+    sent, one = pack(me, counts[0, 0], destination[0], tokens[0], cotangent[0])
+    (other,) = swap(one)
+    own = exchange(sent, PLANE)
+    other = exchange(jnp.concatenate([other] * Y, axis=0), PLANE)
+    x, xt = prepare(own, other)
+    parts = first(expert, x, weight).reshape(G, H, 3 * S)
     act = middle(exchange(parts, GRP))
     act = exchange(act, GRP).reshape(Z, R, 3 * S)
-    own = scatter(weigh(expert, xt, act))
-    out = last(expert, gate_up, down, act)
-    layer_out, input_grad = unpack(exchange(out, PLANE))
-    gate_up_grad, down_grad = widen(own)
+    reduced = scatter(weigh(expert, xt, act))
+    own, other = last(expert, weight, act)
+    other = unpack(exchange(other, PLANE))
+    other = swap(*other)
+    layer_out, input_grad = unpack(exchange(own, PLANE), *other)
+    gate_up_grad, down_grad = widen(reduced)
     return (layer_out[None], input_grad[None], gate_up_grad, down_grad)
 
 

time: 240 us -> 220 us (0.917)
  the two profiles are of different devices: /device:TPU:2 before, /device:TPU:1 now
where the time goes in v4:
time: 220 us; the launch traced here: 219 us
  blocking collectives  75.3 us (34%)
  waiting for transfers between devices  61.6 us (28%)
  starting transfers between devices  31.4 us (14%)
  Pallas kernels  31.1 us (14%)
  between operations  14.1 us (6%)
  other arithmetic  3.18 us (1%)
    all_to_all x3, blocking collectives, exchange(): return lax.all_to_all(x, axes, split_axis=0, concat_axis=0, tiled=True)  75.3 us
    all_to_all x3, starting transfers between devices, exchange(): return lax.all_to_all(x, axes, split_axis=0, concat_axis=0, tiled=True)  24.2 us
    ppermute x3, waiting for transfers between devices, swap(): return [lax.ppermute(x, 'z_lo', ((0, 1), (1, 0))) for x in xs]  23.9 us
    all_to_all x3, waiting for transfers between devices, exchange(): return lax.all_to_all(x, axes, split_axis=0, concat_axis=0, tiled=True)  21.6 us
    all_gather x1, waiting for transfers between devices, gather(): return lax.all_gather(x, 'z_hi', axis=0, tiled=True)  15.1 us
    ppermute x3, starting transfers between devices, swap(): return [lax.ppermute(x, 'z_lo', ((0, 1), (1, 0))) for x in xs]  7.19 us
    pallas_call x1, Pallas kernels, last(): pl.pallas_call(last_kernel, out_shape=(shape, shape), in_specs=[SMEM, VME...  6.09 us
    pallas_call x1, Pallas kernels, first(): pl.pallas_call(first_kernel, grid=(Z // 2,), out_shape=jax.ShapeDtypeStru...  4.93 us
  transfers between devices with their start and end apart: 8, of which 8 were waited for; matrix products, arithmetic and copies ran while one was open for 1% of the time, Pallas kernels for 7%

profile of v4, /device:TPU:1, one launch (start us, length us, event | category | flops | bytes accessed | tf_op | source)
XLA Modules:
  0.0 218.6 jit_solution(5449650467095530128)
XLA Ops:
  7.2 0.0 all-gather.2.cloned.1.call-start
  7.2 1.7 pad_maximum_fusion.1
  8.9 0.0 all-gather.2.cloned.1.call-update
  8.9 2.4 %pack.1 = (bf16[32,32,384]{2,1,0:T(8,128)(2,1)}, bf16[16,32,384]{2,1,0:T(8,128)(2,1)}) custom-call(s32[1]{0:T(128)} %bitcast.1.me_ref, s32[4]{0:T(128)} %bitcast.16, s32[1,16]{1,0:T(1,128)} %bitcast.17, bf16[16,5120]{1,0:T(8,128)(2,1)} %bitcast.13, bf16[16,5120]{1,0:T(8,128)(2,1)} %bitcast.14), custom_call_target="tpu_custom_call" | custom-call | tf_op jit(solution)/shard_map/pack/pallas_call | solution.py:61
  11.3 0.0 copy-start.6
  11.3 10.5 %all-to-all-start = ((bf16[32,32,384]{2,1,0:T(8,128)(2,1)}), bf16[32,32,384]{2,1,0:T(8,128)(2,1)S(1)}, u32[]{:S(2)}, u32[]{:S(2)}) async-start(bf16[32,32,384]{2,1,0:T(8,128)(2,1)} %get-tuple-element.16), calls=%async_computation | async-start | bytes 1572864 | tf_op jit(solution)/shard_map/all_to_all | solution.py:265
  21.9 0.0 copy-start.5
  21.9 0.0 copy-done.6
  21.9 1.9 collective-permute-start
  23.8 10.3 %collective-permute-done = bf16[16,32,384]{2,1,0:T(8,128)(2,1)S(1)} collective-permute-done((bf16[16,32,384]{2,1,0:T(8,128)(2,1)S(1)}, bf16[16,32,384]{2,1,0:T(8,128)(2,1)S(1)}, u32[]{:S(2)}, u32[]{:S(2)}) %collective-permute-start) | collective-permute-done | bytes 393248 | tf_op jit(solution)/shard_map/ppermute | solution.py:277
  34.1 1.0 pad_maximum_fusion
  35.1 1.1 all-to-all-done.own_ref
  36.2 0.0 copy-start
  36.2 9.5 %all-to-all-start.1 = ((bf16[32,32,384]{2,1,0:T(8,128)(2,1)}), bf16[32,32,384]{2,1,0:T(8,128)(2,1)S(1)}, u32[]{:S(2)}, u32[]{:S(2)}) async-start(bf16[32,32,384]{2,1,0:T(8,128)(2,1)} %pad_maximum_fusion), calls=%async_computation.1 | async-start | bytes 1572864 | tf_op jit(solution)/shard_map/all_to_all | solution.py:265
  45.8 0.0 reduce-scatter.2.cloned.1.call-start
  45.8 0.0 copy-done.5
  45.8 0.1 reshape.20
  45.9 0.2 dynamic-slice_reduce_fusion
  46.1 0.5 and_select_fusion.expert_ref
  46.6 13.4 %all-to-all-done.1.other_ref = bf16[32,32,384]{2,1,0:T(8,128)(2,1)S(1)} async-done(((bf16[32,32,384]{2,1,0:T(8,128)(2,1)}), bf16[32,32,384]{2,1,0:T(8,128)(2,1)S(1)}, u32[]{:S(2)}, u32[]{:S(2)}) %all-to-all-start.1) | async-done | bytes 786464 | tf_op jit(solution)/shard_map/all_to_all | solution.py:265
  60.0 0.0 copy-done
  60.0 0.0 copy-start.1
  60.0 0.9 copy-done.1
  60.9 3.4 %prepare.1 = (bf16[2,4,256,320]{3,2,1,0:T(8,128)(2,1)}, bf16[2,4,320,256]{3,2,1,0:T(8,128)(2,1)}) custom-call(bf16[32,32,384]{2,1,0:T(8,128)(2,1)} %copy-done, bf16[32,32,384]{2,1,0:T(8,128)(2,1)} %copy-done.1), custom_call_target="tpu_custom_call" | custom-call | tf_op jit(solution)/shard_map/prepare/pallas_call | solution.py:95
  64.3 15.1 %all-gather.2.cloned.1.call-done.weight_ref = bf16[8,3,320,128]{3,2,1,0:T(8,128)(2,1)} async-done(((bf16[1,3,320,128]{3,2,1,0:T(8,128)(2,1)}), bf16[8,3,320,128]{3,2,1,0:T(8,128)(2,1)}) %all-gather.2.cloned.1.call-update) | async-done | bytes 1966096 | tf_op jit(solution)/shard_map/all_gather | solution.py:269
  79.4 4.9 %first.1 = bf16[8,256,384]{2,1,0:T(8,128)(2,1)} custom-call(s32[8]{0:T(128)} %and_select_fusion.expert_ref, bf16[2,4,256,320]{3,2,1,0:T(8,128)(2,1)} %get-tuple-element.18.x_ref, bf16[8,3,320,128]{3,2,1,0:T(8,128)(2,1)} %all-gather.2.cloned.1.call-done.weight_ref), custom_call_target="tpu_custom_call" | custom-call | tf_op jit(solution)/shard_map/first/pallas_call | solution.py:113
  84.4 28.3 %all_to_all.30.part_ref = bf16[16,128,384]{2,1,0:T(8,128)(2,1)} all-to-all(bf16[16,128,384]{2,1,0:T(8,128)(2,1)} %bitcast.12), channel_id=1, replica_groups=mesh['y_lo'=2,'x'=4,'core'=2,'z_hi'=8,'z_lo'=2,'y_hi'=2] {'y_lo','x','co..., dimensions={0} | all-to-all | bytes 3145728 | tf_op jit(solution)/shard_map/all_to_all | solution.py:265
  112.6 3.7 %middle.1 = bf16[16,128,384]{2,1,0:T(8,128)(2,1)} custom-call(bf16[16,128,384]{2,1,0:T(8,128)(2,1)} %all_to_all.30.part_ref), custom_call_target="tpu_custom_call" | custom-call | tf_op jit(solution)/shard_map/middle/pallas_call | solution.py:147
  116.4 26.5 %all_to_all.31 = bf16[16,128,384]{2,1,0:T(8,128)(2,1)} all-to-all(bf16[16,128,384]{2,1,0:T(8,128)(2,1)} %middle.1), channel_id=1, replica_groups=mesh['y_lo'=2,'x'=4,'core'=2,'z_hi'=8,'z_lo'=2,'y_hi'=2] {'y_lo','x','co..., dimensions={0} | all-to-all | bytes 3145728 | tf_op jit(solution)/shard_map/all_to_all | solution.py:265
  142.9 4.7 %weigh.1 = bf16[8,3,320,128]{3,2,1,0:T(8,128)(2,1)} custom-call(s32[8]{0:T(128)} %and_select_fusion.expert_ref, bf16[2,4,320,256]{3,2,1,0:T(8,128)(2,1)} %get-tuple-element.25.xt_ref, bf16[8,256,384]{2,1,0:T(8,128)(2,1)} %bitcast.10), custom_call_target="tpu_custom_call" | custom-call | tf_op jit(solution)/shard_map/weigh/pallas_call | solution.py:167
  147.6 0.0 reduce-scatter.2.cloned.1.call-update
  147.6 6.1 %last.1 = (bf16[32,32,384]{2,1,0:T(8,128)(2,1)}, bf16[32,32,384]{2,1,0:T(8,128)(2,1)}) custom-call(s32[8]{0:T(128)} %and_select_fusion.expert_ref, bf16[8,3,320,128]{3,2,1,0:T(8,128)(2,1)} %all-gather.2.cloned.1.call-done.weight_ref, bf16[8,256,384]{2,1,0:T(8,128)(2,1)} %bitcast.11), custom_call_target="tpu_custom_call" | custom-call | tf_op jit(solution)/shard_map/last/pallas_call | solution.py:210
  153.7 20.6 %all_to_all.32.refs_0_ = bf16[32,32,384]{2,1,0:T(8,128)(2,1)} all-to-all(bf16[32,32,384]{2,1,0:T(8,128)(2,1)} %get-tuple-element.20), channel_id=1, replica_groups=mesh['y_lo'=2,'x'=4,'core'=2,'z_hi'=8,'z_lo'=2,'y_hi'=2] {'y_hi','y_lo',..., dimensions={0} | all-to-all | bytes 1572864 | tf_op jit(solution)/shard_map/all_to_all | solution.py:265
  174.3 4.1 %all-to-all-start.4 = ((bf16[32,32,384]{2,1,0:T(8,128)(2,1)}), bf16[32,32,384]{2,1,0:T(8,128)(2,1)S(1)}, u32[]{:S(2)}, u32[]{:S(2)}) async-start(bf16[32,32,384]{2,1,0:T(8,128)(2,1)} %get-tuple-element.19), calls=%async_computation.4 | async-start | bytes 1572864 | tf_op jit(solution)/shard_map/all_to_all | solution.py:265
  178.4 2.0 unpack.2
  180.3 1.9 collective-permute-start.1
  182.2 3.4 %collective-permute-start.2 = (bf16[16,5120]{1,0:T(8,128)(2,1)}, bf16[16,5120]{1,0:T(8,128)(2,1)S(1)}, u32[]{:S(2)}, u32[]{:S(2)}) collective-permute-start(bf16[16,5120]{1,0:T(8,128)(2,1)} %get-tuple-element.22), channel_id=1, source_target_pairs={{0,2},{2,0},{1,3},{3,1},{4,6},{6,4},{5,7},{7,5},{8,10},{10,8},{9,1... | collective-permute-start | bytes 491528 | tf_op jit(solution)/shard_map/ppermute | solution.py:277
  185.6 7.1 %all-to-all-done.4.refs_0_ = bf16[32,32,384]{2,1,0:T(8,128)(2,1)S(1)} async-done(((bf16[32,32,384]{2,1,0:T(8,128)(2,1)}), bf16[32,32,384]{2,1,0:T(8,128)(2,1)S(1)}, u32[]{:S(2)}, u32[]{:S(2)}) %all-to-all-start.4) | async-done | bytes 786464 | tf_op jit(solution)/shard_map/all_to_all | solution.py:265
  192.7 0.0 copy-start.2
  192.7 3.2 %collective-permute-done.1.refs_1_ = bf16[16,5120]{1,0:T(8,128)(2,1)S(1)} collective-permute-done((bf16[16,5120]{1,0:T(8,128)(2,1)}, bf16[16,5120]{1,0:T(8,128)(2,1)S(1)}, u32[]{:S(2)}, u32[]{:S(2)}) %collective-permute-start.1) | collective-permute-done | bytes 163872 | tf_op jit(solution)/shard_map/ppermute | solution.py:277
  195.9 0.0 copy-start.3
  195.9 10.4 %collective-permute-done.2.refs_2_ = bf16[16,5120]{1,0:T(8,128)(2,1)S(1)} collective-permute-done((bf16[16,5120]{1,0:T(8,128)(2,1)}, bf16[16,5120]{1,0:T(8,128)(2,1)S(1)}, u32[]{:S(2)}, u32[]{:S(2)}) %collective-permute-start.2) | collective-permute-done | bytes 163872 | tf_op jit(solution)/shard_map/ppermute | solution.py:277
  206.3 0.0 copy-done.2
  206.3 0.0 copy-done.3
  206.3 0.0 copy-start.4
  206.3 0.7 copy-done.4
  207.0 2.1 unpack.3
  209.1 0.9 reduce-scatter.2.cloned.1.call-done.own_ref
  210.0 1.7 widen.1
Async XLA Ops:
  7.2 72.3 %all-gather.2.cloned.1.call-start = ((), (), s32[]{:S(2)}) async-start(), calls=%async_computation.7 | async-start | bytes 2211840 | tf_op jit(solution)/shard_map/all_gather | solution.py:269
  11.3 10.6 %copy-start.6 = (bf16[16,32,384]{2,1,0:T(8,128)(2,1)S(1)}, bf16[16,32,384]{2,1,0:T(8,128)(2,1)}, u32[]{:S(2)}) copy-start(bf16[16,32,384]{2,1,0:T(8,128)(2,1)} %get-tuple-element.17) | copy-start | bytes 1179652
  11.3 24.9 %all-to-all-start = ((bf16[32,32,384]{2,1,0:T(8,128)(2,1)}), bf16[32,32,384]{2,1,0:T(8,128)(2,1)S(1)}, u32[]{:S(2)}, u32[]{:S(2)}) async-start(bf16[32,32,384]{2,1,0:T(8,128)(2,1)} %get-tuple-element.16), calls=%async_computation | async-start | bytes 1572864 | tf_op jit(solution)/shard_map/all_to_all | solution.py:265
  21.9 24.0 %copy-start.5 = (s32[32]{0:T(128)S(1)}, s32[32]{0:T(128)}, u32[]{:S(2)}) copy-start(s32[32]{0:T(128)} %param.11) | copy-start | bytes 388
  21.9 12.2 %collective-permute-start = (bf16[16,32,384]{2,1,0:T(8,128)(2,1)S(1)}, bf16[16,32,384]{2,1,0:T(8,128)(2,1)S(1)}, u32[]{:S(2)}, u32[]{:S(2)}) collective-permute-start(bf16[16,32,384]{2,1,0:T(8,128)(2,1)S(1)} %copy-done.6), channel_id=1, source_target_pairs={{0,2},{2,0},{1,3},{3,1},{4,6},{6,4},{5,7},{7,5},{8,10},{10,8},{9,1... | collective-permute-start | bytes 1179656 | tf_op jit(solution)/shard_map/ppermute | solution.py:277
  36.2 23.8 %copy-start = (bf16[32,32,384]{2,1,0:T(8,128)(2,1)}, bf16[32,32,384]{2,1,0:T(8,128)(2,1)S(1)}, u32[]{:S(2)}) copy-start(bf16[32,32,384]{2,1,0:T(8,128)(2,1)S(1)} %all-to-all-done.own_ref) | copy-start | bytes 2359300
  36.2 23.8 %all-to-all-start.1 = ((bf16[32,32,384]{2,1,0:T(8,128)(2,1)}), bf16[32,32,384]{2,1,0:T(8,128)(2,1)S(1)}, u32[]{:S(2)}, u32[]{:S(2)}) async-start(bf16[32,32,384]{2,1,0:T(8,128)(2,1)} %pad_maximum_fusion), calls=%async_computation.1 | async-start | bytes 1572864 | tf_op jit(solution)/shard_map/all_to_all | solution.py:265
  45.8 164.3 %reduce-scatter.2.cloned.1.call-start = ((), (), s32[]{:S(2)}) async-start(), calls=%async_computation.8 | async-start | bytes 2211840 | tf_op jit(solution)/shard_map/reduce_scatter | solution.py:273
  60.0 0.9 copy-start.1
  174.3 18.4 %all-to-all-start.4 = ((bf16[32,32,384]{2,1,0:T(8,128)(2,1)}), bf16[32,32,384]{2,1,0:T(8,128)(2,1)S(1)}, u32[]{:S(2)}, u32[]{:S(2)}) async-start(bf16[32,32,384]{2,1,0:T(8,128)(2,1)} %get-tuple-element.19), calls=%async_computation.4 | async-start | bytes 1572864 | tf_op jit(solution)/shard_map/all_to_all | solution.py:265
  180.3 15.6 %collective-permute-start.1 = (bf16[16,5120]{1,0:T(8,128)(2,1)}, bf16[16,5120]{1,0:T(8,128)(2,1)S(1)}, u32[]{:S(2)}, u32[]{:S(2)}) collective-permute-start(bf16[16,5120]{1,0:T(8,128)(2,1)} %get-tuple-element.21), channel_id=1, source_target_pairs={{0,2},{2,0},{1,3},{3,1},{4,6},{6,4},{5,7},{7,5},{8,10},{10,8},{9,1... | collective-permute-start | bytes 491528 | tf_op jit(solution)/shard_map/ppermute | solution.py:277
  182.2 24.1 %collective-permute-start.2 = (bf16[16,5120]{1,0:T(8,128)(2,1)}, bf16[16,5120]{1,0:T(8,128)(2,1)S(1)}, u32[]{:S(2)}, u32[]{:S(2)}) collective-permute-start(bf16[16,5120]{1,0:T(8,128)(2,1)} %get-tuple-element.22), channel_id=1, source_target_pairs={{0,2},{2,0},{1,3},{3,1},{4,6},{6,4},{5,7},{7,5},{8,10},{10,8},{9,1... | collective-permute-start | bytes 491528 | tf_op jit(solution)/shard_map/ppermute | solution.py:277
  192.7 13.6 %copy-start.2 = (bf16[32,32,384]{2,1,0:T(8,128)(2,1)}, bf16[32,32,384]{2,1,0:T(8,128)(2,1)S(1)}, u32[]{:S(2)}) copy-start(bf16[32,32,384]{2,1,0:T(8,128)(2,1)S(1)} %all-to-all-done.4.refs_0_) | copy-start | bytes 2359300
  195.9 10.4 %copy-start.3 = (bf16[16,5120]{1,0:T(8,128)(2,1)}, bf16[16,5120]{1,0:T(8,128)(2,1)S(1)}, u32[]{:S(2)}) copy-start(bf16[16,5120]{1,0:T(8,128)(2,1)S(1)} %collective-permute-done.1.refs_1_) | copy-start | bytes 491524
  206.3 0.7 copy-start.4
Sparse Core Ops, SparseCore 0:
  10.6 68.7 all-gather.1
  147.7 62.2 reduce-scatter.1

commit v5 on v4

--- a/solution.py
+++ b/solution.py
@@ -25,9 +25,11 @@
 S = 128
 Q = C * G
 R = N * Q
-H = Z * R // G
+CHIPS = ("y_lo", "x")
+H = R // 2
 BF = jnp.bfloat16
 F32 = jnp.float32
+LIMIT = 24 << 20
 VMEM = pl.BlockSpec(memory_space=pltpu.VMEM)
 SMEM = pl.BlockSpec(memory_space=pltpu.SMEM)
 
@@ -101,32 +103,43 @@
     )(own, other)
 
 
-def first_kernel(expert_ref, x_ref, weight_ref, out_ref):
-    for i in range(2):
-        e = expert_ref[2 * pl.program_id(0) + i]
+def first_kernel(expert_ref, half_ref, x_ref, weight_ref, *refs):
+    out_ref = refs[-1]
+    for i in range(Z // 2):
+        e = expert_ref[Z // 2 * pl.program_id(0) + i]
         both = jnp.concatenate([weight_ref[i, 0], weight_ref[i, 1]], axis=1)
-        out_ref[i, :, 0 : 2 * S] = dot(x_ref[0, e], both).astype(BF)
-        out_ref[i, :, 2 * S : 3 * S] = dot(x_ref[1, e], weight_ref[i, 2]).astype(BF)
-
-
-def first(expert, x, weight):
+        gate_up = dot(x_ref[0, e], both)
+        hidden_grad = dot(x_ref[1, e], weight_ref[i, 2])
+        if len(refs) > 1:
+            gate_up = gate_up + refs[0][i, :, 0 : 2 * S].astype(F32)
+            hidden_grad = hidden_grad + refs[0][i, :, 2 * S : 3 * S].astype(F32)
+        out_ref[i, :, 0 : 2 * S] = gate_up.astype(BF)
+        out_ref[i, :, 2 * S : 3 * S] = hidden_grad.astype(BF)
+
+
+def first(expert, half, x, weight, *add):
+    rows = pl.BlockSpec((Z // 2, H, 3 * S), lambda i, expert, half: (i, 0, 0))
     return pl.pallas_call(
         first_kernel,
-        grid=(Z // 2,),
-        out_shape=jax.ShapeDtypeStruct((Z, R, 3 * S), BF),
-        in_specs=[
-            SMEM,
-            pl.BlockSpec((2, E, R, W), lambda i: (0, 0, 0, 0)),
-            pl.BlockSpec((2, 3, W, S), lambda i: (i, 0, 0, 0)),
-        ],
-        out_specs=pl.BlockSpec((2, R, 3 * S), lambda i: (i, 0, 0)),
+        out_shape=jax.ShapeDtypeStruct((Z, H, 3 * S), BF),
+        grid_spec=pltpu.PrefetchScalarGridSpec(
+            num_scalar_prefetch=2,
+            grid=(2,),
+            in_specs=[
+                pl.BlockSpec((2, E, H, W), lambda i, expert, half: (0, 0, half[0], 0)),
+                pl.BlockSpec((Z // 2, 3, W, S), lambda i, expert, half: (i, 0, 0, 0)),
+            ]
+            + [rows] * len(add),
+            out_specs=rows,
+        ),
+        compiler_params=pltpu.CompilerParams(vmem_limit_bytes=LIMIT),
         name="first",
-    )(expert, x, weight)
+    )(expert, half, x, weight, *add)
 
 
 def middle_kernel(part_ref, out_ref):
     total = part_ref[0].astype(F32)
-    for d in range(1, G):
+    for d in range(1, Z):
         total = total + part_ref[d].astype(F32)
     gate = total[:, 0:S]
     up = total[:, S : 2 * S]
@@ -136,57 +149,63 @@
     hidden = (activated * up).astype(BF)
     gate_grad = (hidden_grad * up * sigmoid * (1.0 + gate * (1.0 - sigmoid))).astype(BF)
     up_grad = (hidden_grad * activated).astype(BF)
-    for d in range(G):
+    for d in range(Z):
         out_ref[d, :, 0:S] = hidden
         out_ref[d, :, S : 2 * S] = gate_grad
         out_ref[d, :, 2 * S : 3 * S] = up_grad
 
 
 def middle(parts):
-    block = pl.BlockSpec((G, H // 4, 3 * S), lambda i: (0, i, 0))
+    block = pl.BlockSpec((Z, H // 2, 3 * S), lambda i: (0, i, 0))
     return pl.pallas_call(
         middle_kernel,
-        grid=(4,),
-        out_shape=jax.ShapeDtypeStruct((G, H, 3 * S), BF),
+        grid=(2,),
+        out_shape=jax.ShapeDtypeStruct((Z, H, 3 * S), BF),
         in_specs=[block],
         out_specs=block,
+        compiler_params=pltpu.CompilerParams(vmem_limit_bytes=LIMIT),
         name="middle",
     )(parts)
 
 
-def weigh_kernel(expert_ref, xt_ref, act_ref, out_ref):
-    for i in range(2):
-        e = expert_ref[2 * pl.program_id(0) + i]
-        both = dot(xt_ref[0, e], act_ref[i, :, S : 3 * S])
+def in_order(core, mine, other):
+    low = jnp.broadcast_to(core, mine.shape) == 0
+    return jnp.concatenate([jnp.where(low, mine, other), jnp.where(low, other, mine)], axis=0)
+
+
+def weigh_kernel(expert_ref, core_ref, xt_ref, mine_ref, other_ref, out_ref):
+    for i in range(Z // 2):
+        e = expert_ref[Z // 2 * pl.program_id(0) + i]
+        act = in_order(core_ref[0], mine_ref[i], other_ref[i])
+        both = dot(xt_ref[0, e], act[:, S : 3 * S])
         out_ref[i, 0] = both[:, 0:S].astype(BF)
         out_ref[i, 1] = both[:, S : 2 * S].astype(BF)
-        out_ref[i, 2] = dot(xt_ref[1, e], act_ref[i, :, 0:S]).astype(BF)
-
-
-def weigh(expert, xt, act):
+        out_ref[i, 2] = dot(xt_ref[1, e], act[:, 0:S]).astype(BF)
+
+
+def weigh(expert, core, xt, mine, other):
+    rows = pl.BlockSpec((Z // 2, H, 3 * S), lambda i: (i, 0, 0))
     return pl.pallas_call(
         weigh_kernel,
-        grid=(Z // 2,),
+        grid=(2,),
         out_shape=jax.ShapeDtypeStruct((Z, 3, W, S), BF),
-        in_specs=[
-            SMEM,
-            pl.BlockSpec((2, E, W, R), lambda i: (0, 0, 0, 0)),
-            pl.BlockSpec((2, R, 3 * S), lambda i: (i, 0, 0)),
-        ],
-        out_specs=pl.BlockSpec((2, 3, W, S), lambda i: (i, 0, 0, 0)),
+        in_specs=[SMEM, SMEM, pl.BlockSpec((2, E, W, R), lambda i: (0, 0, 0, 0)), rows, rows],
+        out_specs=pl.BlockSpec((Z // 2, 3, W, S), lambda i: (i, 0, 0, 0)),
+        compiler_params=pltpu.CompilerParams(vmem_limit_bytes=LIMIT),
         name="weigh",
-    )(expert, xt, act)
-
-
-def last_kernel(expert_ref, weight_ref, act_ref, own_ref, other_ref, acc_ref):
+    )(expert, core, xt, mine, other)
+
+
+def last_kernel(expert_ref, core_ref, weight_ref, mine_ref, far_ref, own_ref, other_ref, acc_ref):
     acc_ref[...] = jnp.zeros_like(acc_ref)
     tail = ((1,), (1,))
 
     def step(z, carry):
         e = expert_ref[z]
-        acc_ref[0, e] += dot(act_ref[z, :, 0:S], weight_ref[z, 2], tail)
+        act = in_order(core_ref[0], mine_ref[z], far_ref[z])
+        acc_ref[0, e] += dot(act[:, 0:S], weight_ref[z, 2], tail)
         both = jnp.concatenate([weight_ref[z, 0], weight_ref[z, 1]], axis=1)
-        acc_ref[1, e] += dot(act_ref[z, :, S : 3 * S], both, tail)
+        acc_ref[1, e] += dot(act[:, S : 3 * S], both, tail)
         return carry
 
     lax.fori_loop(0, Z, step, 0)
@@ -205,16 +224,16 @@
                 out_ref[first_block + h, t * G : (t + 1) * G, W:WP] = jnp.zeros((E * C, WP - W), BF)
 
 
-def last(expert, weight, act):
+def last(expert, core, weight, mine, far):
     shape = jax.ShapeDtypeStruct((Y * G, 2 * G, WP), BF)
     return pl.pallas_call(
         last_kernel,
         out_shape=(shape, shape),
-        in_specs=[SMEM, VMEM, VMEM],
+        in_specs=[SMEM, SMEM, VMEM, VMEM, VMEM],
         out_specs=(VMEM, VMEM),
         scratch_shapes=[pltpu.VMEM((2, E, R, W), F32)],
         name="last",
-    )(expert, weight, act)
+    )(expert, core, weight, mine, far)
 
 
 def unpack_kernel(*refs):
@@ -273,8 +292,12 @@
     return lax.psum_scatter(x, "z_hi", scatter_dimension=0, tiled=True)
 
 
-def swap(*xs):
-    return [lax.ppermute(x, "z_lo", ((0, 1), (1, 0))) for x in xs]
+def swap(*xs, axis="z_lo"):
+    return [lax.ppermute(x, axis, ((0, 1), (1, 0))) for x in xs]
+
+
+def swap_cores(x):
+    return swap(x, axis="core")[0]
 
 
 def body(tokens, cotangent, counts, destination, placement, gate_up_weight, down_weight):
@@ -288,11 +311,14 @@
     own = exchange(sent, PLANE)
     other = exchange(jnp.concatenate([other] * Y, axis=0), PLANE)
     x, xt = prepare(own, other)
-    parts = first(expert, x, weight).reshape(G, H, 3 * S)
-    act = middle(exchange(parts, GRP))
-    act = exchange(act, GRP).reshape(Z, R, 3 * S)
-    reduced = scatter(weigh(expert, xt, act))
-    own, other = last(expert, weight, act)
+    core = lax.axis_index("core").reshape(1).astype(jnp.int32)
+    got = swap_cores(first(expert, 1 - core, x, weight))
+    parts = first(expert, core, x, weight, got)
+    act = middle(exchange(parts, CHIPS))
+    mine = exchange(act, CHIPS)
+    far = swap_cores(mine)
+    reduced = scatter(weigh(expert, core, xt, mine, far))
+    own, other = last(expert, core, weight, mine, far)
     other = unpack(exchange(other, PLANE))
     other = swap(*other)
     layer_out, input_grad = unpack(exchange(own, PLANE), *other)

time: 220 us -> 204 us (0.927)
  the two profiles are of different devices: /device:TPU:1 before, /device:TPU:2 now
where the time goes in v5:
time: 204 us
  waiting for transfers between devices  71.8 us (35%)
  blocking collectives  52.5 us (26%)
  starting transfers between devices  34 us (17%)
  Pallas kernels  23.5 us (12%)
  between operations  14.2 us (7%)
  local copies, waits for them, and re-layouts  4.82 us (2%)
  other arithmetic  2.66 us (1%)
    all_to_all x3, blocking collectives, exchange(): return lax.all_to_all(x, axes, split_axis=0, concat_axis=0, tiled=True)  52.5 us
    ppermute x5, waiting for transfers between devices, swap(): return [lax.ppermute(x, axis, ((0, 1), (1, 0))) for x in xs]  34 us
    all_to_all x3, starting transfers between devices, exchange(): return lax.all_to_all(x, axes, split_axis=0, concat_axis=0, tiled=True)  22.3 us
    all_to_all x3, waiting for transfers between devices, exchange(): return lax.all_to_all(x, axes, split_axis=0, concat_axis=0, tiled=True)  18.3 us
    all_gather x1, waiting for transfers between devices, gather(): return lax.all_gather(x, 'z_hi', axis=0, tiled=True)  17.2 us
    ppermute x5, starting transfers between devices, swap(): return [lax.ppermute(x, axis, ((0, 1), (1, 0))) for x in xs]  11.7 us
    pallas_call x1, Pallas kernels, last(): pl.pallas_call(last_kernel, out_shape=(shape, shape), in_specs=[SMEM, SME...  6.03 us
    unnamed x26, local copies, waits for them, and re-layouts  4.55 us
  transfers between devices with their start and end apart: 10, of which 9 were waited for; matrix products, arithmetic and copies ran while one was open for 1% of the time, Pallas kernels for 8%

profile of v5, /device:TPU:2, one launch (start us, length us, event | category | flops | bytes accessed | tf_op | source)
XLA Modules:
  0.0 203.5 jit_solution(14639786140495861032)
XLA Ops:
  7.2 0.0 all-gather.2.cloned.1.call-start
  7.2 1.7 pad_maximum_fusion.1
  8.9 0.0 all-gather.2.cloned.1.call-update
  8.9 2.4 %pack.1 = (bf16[32,32,384]{2,1,0:T(8,128)(2,1)}, bf16[16,32,384]{2,1,0:T(8,128)(2,1)}) custom-call(s32[1]{0:T(128)} %bitcast.2.me_ref, s32[4]{0:T(128)} %bitcast.12, s32[1,16]{1,0:T(1,128)} %bitcast.13, bf16[16,5120]{1,0:T(8,128)(2,1)} %bitcast.9, bf16[16,5120]{1,0:T(8,128)(2,1)} %bitcast.10), custom_call_target="tpu_custom_call" | custom-call | tf_op jit(solution)/shard_map/pack/pallas_call | solution.py:63
  11.3 0.0 copy-start.12
  11.3 9.6 %all-to-all-start = ((bf16[32,32,384]{2,1,0:T(8,128)(2,1)}), bf16[32,32,384]{2,1,0:T(8,128)(2,1)S(1)}, u32[]{:S(2)}, u32[]{:S(2)}) async-start(bf16[32,32,384]{2,1,0:T(8,128)(2,1)} %get-tuple-element.16), calls=%async_computation | async-start | bytes 1572864 | tf_op jit(solution)/shard_map/all_to_all | solution.py:284
  20.9 2.0 collective-permute-start
  22.9 13.8 %collective-permute-done = bf16[16,32,384]{2,1,0:T(8,128)(2,1)S(1)} collective-permute-done((bf16[16,32,384]{2,1,0:T(8,128)(2,1)}, bf16[16,32,384]{2,1,0:T(8,128)(2,1)S(1)}, u32[]{:S(2)}, u32[]{:S(2)}) %collective-permute-start) | collective-permute-done | bytes 393248 | tf_op jit(solution)/shard_map/ppermute | solution.py:296
  36.7 1.0 pad_maximum_fusion
  37.7 0.0 all-to-all-done.own_ref
  37.7 0.0 copy-start.7
  37.7 7.6 %all-to-all-start.1 = ((bf16[32,32,384]{2,1,0:T(8,128)(2,1)}), bf16[32,32,384]{2,1,0:T(8,128)(2,1)S(1)}, u32[]{:S(2)}, u32[]{:S(2)}) async-start(bf16[32,32,384]{2,1,0:T(8,128)(2,1)} %pad_maximum_fusion), calls=%async_computation.1 | async-start | bytes 1572864 | tf_op jit(solution)/shard_map/all_to_all | solution.py:284
  45.3 0.0 reduce-scatter.2.cloned.1.call-start
  45.4 0.0 copy-done.12
  45.4 0.1 reshape.17
  45.5 0.2 dynamic-slice_reduce_fusion
  45.7 0.0 copy-start.6
  45.7 12.8 %all-to-all-done.1.other_ref = bf16[32,32,384]{2,1,0:T(8,128)(2,1)S(1)} async-done(((bf16[32,32,384]{2,1,0:T(8,128)(2,1)}), bf16[32,32,384]{2,1,0:T(8,128)(2,1)S(1)}, u32[]{:S(2)}, u32[]{:S(2)}) %all-to-all-start.1) | async-done | bytes 786464 | tf_op jit(solution)/shard_map/all_to_all | solution.py:284
  58.5 0.0 copy-done.7
  58.5 0.0 copy-start.8
  58.5 0.9 copy-done.8
  59.4 3.4 %prepare.1 = (bf16[2,4,256,320]{3,2,1,0:T(8,128)(2,1)}, bf16[2,4,320,256]{3,2,1,0:T(8,128)(2,1)}) custom-call(bf16[32,32,384]{2,1,0:T(8,128)(2,1)} %copy-done.7, bf16[32,32,384]{2,1,0:T(8,128)(2,1)} %copy-done.8), custom_call_target="tpu_custom_call" | custom-call | tf_op jit(solution)/shard_map/prepare/pallas_call | solution.py:97
  62.8 17.2 %all-gather.2.cloned.1.call-done.weight_ref = bf16[8,3,320,128]{3,2,1,0:T(8,128)(2,1)} async-done(((bf16[1,3,320,128]{3,2,1,0:T(8,128)(2,1)}), bf16[8,3,320,128]{3,2,1,0:T(8,128)(2,1)}) %all-gather.2.cloned.1.call-update) | async-done | bytes 1966096 | tf_op jit(solution)/shard_map/all_gather | solution.py:288
  80.0 0.0 copy-start
  80.0 1.5 copy-done
  81.6 0.0 copy-start.3
  81.6 1.4 copy-done.3
  83.0 0.0 copy-start.1
  83.0 1.5 first.2
  84.5 1.9 collective-permute-start.1
  86.4 2.3 %collective-permute-done.1.refs_0_ = bf16[8,128,384]{2,1,0:T(8,128)(2,1)S(1)} collective-permute-done((bf16[8,128,384]{2,1,0:T(8,128)(2,1)S(1)}, bf16[8,128,384]{2,1,0:T(8,128)(2,1)S(1)}, u32[]{:S(2)}, u32[]{:S(2)}) %collective-permute-start.1) | collective-permute-done | bytes 786464 | tf_op jit(solution)/shard_map/ppermute | solution.py:296
  88.7 0.0 copy-done.1
  88.7 1.5 first.3
  90.2 18.3 %all_to_all.30.part_ref = bf16[8,128,384]{2,1,0:T(8,128)(2,1)S(1)} all-to-all(bf16[8,128,384]{2,1,0:T(8,128)(2,1)S(1)} %first.3), channel_id=1, replica_groups=mesh['y_lo'=2,'x'=4,'core'=2,'z_hi'=8,'z_lo'=2,'y_hi'=2] {'y_lo','x'}, dimensions={0} | all-to-all | bytes 1572864 | tf_op jit(solution)/shard_map/all_to_all | solution.py:284
  108.5 0.0 copy-start.5
  108.5 0.4 middle.1
  108.9 15.1 %all_to_all.31.mine_ref = bf16[8,128,384]{2,1,0:T(8,128)(2,1)S(1)} all-to-all(bf16[8,128,384]{2,1,0:T(8,128)(2,1)S(1)} %middle.1), channel_id=1, replica_groups=mesh['y_lo'=2,'x'=4,'core'=2,'z_hi'=8,'z_lo'=2,'y_hi'=2] {'y_lo','x'}, dimensions={0} | all-to-all | bytes 1572864 | tf_op jit(solution)/shard_map/all_to_all | solution.py:284
  124.0 0.0 copy-start.2
  124.0 1.9 collective-permute-start.2
  125.9 2.3 %collective-permute-done.2.far_ref.other_ref = bf16[8,128,384]{2,1,0:T(8,128)(2,1)S(1)} collective-permute-done((bf16[8,128,384]{2,1,0:T(8,128)(2,1)S(1)}, bf16[8,128,384]{2,1,0:T(8,128)(2,1)S(1)}, u32[]{:S(2)}, u32[]{:S(2)}) %collective-permute-start.2) | collective-permute-done | bytes 786464 | tf_op jit(solution)/shard_map/ppermute | solution.py:296
  128.1 0.0 copy-start.4
  128.1 0.0 copy-done.6
  128.1 0.0 copy-done.5
  128.1 2.6 %weigh.1 = bf16[8,3,320,128]{3,2,1,0:T(8,128)(2,1)} custom-call(s32[8]{0:T(128)S(1)} %and_select_fusion.expert_ref, s32[1]{0:T(128)} %bitcast.half_ref.core_ref, bf16[2,4,320,256]{3,2,1,0:T(8,128)(2,1)S(1)} %copy-done.5, bf16[8,128,384]{2,1,0:T(8,128)(2,1)S(1)} %all_to_all.31.mine_ref, bf16[8,128,384]{2,1,0:T(8,128)(2,1)S(1)} %collective-permute-done.2.far_ref.other_ref), custom_call_target="tpu_custom_call" | custom-call | tf_op jit(solution)/shard_map/weigh/pallas_call | solution.py:188
  130.7 0.0 copy-done.2
  130.7 0.0 copy-done.4
  130.7 0.0 reduce-scatter.2.cloned.1.call-update
  130.7 6.0 %last.1 = (bf16[32,32,384]{2,1,0:T(8,128)(2,1)}, bf16[32,32,384]{2,1,0:T(8,128)(2,1)}) custom-call(s32[8]{0:T(128)} %copy-done.6, s32[1]{0:T(128)} %bitcast.half_ref.core_ref, bf16[8,3,320,128]{3,2,1,0:T(8,128)(2,1)} %all-gather.2.cloned.1.call-done.weight_ref, bf16[8,128,384]{2,1,0:T(8,128)(2,1)} %copy-done.2, bf16[8,128,384]{2,1,0:T(8,128)(2,1)} %copy-done.4), custom_call_target="tpu_custom_call" | custom-call | tf_op jit(solution)/shard_map/last/pallas_call | solution.py:229
  136.8 19.1 %all_to_all.32.refs_0_ = bf16[32,32,384]{2,1,0:T(8,128)(2,1)} all-to-all(bf16[32,32,384]{2,1,0:T(8,128)(2,1)} %get-tuple-element.20), channel_id=1, replica_groups=mesh['y_lo'=2,'x'=4,'core'=2,'z_hi'=8,'z_lo'=2,'y_hi'=2] {'y_hi','y_lo',..., dimensions={0} | all-to-all | bytes 1572864 | tf_op jit(solution)/shard_map/all_to_all | solution.py:284
  155.9 5.1 %all-to-all-start.4 = ((bf16[32,32,384]{2,1,0:T(8,128)(2,1)}), bf16[32,32,384]{2,1,0:T(8,128)(2,1)S(1)}, u32[]{:S(2)}, u32[]{:S(2)}) async-start(bf16[32,32,384]{2,1,0:T(8,128)(2,1)} %get-tuple-element.19), calls=%async_computation.4 | async-start | bytes 1572864 | tf_op jit(solution)/shard_map/all_to_all | solution.py:284
  161.0 2.0 unpack.2
  163.0 1.9 collective-permute-start.3
  164.9 3.9 %collective-permute-start.4 = (bf16[16,5120]{1,0:T(8,128)(2,1)}, bf16[16,5120]{1,0:T(8,128)(2,1)S(1)}, u32[]{:S(2)}, u32[]{:S(2)}) collective-permute-start(bf16[16,5120]{1,0:T(8,128)(2,1)} %get-tuple-element.22), channel_id=1, source_target_pairs={{0,2},{2,0},{1,3},{3,1},{4,6},{6,4},{5,7},{7,5},{8,10},{10,8},{9,1... | collective-permute-start | bytes 491528 | tf_op jit(solution)/shard_map/ppermute | solution.py:296
  168.8 5.5 %all-to-all-done.4.refs_0_ = bf16[32,32,384]{2,1,0:T(8,128)(2,1)S(1)} async-done(((bf16[32,32,384]{2,1,0:T(8,128)(2,1)}), bf16[32,32,384]{2,1,0:T(8,128)(2,1)S(1)}, u32[]{:S(2)}, u32[]{:S(2)}) %all-to-all-start.4) | async-done | bytes 786464 | tf_op jit(solution)/shard_map/all_to_all | solution.py:284
  174.3 0.0 copy-start.9
  174.3 5.9 %collective-permute-done.3.refs_1_ = bf16[16,5120]{1,0:T(8,128)(2,1)S(1)} collective-permute-done((bf16[16,5120]{1,0:T(8,128)(2,1)}, bf16[16,5120]{1,0:T(8,128)(2,1)S(1)}, u32[]{:S(2)}, u32[]{:S(2)}) %collective-permute-start.3) | collective-permute-done | bytes 163872 | tf_op jit(solution)/shard_map/ppermute | solution.py:296
  180.2 9.8 %collective-permute-done.4.refs_2_ = bf16[16,5120]{1,0:T(8,128)(2,1)S(1)} collective-permute-done((bf16[16,5120]{1,0:T(8,128)(2,1)}, bf16[16,5120]{1,0:T(8,128)(2,1)S(1)}, u32[]{:S(2)}, u32[]{:S(2)}) %collective-permute-start.4) | collective-permute-done | bytes 163872 | tf_op jit(solution)/shard_map/ppermute | solution.py:296
  190.0 0.0 copy-done.9
  190.0 0.0 copy-done.10
  190.0 0.0 copy-start.11
  190.0 0.7 copy-done.11
  190.7 2.1 %unpack.3 = (bf16[16,5120]{1,0:T(8,128)(2,1)}, bf16[16,5120]{1,0:T(8,128)(2,1)}) custom-call(bf16[32,32,384]{2,1,0:T(8,128)(2,1)} %copy-done.9, bf16[16,5120]{1,0:T(8,128)(2,1)} %copy-done.10, bf16[16,5120]{1,0:T(8,128)(2,1)} %copy-done.11), custom_call_target="tpu_custom_call" | custom-call | tf_op jit(solution)/shard_map/unpack/pallas_call | solution.py:259
  192.8 2.2 %reduce-scatter.2.cloned.1.call-done.own_ref = bf16[1,3,320,128]{3,2,1,0:T(8,128)(2,1)} async-done(((bf16[8,3,320,128]{3,2,1,0:T(8,128)(2,1)}), bf16[1,3,320,128]{3,2,1,0:T(8,128)(2,1)}) %reduce-scatter.2.cloned.1.call-update) | async-done | bytes 245776 | tf_op jit(solution)/shard_map/reduce_scatter | solution.py:292
  194.9 1.7 widen.1
  (2 shorter events, 0.0 us)
Async XLA Ops:
  7.2 72.9 %all-gather.2.cloned.1.call-start = ((), (), s32[]{:S(2)}) async-start(), calls=%async_computation.7 | async-start | bytes 2211840 | tf_op jit(solution)/shard_map/all_gather | solution.py:288
  11.3 34.1 %copy-start.12 = (s32[32]{0:T(128)S(1)}, s32[32]{0:T(128)}, u32[]{:S(2)}) copy-start(s32[32]{0:T(128)} %param.11) | copy-start | bytes 388
  11.3 26.4 %all-to-all-start = ((bf16[32,32,384]{2,1,0:T(8,128)(2,1)}), bf16[32,32,384]{2,1,0:T(8,128)(2,1)S(1)}, u32[]{:S(2)}, u32[]{:S(2)}) async-start(bf16[32,32,384]{2,1,0:T(8,128)(2,1)} %get-tuple-element.16), calls=%async_computation | async-start | bytes 1572864 | tf_op jit(solution)/shard_map/all_to_all | solution.py:284
  20.9 15.8 %collective-permute-start = (bf16[16,32,384]{2,1,0:T(8,128)(2,1)}, bf16[16,32,384]{2,1,0:T(8,128)(2,1)S(1)}, u32[]{:S(2)}, u32[]{:S(2)}) collective-permute-start(bf16[16,32,384]{2,1,0:T(8,128)(2,1)} %get-tuple-element.17), channel_id=1, source_target_pairs={{0,2},{2,0},{1,3},{3,1},{4,6},{6,4},{5,7},{7,5},{8,10},{10,8},{9,1... | collective-permute-start | bytes 1179656 | tf_op jit(solution)/shard_map/ppermute | solution.py:296
  37.7 20.8 %copy-start.7 = (bf16[32,32,384]{2,1,0:T(8,128)(2,1)}, bf16[32,32,384]{2,1,0:T(8,128)(2,1)S(1)}, u32[]{:S(2)}) copy-start(bf16[32,32,384]{2,1,0:T(8,128)(2,1)S(1)} %all-to-all-done.own_ref) | copy-start | bytes 2359300
  37.7 20.8 %all-to-all-start.1 = ((bf16[32,32,384]{2,1,0:T(8,128)(2,1)}), bf16[32,32,384]{2,1,0:T(8,128)(2,1)S(1)}, u32[]{:S(2)}, u32[]{:S(2)}) async-start(bf16[32,32,384]{2,1,0:T(8,128)(2,1)} %pad_maximum_fusion), calls=%async_computation.1 | async-start | bytes 1572864 | tf_op jit(solution)/shard_map/all_to_all | solution.py:284
  45.3 149.6 %reduce-scatter.2.cloned.1.call-start = ((), (), s32[]{:S(2)}) async-start(), calls=%async_computation.8 | async-start | bytes 2211840 | tf_op jit(solution)/shard_map/reduce_scatter | solution.py:292
  45.7 82.5 %copy-start.6 = (s32[8]{0:T(128)}, s32[8]{0:T(128)S(1)}, u32[]{:S(2)}) copy-start(s32[8]{0:T(128)S(1)} %and_select_fusion.expert_ref) | copy-start | bytes 100
  58.5 0.9 copy-start.8
  80.0 1.5 copy-start
  81.6 1.4 copy-start.3
  83.0 5.7 %copy-start.1 = (bf16[8,3,320,128]{3,2,1,0:T(8,128)(2,1)S(1)}, bf16[8,3,320,128]{3,2,1,0:T(8,128)(2,1)}, u32[]{:S(2)}) copy-start(bf16[8,3,320,128]{3,2,1,0:T(8,128)(2,1)} %all-gather.2.cloned.1.call-done.weight_ref) | copy-start | bytes 5898244
  84.5 4.2 %collective-permute-start.1 = (bf16[8,128,384]{2,1,0:T(8,128)(2,1)S(1)}, bf16[8,128,384]{2,1,0:T(8,128)(2,1)S(1)}, u32[]{:S(2)}, u32[]{:S(2)}) collective-permute-start(bf16[8,128,384]{2,1,0:T(8,128)(2,1)S(1)} %first.2), channel_id=1, source_target_pairs={{0,32},{32,0},{1,33},{33,1},{2,34},{34,2},{3,35},{35,3},{4,36},{36... | collective-permute-start | bytes 2359304 | tf_op jit(solution)/shard_map/ppermute | solution.py:296
  108.5 19.6 %copy-start.5 = (bf16[2,4,320,256]{3,2,1,0:T(8,128)(2,1)S(1)}, bf16[2,4,320,256]{3,2,1,0:T(8,128)(2,1)}, u32[]{:S(2)}) copy-start(bf16[2,4,320,256]{3,2,1,0:T(8,128)(2,1)} %get-tuple-element.25.xt_ref) | copy-start | bytes 3932164
  124.0 6.8 %copy-start.2 = (bf16[8,128,384]{2,1,0:T(8,128)(2,1)}, bf16[8,128,384]{2,1,0:T(8,128)(2,1)S(1)}, u32[]{:S(2)}) copy-start(bf16[8,128,384]{2,1,0:T(8,128)(2,1)S(1)} %all_to_all.31.mine_ref) | copy-start | bytes 2359300
  124.0 4.2 %collective-permute-start.2 = (bf16[8,128,384]{2,1,0:T(8,128)(2,1)S(1)}, bf16[8,128,384]{2,1,0:T(8,128)(2,1)S(1)}, u32[]{:S(2)}, u32[]{:S(2)}) collective-permute-start(bf16[8,128,384]{2,1,0:T(8,128)(2,1)S(1)} %all_to_all.31.mine_ref), channel_id=1, source_target_pairs={{0,32},{32,0},{1,33},{33,1},{2,34},{34,2},{3,35},{35,3},{4,36},{36... | collective-permute-start | bytes 2359304 | tf_op jit(solution)/shard_map/ppermute | solution.py:296
  128.1 2.6 %copy-start.4 = (bf16[8,128,384]{2,1,0:T(8,128)(2,1)}, bf16[8,128,384]{2,1,0:T(8,128)(2,1)S(1)}, u32[]{:S(2)}) copy-start(bf16[8,128,384]{2,1,0:T(8,128)(2,1)S(1)} %collective-permute-done.2.far_ref.other_ref) | copy-start | bytes 2359300
  155.9 18.4 %all-to-all-start.4 = ((bf16[32,32,384]{2,1,0:T(8,128)(2,1)}), bf16[32,32,384]{2,1,0:T(8,128)(2,1)S(1)}, u32[]{:S(2)}, u32[]{:S(2)}) async-start(bf16[32,32,384]{2,1,0:T(8,128)(2,1)} %get-tuple-element.19), calls=%async_computation.4 | async-start | bytes 1572864 | tf_op jit(solution)/shard_map/all_to_all | solution.py:284
  163.0 17.2 %collective-permute-start.3 = (bf16[16,5120]{1,0:T(8,128)(2,1)}, bf16[16,5120]{1,0:T(8,128)(2,1)S(1)}, u32[]{:S(2)}, u32[]{:S(2)}) collective-permute-start(bf16[16,5120]{1,0:T(8,128)(2,1)} %get-tuple-element.21), channel_id=1, source_target_pairs={{0,2},{2,0},{1,3},{3,1},{4,6},{6,4},{5,7},{7,5},{8,10},{10,8},{9,1... | collective-permute-start | bytes 491528 | tf_op jit(solution)/shard_map/ppermute | solution.py:296
  164.9 25.1 %collective-permute-start.4 = (bf16[16,5120]{1,0:T(8,128)(2,1)}, bf16[16,5120]{1,0:T(8,128)(2,1)S(1)}, u32[]{:S(2)}, u32[]{:S(2)}) collective-permute-start(bf16[16,5120]{1,0:T(8,128)(2,1)} %get-tuple-element.22), channel_id=1, source_target_pairs={{0,2},{2,0},{1,3},{3,1},{4,6},{6,4},{5,7},{7,5},{8,10},{10,8},{9,1... | collective-permute-start | bytes 491528 | tf_op jit(solution)/shard_map/ppermute | solution.py:296
  174.3 15.7 %copy-start.9 = (bf16[32,32,384]{2,1,0:T(8,128)(2,1)}, bf16[32,32,384]{2,1,0:T(8,128)(2,1)S(1)}, u32[]{:S(2)}) copy-start(bf16[32,32,384]{2,1,0:T(8,128)(2,1)S(1)} %all-to-all-done.4.refs_0_) | copy-start | bytes 2359300
  180.2 9.8 %copy-start.10 = (bf16[16,5120]{1,0:T(8,128)(2,1)}, bf16[16,5120]{1,0:T(8,128)(2,1)S(1)}, u32[]{:S(2)}) copy-start(bf16[16,5120]{1,0:T(8,128)(2,1)S(1)} %collective-permute-done.3.refs_1_) | copy-start | bytes 491524
  190.0 0.7 copy-start.11
Sparse Core Ops, SparseCore 0:
  10.6 69.3 all-gather.1
  130.9 64.0 reduce-scatter.1

commit v6 on v5

--- a/solution.py
+++ b/solution.py
@@ -38,7 +38,7 @@
     return lax.dot_general(a, b, (dims, ((), ())), preferred_element_type=F32)
 
 
-def pack_kernel(me_ref, counts_ref, dest_ref, tok_ref, cot_ref, out_ref, one_ref):
+def pack_kernel(me_ref, counts_ref, dest_ref, tok_ref, cot_ref, out_ref):
     me = me_ref[0]
     rows = lax.broadcasted_iota(jnp.int32, (G, G), 0)
     pick = (rows == dest_ref[...]).astype(F32).astype(BF)
@@ -54,7 +54,6 @@
             if start != d * W:
                 moved = pltpu.roll(moved, WP - (d * W - start), 1)
             moved = jnp.where(lane < W, moved, extra).astype(BF)
-            one_ref[d, t * G : (t + 1) * G, :] = moved
             for y in range(Y):
                 out_ref[y * G + d, t * G : (t + 1) * G, :] = moved
 
@@ -62,12 +61,9 @@
 def pack(me, counts, dest, tokens, cotangent):
     return pl.pallas_call(
         pack_kernel,
-        out_shape=(
-            jax.ShapeDtypeStruct((Y * G, 2 * G, WP), BF),
-            jax.ShapeDtypeStruct((G, 2 * G, WP), BF),
-        ),
+        out_shape=jax.ShapeDtypeStruct((Y * G, 2 * G, WP), BF),
         in_specs=[SMEM, SMEM, VMEM, VMEM, VMEM],
-        out_specs=(VMEM, VMEM),
+        out_specs=VMEM,
         name="pack",
     )(me, counts, dest, tokens, cotangent)
 
@@ -99,6 +95,7 @@
         out_shape=(jax.ShapeDtypeStruct((2, E, R, W), BF), jax.ShapeDtypeStruct((2, E, W, R), BF)),
         in_specs=[VMEM, VMEM],
         out_specs=(VMEM, VMEM),
+        compiler_params=pltpu.CompilerParams(vmem_limit_bytes=LIMIT),
         name="prepare",
     )(own, other)
 
@@ -134,7 +131,7 @@
         ),
         compiler_params=pltpu.CompilerParams(vmem_limit_bytes=LIMIT),
         name="first",
-    )(expert, half, x, weight, *add)
+    )(expert, half, x, pltpu.with_memory_space_constraint(weight, pltpu.HBM), *add)
 
 
 def middle_kernel(part_ref, out_ref):
@@ -236,33 +233,51 @@
     )(expert, core, weight, mine, far)
 
 
-def unpack_kernel(*refs):
-    recv_ref, layer_ref, grad_ref = refs[0], refs[-2], refs[-1]
-    add_refs = refs[1:-2]
+def unpack_rows(recv_ref, t):
     low = lax.broadcasted_iota(jnp.int32, (G, 128), 1) < W - 256
+    rows = slice(t * G, (t + 1) * G)
+    for d in range(0, G, 2):
+        left = recv_ref[d, rows, :].astype(F32) + recv_ref[G + d, rows, :].astype(F32)
+        right = recv_ref[d + 1, rows, :].astype(F32) + recv_ref[G + d + 1, rows, :].astype(F32)
+        right = pltpu.roll(right, W - 256, 1)
+        yield slice(d * W, d * W + 256), left[:, 0:256]
+        yield slice(d * W + 256, d * W + 384), jnp.where(low, left[:, 256:384], right[:, 0:128])
+        yield slice(d * W + 384, d * W + 640), right[:, 128:384]
+
+
+def unpack_other_kernel(recv_ref, out_ref):
+    for t in range(2):
+        for at, part in unpack_rows(recv_ref, t):
+            out_ref[t, :, at] = part.astype(BF)
+
+
+def unpack_other(recv):
+    return pl.pallas_call(
+        unpack_other_kernel,
+        out_shape=jax.ShapeDtypeStruct((2, E * C, D), BF),
+        in_specs=[VMEM],
+        out_specs=VMEM,
+        compiler_params=pltpu.CompilerParams(vmem_limit_bytes=LIMIT),
+        name="unpack_other",
+    )(recv)
+
+
+def unpack_own_kernel(recv_ref, add_ref, layer_ref, grad_ref):
     for t, ref in enumerate((layer_ref, grad_ref)):
-        rows = slice(t * G, (t + 1) * G)
-        for d in range(0, G, 2):
-            left = recv_ref[d, rows, :].astype(F32) + recv_ref[G + d, rows, :].astype(F32)
-            right = recv_ref[d + 1, rows, :].astype(F32) + recv_ref[G + d + 1, rows, :].astype(F32)
-            right = pltpu.roll(right, W - 256, 1)
-            at = d * W
-            cut = jnp.where(low, left[:, 256:384], right[:, 0:128])
-            for lo, hi, part in ((0, 256, left[:, 0:256]), (256, 384, cut), (384, 640, right[:, 128:384])):
-                if add_refs:
-                    part = part + add_refs[t][:, at + lo : at + hi].astype(F32)
-                ref[:, at + lo : at + hi] = part.astype(BF)
-
-
-def unpack(recv, *add):
+        for at, part in unpack_rows(recv_ref, t):
+            ref[:, at] = (part + add_ref[t, :, at].astype(F32)).astype(BF)
+
+
+def unpack_own(recv, add):
     shape = jax.ShapeDtypeStruct((E * C, D), BF)
     return pl.pallas_call(
-        unpack_kernel,
+        unpack_own_kernel,
         out_shape=(shape, shape),
-        in_specs=[VMEM] * (1 + len(add)),
+        in_specs=[VMEM, VMEM],
         out_specs=(VMEM, VMEM),
-        name="unpack",
-    )(recv, *add)
+        compiler_params=pltpu.CompilerParams(vmem_limit_bytes=LIMIT),
+        name="unpack_own",
+    )(recv, add)
 
 
 def widen_kernel(own_ref, gate_up_ref, down_ref):
@@ -306,10 +321,13 @@
     me = lax.axis_index(GRP).reshape(1).astype(jnp.int32)
     near = lax.dynamic_index_in_dim(placement.reshape(Z, N), lax.axis_index(NEAR), 1, keepdims=False)
     expert = near // (Z * N // E)
-    sent, one = pack(me, counts[0, 0], destination[0], tokens[0], cotangent[0])
-    (other,) = swap(one)
+    rows = jnp.concatenate([tokens, cotangent], axis=0)
+    table = jnp.concatenate([counts[0, 0], destination[0, 0]])[None]
+    far_table, far_rows = swap(table, rows)
+    sent = pack(me, counts[0, 0], destination[0], tokens[0], cotangent[0])
     own = exchange(sent, PLANE)
-    other = exchange(jnp.concatenate([other] * Y, axis=0), PLANE)
+    sent = pack(me, far_table[0, 0:E], far_table[:, E:], far_rows[0], far_rows[1])
+    other = exchange(sent, PLANE)
     x, xt = prepare(own, other)
     core = lax.axis_index("core").reshape(1).astype(jnp.int32)
     got = swap_cores(first(expert, 1 - core, x, weight))
@@ -319,9 +337,9 @@
     far = swap_cores(mine)
     reduced = scatter(weigh(expert, core, xt, mine, far))
     own, other = last(expert, core, weight, mine, far)
-    other = unpack(exchange(other, PLANE))
-    other = swap(*other)
-    layer_out, input_grad = unpack(exchange(own, PLANE), *other)
+    other = unpack_other(exchange(other, PLANE))
+    (other,) = swap(other)
+    layer_out, input_grad = unpack_own(exchange(own, PLANE), other)
     gate_up_grad, down_grad = widen(reduced)
     return (layer_out[None], input_grad[None], gate_up_grad, down_grad)
 

time: 204 us -> 199 us (0.975)
  the two profiles are of different devices: /device:TPU:2 before, /device:TPU:18 now
where the time goes in v6:
time: 199 us; the launch traced here: 198 us
  waiting for transfers between devices  69.2 us (35%)
  blocking collectives  49 us (25%)
  starting transfers between devices  36.9 us (19%)
  Pallas kernels  22.3 us (11%)
  between operations  14.2 us (7%)
  other arithmetic  3.46 us (2%)
  local copies, waits for them, and re-layouts  3.23 us (2%)
    all_to_all x3, blocking collectives, exchange(): return lax.all_to_all(x, axes, split_axis=0, concat_axis=0, tiled=True)  49 us
    all_to_all x3, waiting for transfers between devices, exchange(): return lax.all_to_all(x, axes, split_axis=0, concat_axis=0, tiled=True)  25.4 us
    all_to_all x3, starting transfers between devices, exchange(): return lax.all_to_all(x, axes, split_axis=0, concat_axis=0, tiled=True)  24.3 us
    ppermute x5, waiting for transfers between devices, swap(): return [lax.ppermute(x, axis, ((0, 1), (1, 0))) for x in xs]  21.2 us
    all_gather x1, waiting for transfers between devices, gather(): return lax.all_gather(x, 'z_hi', axis=0, tiled=True)  18 us
    ppermute x5, starting transfers between devices, swap(): return [lax.ppermute(x, axis, ((0, 1), (1, 0))) for x in xs]  12.5 us
    pallas_call x1, Pallas kernels, last(): pl.pallas_call(last_kernel, out_shape=(shape, shape), in_specs=[SMEM, SME...  6.05 us
    pallas_call x2, Pallas kernels, first(): pl.pallas_call(first_kernel, out_shape=jax.ShapeDtypeStruct((Z, H, 3 * S)...  5.22 us
  transfers between devices with their start and end apart: 10, of which 8 were waited for; matrix products, arithmetic and copies ran while one was open for 2% of the time, Pallas kernels for 6%

profile of v6, /device:TPU:18, one launch (start us, length us, event | category | flops | bytes accessed | tf_op | source)
XLA Modules:
  0.0 198.3 jit_solution(9567818709831684745)
XLA Ops:
  7.2 0.0 all-gather.2.cloned.1.call-start
  7.2 1.7 pad_maximum_fusion.1
  8.9 0.0 all-gather.2.cloned.1.call-update
  8.9 1.0 pad_maximum_fusion
  9.9 3.8 %collective-permute-start.1 = (bf16[2,16,5120]{2,1,0:T(8,128)(2,1)S(1)}, bf16[2,16,5120]{2,1,0:T(8,128)(2,1)S(1)}, u32[]{:S(2)}, u32[]{:S(2)}) collective-permute-start(bf16[2,16,5120]{2,1,0:T(8,128)(2,1)S(1)} %pad_maximum_fusion), channel_id=1, source_target_pairs={{0,2},{2,0},{1,3},{3,1},{4,6},{6,4},{5,7},{7,5},{8,10},{10,8},{9,1... | collective-permute-start | bytes 983048 | tf_op jit(solution)/shard_map/ppermute | solution.py:311
  13.8 0.7 add_bitcast_fusion
  14.5 2.0 %collective-permute-start = (s32[1,20]{1,0:T(1,128)S(1)}, s32[1,20]{1,0:T(1,128)S(1)}, u32[]{:S(2)}, u32[]{:S(2)}) collective-permute-start(s32[1,20]{1,0:T(1,128)S(1)} %add_bitcast_fusion), channel_id=1, source_target_pairs={{0,2},{2,0},{1,3},{3,1},{4,6},{6,4},{5,7},{7,5},{8,10},{10,8},{9,1... | collective-permute-start | bytes 248 | tf_op jit(solution)/shard_map/ppermute | solution.py:311
  16.5 2.3 %pack.2 = bf16[32,32,384]{2,1,0:T(8,128)(2,1)} custom-call(s32[1]{0:T(128)} %bitcast.2.me_ref, s32[4]{0:T(128)} %bitcast.22, s32[1,16]{1,0:T(1,128)} %bitcast.24, bf16[16,5120]{1,0:T(8,128)(2,1)} %bitcast.18, bf16[16,5120]{1,0:T(8,128)(2,1)} %bitcast.19), custom_call_target="tpu_custom_call" | custom-call | tf_op jit(solution)/shard_map/pack/pallas_call | solution.py:62
  18.8 9.3 %all-to-all-start = ((bf16[32,32,384]{2,1,0:T(8,128)(2,1)}), bf16[32,32,384]{2,1,0:T(8,128)(2,1)S(1)}, u32[]{:S(2)}, u32[]{:S(2)}) async-start(bf16[32,32,384]{2,1,0:T(8,128)(2,1)} %pack.2), calls=%async_computation | async-start | bytes 1572864 | tf_op jit(solution)/shard_map/all_to_all | solution.py:299
  28.2 0.0 copy-start.5
  28.2 0.0 collective-permute-done
  28.2 0.6 slice.13.dest_ref
  28.8 0.5 slice_bitcast_fusion.2.counts_ref
  29.3 0.0 collective-permute-done.1
  29.3 0.7 slice_bitcast_fusion
  30.1 2.2 %pack.3 = bf16[32,32,384]{2,1,0:T(8,128)(2,1)} custom-call(s32[1]{0:T(128)} %bitcast.2.me_ref, s32[4]{0:T(128)} %slice_bitcast_fusion.2.counts_ref, s32[1,16]{1,0:T(1,128)} %slice.13.dest_ref, bf16[16,5120]{1,0:T(8,128)(2,1)} %get-tuple-element.21.tok_ref, bf16[16,5120]{1,0:T(8,128)(2,1)} %get-tuple-element.20.cot_ref), custom_call_target="tpu_custom_call" | custom-call | tf_op jit(solution)/shard_map/pack/pallas_call | solution.py:62
  32.3 6.8 %all-to-all-done.own_ref = bf16[32,32,384]{2,1,0:T(8,128)(2,1)S(1)} async-done(((bf16[32,32,384]{2,1,0:T(8,128)(2,1)}), bf16[32,32,384]{2,1,0:T(8,128)(2,1)S(1)}, u32[]{:S(2)}, u32[]{:S(2)}) %all-to-all-start) | async-done | bytes 786464 | tf_op jit(solution)/shard_map/all_to_all | solution.py:299
  39.1 7.5 %all-to-all-start.1 = ((bf16[32,32,384]{2,1,0:T(8,128)(2,1)}), bf16[32,32,384]{2,1,0:T(8,128)(2,1)S(1)}, u32[]{:S(2)}, u32[]{:S(2)}) async-start(bf16[32,32,384]{2,1,0:T(8,128)(2,1)} %pack.3), calls=%async_computation.1 | async-start | bytes 1572864 | tf_op jit(solution)/shard_map/all_to_all | solution.py:299
  46.6 0.0 reduce-scatter.2.cloned.1.call-start
  46.6 0.0 copy-done.5
  46.7 0.1 reshape.17
  46.7 0.2 dynamic-slice_reduce_fusion
  46.9 0.0 copy-start.4
  46.9 10.6 %all-to-all-done.1.other_ref = bf16[32,32,384]{2,1,0:T(8,128)(2,1)S(1)} async-done(((bf16[32,32,384]{2,1,0:T(8,128)(2,1)}), bf16[32,32,384]{2,1,0:T(8,128)(2,1)S(1)}, u32[]{:S(2)}, u32[]{:S(2)}) %all-to-all-start.1) | async-done | bytes 786464 | tf_op jit(solution)/shard_map/all_to_all | solution.py:299
  57.6 0.8 prepare.1
  58.4 0.0 copy-start.2
  58.4 1.0 copy-done.2
  59.5 18.0 %all-gather.2.cloned.1.call-done.weight_ref = bf16[8,3,320,128]{3,2,1,0:T(8,128)(2,1)} async-done(((bf16[1,3,320,128]{3,2,1,0:T(8,128)(2,1)}), bf16[8,3,320,128]{3,2,1,0:T(8,128)(2,1)}) %all-gather.2.cloned.1.call-update) | async-done | bytes 1966096 | tf_op jit(solution)/shard_map/all_gather | solution.py:303
  77.5 2.6 %first.2 = bf16[8,128,384]{2,1,0:T(8,128)(2,1)S(1)} custom-call(s32[8]{0:T(128)S(1)} %and_select_fusion.expert_ref, s32[1]{0:T(128)S(6)} %sub.8.half_ref, bf16[2,4,256,320]{3,2,1,0:T(8,128)(2,1)S(1)} %get-tuple-element.12.x_ref, bf16[8,3,320,128]{3,2,1,0:T(8,128)(2,1)} %all-gather.2.cloned.1.call-done.weight_ref), custom_call_target="tpu_custom_call" | custom-call | tf_op jit(solution)/shard_map/first/pallas_call | solution.py:119
  80.1 1.9 collective-permute-start.2
  82.0 2.3 %collective-permute-done.2.refs_0_ = bf16[8,128,384]{2,1,0:T(8,128)(2,1)S(1)} collective-permute-done((bf16[8,128,384]{2,1,0:T(8,128)(2,1)S(1)}, bf16[8,128,384]{2,1,0:T(8,128)(2,1)S(1)}, u32[]{:S(2)}, u32[]{:S(2)}) %collective-permute-start.2) | collective-permute-done | bytes 786464 | tf_op jit(solution)/shard_map/ppermute | solution.py:311
  84.3 2.6 %first.3 = bf16[8,128,384]{2,1,0:T(8,128)(2,1)S(1)} custom-call(s32[8]{0:T(128)S(1)} %and_select_fusion.expert_ref, s32[1]{0:T(128)} %bitcast.half_ref.core_ref, bf16[2,4,256,320]{3,2,1,0:T(8,128)(2,1)S(1)} %get-tuple-element.12.x_ref, bf16[8,3,320,128]{3,2,1,0:T(8,128)(2,1)} %all-gather.2.cloned.1.call-done.weight_ref, ...), custom_call_target="tpu_custom_call" | custom-call | tf_op jit(solution)/shard_map/first/pallas_call | solution.py:119
  86.9 17.2 %all_to_all.30.part_ref = bf16[8,128,384]{2,1,0:T(8,128)(2,1)S(1)} all-to-all(bf16[8,128,384]{2,1,0:T(8,128)(2,1)S(1)} %first.3), channel_id=1, replica_groups=mesh['y_lo'=2,'x'=4,'core'=2,'z_hi'=8,'z_lo'=2,'y_hi'=2] {'y_lo','x'}, dimensions={0} | all-to-all | bytes 1572864 | tf_op jit(solution)/shard_map/all_to_all | solution.py:299
  104.1 0.0 copy-start.3
  104.1 0.4 middle.1
  104.5 14.7 %all_to_all.31.mine_ref = bf16[8,128,384]{2,1,0:T(8,128)(2,1)S(1)} all-to-all(bf16[8,128,384]{2,1,0:T(8,128)(2,1)S(1)} %middle.1), channel_id=1, replica_groups=mesh['y_lo'=2,'x'=4,'core'=2,'z_hi'=8,'z_lo'=2,'y_hi'=2] {'y_lo','x'}, dimensions={0} | all-to-all | bytes 1572864 | tf_op jit(solution)/shard_map/all_to_all | solution.py:299
  119.2 0.0 copy-start
  119.2 1.9 collective-permute-start.3
  121.1 2.3 %collective-permute-done.3.far_ref.other_ref = bf16[8,128,384]{2,1,0:T(8,128)(2,1)S(1)} collective-permute-done((bf16[8,128,384]{2,1,0:T(8,128)(2,1)S(1)}, bf16[8,128,384]{2,1,0:T(8,128)(2,1)S(1)}, u32[]{:S(2)}, u32[]{:S(2)}) %collective-permute-start.3) | collective-permute-done | bytes 786464 | tf_op jit(solution)/shard_map/ppermute | solution.py:311
  123.4 0.0 copy-start.1
  123.4 0.0 copy-done.4
  123.4 0.0 copy-done.3
  123.4 2.6 %weigh.1 = bf16[8,3,320,128]{3,2,1,0:T(8,128)(2,1)} custom-call(s32[8]{0:T(128)S(1)} %and_select_fusion.expert_ref, s32[1]{0:T(128)} %bitcast.half_ref.core_ref, bf16[2,4,320,256]{3,2,1,0:T(8,128)(2,1)S(1)} %copy-done.3, bf16[8,128,384]{2,1,0:T(8,128)(2,1)S(1)} %all_to_all.31.mine_ref, bf16[8,128,384]{2,1,0:T(8,128)(2,1)S(1)} %collective-permute-done.3.far_ref.other_ref), custom_call_target="tpu_custom_call" | custom-call | tf_op jit(solution)/shard_map/weigh/pallas_call | solution.py:185
  126.0 0.0 copy-done
  126.0 0.0 copy-done.1
  126.0 0.0 reduce-scatter.2.cloned.1.call-update
  126.0 6.1 %last.1 = (bf16[32,32,384]{2,1,0:T(8,128)(2,1)}, bf16[32,32,384]{2,1,0:T(8,128)(2,1)}) custom-call(s32[8]{0:T(128)} %copy-done.4, s32[1]{0:T(128)} %bitcast.half_ref.core_ref, bf16[8,3,320,128]{3,2,1,0:T(8,128)(2,1)} %all-gather.2.cloned.1.call-done.weight_ref, bf16[8,128,384]{2,1,0:T(8,128)(2,1)} %copy-done, bf16[8,128,384]{2,1,0:T(8,128)(2,1)} %copy-done.1), custom_call_target="tpu_custom_call" | custom-call | tf_op jit(solution)/shard_map/last/pallas_call | solution.py:226
  132.1 17.1 %all_to_all.32.recv_ref = bf16[32,32,384]{2,1,0:T(8,128)(2,1)S(1)} all-to-all(bf16[32,32,384]{2,1,0:T(8,128)(2,1)} %get-tuple-element.14), channel_id=1, replica_groups=mesh['y_lo'=2,'x'=4,'core'=2,'z_hi'=8,'z_lo'=2,'y_hi'=2] {'y_hi','y_lo',..., dimensions={0} | all-to-all | bytes 1572864 | tf_op jit(solution)/shard_map/all_to_all | solution.py:299
  149.1 7.5 %all-to-all-start.4 = ((bf16[32,32,384]{2,1,0:T(8,128)(2,1)}), bf16[32,32,384]{2,1,0:T(8,128)(2,1)S(1)}, u32[]{:S(2)}, u32[]{:S(2)}) async-start(bf16[32,32,384]{2,1,0:T(8,128)(2,1)} %get-tuple-element.13), calls=%async_computation.4 | async-start | bytes 1572864 | tf_op jit(solution)/shard_map/all_to_all | solution.py:299
  156.6 0.1 unpack_other.1
  156.7 2.9 %collective-permute-start.4 = (bf16[2,16,5120]{2,1,0:T(8,128)(2,1)S(1)}, bf16[2,16,5120]{2,1,0:T(8,128)(2,1)S(1)}, u32[]{:S(2)}, u32[]{:S(2)}) collective-permute-start(bf16[2,16,5120]{2,1,0:T(8,128)(2,1)S(1)} %unpack_other.1), channel_id=1, source_target_pairs={{0,2},{2,0},{1,3},{3,1},{4,6},{6,4},{5,7},{7,5},{8,10},{10,8},{9,1... | collective-permute-start | bytes 983048 | tf_op jit(solution)/shard_map/ppermute | solution.py:311
  159.6 7.9 %all-to-all-done.4.recv_ref = bf16[32,32,384]{2,1,0:T(8,128)(2,1)S(1)} async-done(((bf16[32,32,384]{2,1,0:T(8,128)(2,1)}), bf16[32,32,384]{2,1,0:T(8,128)(2,1)S(1)}, u32[]{:S(2)}, u32[]{:S(2)}) %all-to-all-start.4) | async-done | bytes 786464 | tf_op jit(solution)/shard_map/all_to_all | solution.py:299
  167.6 16.7 %collective-permute-done.4.add_ref = bf16[2,16,5120]{2,1,0:T(8,128)(2,1)S(1)} collective-permute-done((bf16[2,16,5120]{2,1,0:T(8,128)(2,1)S(1)}, bf16[2,16,5120]{2,1,0:T(8,128)(2,1)S(1)}, u32[]{:S(2)}, u32[]{:S(2)}) %collective-permute-start.4) | collective-permute-done | bytes 327712 | tf_op jit(solution)/shard_map/ppermute | solution.py:311
  184.2 0.9 unpack_own.1
  185.1 4.6 %reduce-scatter.2.cloned.1.call-done.own_ref = bf16[1,3,320,128]{3,2,1,0:T(8,128)(2,1)} async-done(((bf16[8,3,320,128]{3,2,1,0:T(8,128)(2,1)}), bf16[1,3,320,128]{3,2,1,0:T(8,128)(2,1)}) %reduce-scatter.2.cloned.1.call-update) | async-done | bytes 245776 | tf_op jit(solution)/shard_map/reduce_scatter | solution.py:307
  189.7 1.7 widen.1
  (1 shorter events, 0.0 us)
Async XLA Ops:
  7.2 70.3 %all-gather.2.cloned.1.call-start = ((), (), s32[]{:S(2)}) async-start(), calls=%async_computation.7 | async-start | bytes 2211840 | tf_op jit(solution)/shard_map/all_gather | solution.py:303
  9.9 19.4 %collective-permute-start.1 = (bf16[2,16,5120]{2,1,0:T(8,128)(2,1)S(1)}, bf16[2,16,5120]{2,1,0:T(8,128)(2,1)S(1)}, u32[]{:S(2)}, u32[]{:S(2)}) collective-permute-start(bf16[2,16,5120]{2,1,0:T(8,128)(2,1)S(1)} %pad_maximum_fusion), channel_id=1, source_target_pairs={{0,2},{2,0},{1,3},{3,1},{4,6},{6,4},{5,7},{7,5},{8,10},{10,8},{9,1... | collective-permute-start | bytes 983048 | tf_op jit(solution)/shard_map/ppermute | solution.py:311
  14.5 13.6 %collective-permute-start = (s32[1,20]{1,0:T(1,128)S(1)}, s32[1,20]{1,0:T(1,128)S(1)}, u32[]{:S(2)}, u32[]{:S(2)}) collective-permute-start(s32[1,20]{1,0:T(1,128)S(1)} %add_bitcast_fusion), channel_id=1, source_target_pairs={{0,2},{2,0},{1,3},{3,1},{4,6},{6,4},{5,7},{7,5},{8,10},{10,8},{9,1... | collective-permute-start | bytes 248 | tf_op jit(solution)/shard_map/ppermute | solution.py:311
  18.8 20.3 %all-to-all-start = ((bf16[32,32,384]{2,1,0:T(8,128)(2,1)}), bf16[32,32,384]{2,1,0:T(8,128)(2,1)S(1)}, u32[]{:S(2)}, u32[]{:S(2)}) async-start(bf16[32,32,384]{2,1,0:T(8,128)(2,1)} %pack.2), calls=%async_computation | async-start | bytes 1572864 | tf_op jit(solution)/shard_map/all_to_all | solution.py:299
  28.2 18.5 %copy-start.5 = (s32[32]{0:T(128)S(1)}, s32[32]{0:T(128)}, u32[]{:S(2)}) copy-start(s32[32]{0:T(128)} %param.11) | copy-start | bytes 388
  39.1 18.4 %all-to-all-start.1 = ((bf16[32,32,384]{2,1,0:T(8,128)(2,1)}), bf16[32,32,384]{2,1,0:T(8,128)(2,1)S(1)}, u32[]{:S(2)}, u32[]{:S(2)}) async-start(bf16[32,32,384]{2,1,0:T(8,128)(2,1)} %pack.3), calls=%async_computation.1 | async-start | bytes 1572864 | tf_op jit(solution)/shard_map/all_to_all | solution.py:299
  46.6 143.1 %reduce-scatter.2.cloned.1.call-start = ((), (), s32[]{:S(2)}) async-start(), calls=%async_computation.8 | async-start | bytes 2211840 | tf_op jit(solution)/shard_map/reduce_scatter | solution.py:307
  46.9 76.4 %copy-start.4 = (s32[8]{0:T(128)}, s32[8]{0:T(128)S(1)}, u32[]{:S(2)}) copy-start(s32[8]{0:T(128)S(1)} %and_select_fusion.expert_ref) | copy-start | bytes 100
  58.4 1.1 copy-start.2
  80.1 4.2 %collective-permute-start.2 = (bf16[8,128,384]{2,1,0:T(8,128)(2,1)S(1)}, bf16[8,128,384]{2,1,0:T(8,128)(2,1)S(1)}, u32[]{:S(2)}, u32[]{:S(2)}) collective-permute-start(bf16[8,128,384]{2,1,0:T(8,128)(2,1)S(1)} %first.2), channel_id=1, source_target_pairs={{0,32},{32,0},{1,33},{33,1},{2,34},{34,2},{3,35},{35,3},{4,36},{36... | collective-permute-start | bytes 2359304 | tf_op jit(solution)/shard_map/ppermute | solution.py:311
  104.1 19.3 %copy-start.3 = (bf16[2,4,320,256]{3,2,1,0:T(8,128)(2,1)S(1)}, bf16[2,4,320,256]{3,2,1,0:T(8,128)(2,1)}, u32[]{:S(2)}) copy-start(bf16[2,4,320,256]{3,2,1,0:T(8,128)(2,1)} %copy-done.2) | copy-start | bytes 3932164
  119.2 6.8 %copy-start = (bf16[8,128,384]{2,1,0:T(8,128)(2,1)}, bf16[8,128,384]{2,1,0:T(8,128)(2,1)S(1)}, u32[]{:S(2)}) copy-start(bf16[8,128,384]{2,1,0:T(8,128)(2,1)S(1)} %all_to_all.31.mine_ref) | copy-start | bytes 2359300
  119.2 4.2 %collective-permute-start.3 = (bf16[8,128,384]{2,1,0:T(8,128)(2,1)S(1)}, bf16[8,128,384]{2,1,0:T(8,128)(2,1)S(1)}, u32[]{:S(2)}, u32[]{:S(2)}) collective-permute-start(bf16[8,128,384]{2,1,0:T(8,128)(2,1)S(1)} %all_to_all.31.mine_ref), channel_id=1, source_target_pairs={{0,32},{32,0},{1,33},{33,1},{2,34},{34,2},{3,35},{35,3},{4,36},{36... | collective-permute-start | bytes 2359304 | tf_op jit(solution)/shard_map/ppermute | solution.py:311
  123.4 2.6 %copy-start.1 = (bf16[8,128,384]{2,1,0:T(8,128)(2,1)}, bf16[8,128,384]{2,1,0:T(8,128)(2,1)S(1)}, u32[]{:S(2)}) copy-start(bf16[8,128,384]{2,1,0:T(8,128)(2,1)S(1)} %collective-permute-done.3.far_ref.other_ref) | copy-start | bytes 2359300
  149.1 18.4 %all-to-all-start.4 = ((bf16[32,32,384]{2,1,0:T(8,128)(2,1)}), bf16[32,32,384]{2,1,0:T(8,128)(2,1)S(1)}, u32[]{:S(2)}, u32[]{:S(2)}) async-start(bf16[32,32,384]{2,1,0:T(8,128)(2,1)} %get-tuple-element.13), calls=%async_computation.4 | async-start | bytes 1572864 | tf_op jit(solution)/shard_map/all_to_all | solution.py:299
  156.7 27.5 %collective-permute-start.4 = (bf16[2,16,5120]{2,1,0:T(8,128)(2,1)S(1)}, bf16[2,16,5120]{2,1,0:T(8,128)(2,1)S(1)}, u32[]{:S(2)}, u32[]{:S(2)}) collective-permute-start(bf16[2,16,5120]{2,1,0:T(8,128)(2,1)S(1)} %unpack_other.1), channel_id=1, source_target_pairs={{0,2},{2,0},{1,3},{3,1},{4,6},{6,4},{5,7},{7,5},{8,10},{10,8},{9,1... | collective-permute-start | bytes 983048 | tf_op jit(solution)/shard_map/ppermute | solution.py:311
Sparse Core Ops, SparseCore 0:
  10.6 66.7 all-gather.1
  126.1 63.5 reduce-scatter.1

commit v7 on v6

--- a/solution.py
+++ b/solution.py
@@ -100,38 +100,46 @@
     )(own, other)
 
 
-def first_kernel(expert_ref, half_ref, x_ref, weight_ref, *refs):
-    out_ref = refs[-1]
+def first_kernel(expert_ref, half_ref, x_ref, weight_ref, out_ref):
     for i in range(Z // 2):
         e = expert_ref[Z // 2 * pl.program_id(0) + i]
         both = jnp.concatenate([weight_ref[i, 0], weight_ref[i, 1]], axis=1)
-        gate_up = dot(x_ref[0, e], both)
-        hidden_grad = dot(x_ref[1, e], weight_ref[i, 2])
-        if len(refs) > 1:
-            gate_up = gate_up + refs[0][i, :, 0 : 2 * S].astype(F32)
-            hidden_grad = hidden_grad + refs[0][i, :, 2 * S : 3 * S].astype(F32)
-        out_ref[i, :, 0 : 2 * S] = gate_up.astype(BF)
-        out_ref[i, :, 2 * S : 3 * S] = hidden_grad.astype(BF)
-
-
-def first(expert, half, x, weight, *add):
-    rows = pl.BlockSpec((Z // 2, H, 3 * S), lambda i, expert, half: (i, 0, 0))
+        out_ref[i, :, 0 : 2 * S] = dot(x_ref[0, e], both).astype(out_ref.dtype)
+        out_ref[i, :, 2 * S : 3 * S] = dot(x_ref[1, e], weight_ref[i, 2]).astype(out_ref.dtype)
+
+
+def first(expert, half, x, weight, dtype):
     return pl.pallas_call(
         first_kernel,
-        out_shape=jax.ShapeDtypeStruct((Z, H, 3 * S), BF),
+        out_shape=jax.ShapeDtypeStruct((Z, H, 3 * S), dtype),
         grid_spec=pltpu.PrefetchScalarGridSpec(
             num_scalar_prefetch=2,
             grid=(2,),
             in_specs=[
                 pl.BlockSpec((2, E, H, W), lambda i, expert, half: (0, 0, half[0], 0)),
                 pl.BlockSpec((Z // 2, 3, W, S), lambda i, expert, half: (i, 0, 0, 0)),
-            ]
-            + [rows] * len(add),
-            out_specs=rows,
+            ],
+            out_specs=pl.BlockSpec((Z // 2, H, 3 * S), lambda i, expert, half: (i, 0, 0)),
         ),
         compiler_params=pltpu.CompilerParams(vmem_limit_bytes=LIMIT),
         name="first",
-    )(expert, half, x, pltpu.with_memory_space_constraint(weight, pltpu.HBM), *add)
+    )(expert, half, x, weight)
+
+
+def add_kernel(keep_ref, got_ref, out_ref):
+    for z in range(Z):
+        out_ref[z] = (keep_ref[z] + got_ref[z].astype(F32)).astype(BF)
+
+
+def add_cores(keep, got):
+    return pl.pallas_call(
+        add_kernel,
+        out_shape=jax.ShapeDtypeStruct((Z, H, 3 * S), BF),
+        in_specs=[VMEM, VMEM],
+        out_specs=VMEM,
+        compiler_params=pltpu.CompilerParams(vmem_limit_bytes=LIMIT),
+        name="add_cores",
+    )(keep, got)
 
 
 def middle_kernel(part_ref, out_ref):
@@ -185,7 +193,7 @@
     return pl.pallas_call(
         weigh_kernel,
         grid=(2,),
-        out_shape=jax.ShapeDtypeStruct((Z, 3, W, S), BF),
+        out_shape=pltpu.HBM((Z, 3, W, S), BF),
         in_specs=[SMEM, SMEM, pl.BlockSpec((2, E, W, R), lambda i: (0, 0, 0, 0)), rows, rows],
         out_specs=pl.BlockSpec((Z // 2, 3, W, S), lambda i: (i, 0, 0, 0)),
         compiler_params=pltpu.CompilerParams(vmem_limit_bytes=LIMIT),
@@ -229,6 +237,7 @@
         in_specs=[SMEM, SMEM, VMEM, VMEM, VMEM],
         out_specs=(VMEM, VMEM),
         scratch_shapes=[pltpu.VMEM((2, E, R, W), F32)],
+        compiler_params=pltpu.CompilerParams(vmem_limit_bytes=LIMIT),
         name="last",
     )(expert, core, weight, mine, far)
 
@@ -330,8 +339,10 @@
     other = exchange(sent, PLANE)
     x, xt = prepare(own, other)
     core = lax.axis_index("core").reshape(1).astype(jnp.int32)
-    got = swap_cores(first(expert, 1 - core, x, weight))
-    parts = first(expert, core, x, weight, got)
+    streamed = pltpu.with_memory_space_constraint(weight, pltpu.HBM)
+    got = swap_cores(first(expert, 1 - core, x, streamed, BF))
+    keep = first(expert, core, x, weight, F32)
+    parts = add_cores(keep, got)
     act = middle(exchange(parts, CHIPS))
     mine = exchange(act, CHIPS)
     far = swap_cores(mine)

time: 199 us -> 197 us (0.990)
  the two profiles are of different devices: /device:TPU:18 before, /device:TPU:44 now
where the time goes in v7:
time: 197 us; the launch traced here: 196 us
  waiting for transfers between devices  73.1 us (37%)
  blocking collectives  49.2 us (25%)
  starting transfers between devices  33.6 us (17%)
  Pallas kernels  19 us (10%)
  between operations  14.2 us (7%)
  other arithmetic  3.46 us (2%)
  local copies, waits for them, and re-layouts  3.27 us (2%)
    all_to_all x3, blocking collectives, exchange(): return lax.all_to_all(x, axes, split_axis=0, concat_axis=0, tiled=True)  49.2 us
    all_to_all x3, waiting for transfers between devices, exchange(): return lax.all_to_all(x, axes, split_axis=0, concat_axis=0, tiled=True)  27.5 us
    all_to_all x3, starting transfers between devices, exchange(): return lax.all_to_all(x, axes, split_axis=0, concat_axis=0, tiled=True)  21 us
    all_gather x1, waiting for transfers between devices, gather(): return lax.all_gather(x, 'z_hi', axis=0, tiled=True)  18.7 us
    ppermute x5, waiting for transfers between devices, swap(): return [lax.ppermute(x, axis, ((0, 1), (1, 0))) for x in xs]  18.1 us
    ppermute x5, starting transfers between devices, swap(): return [lax.ppermute(x, axis, ((0, 1), (1, 0))) for x in xs]  12.5 us
    reduce_scatter x1, waiting for transfers between devices, scatter(): return lax.psum_scatter(x, 'z_hi', scatter_dimension=0, tiled=True)  8.86 us
    pallas_call x2, Pallas kernels, pack(): pl.pallas_call(pack_kernel, out_shape=jax.ShapeDtypeStruct((Y * G, 2 * G,...  4.49 us
  transfers between devices with their start and end apart: 10, of which 8 were waited for; matrix products, arithmetic and copies ran while one was open for 2% of the time, Pallas kernels for 6%

profile of v7, /device:TPU:44, one launch (start us, length us, event | category | flops | bytes accessed | tf_op | source)
XLA Modules:
  0.0 195.9 jit_solution(11065228865910684197)
XLA Ops:
  7.2 0.0 all-gather.2.cloned.1.call-start
  7.2 1.7 pad_maximum_fusion.1
  8.9 0.0 all-gather.2.cloned.1.call-update
  8.9 1.0 pad_maximum_fusion
  9.9 2.0 %collective-permute-start.1 = (bf16[2,16,5120]{2,1,0:T(8,128)(2,1)S(1)}, bf16[2,16,5120]{2,1,0:T(8,128)(2,1)S(1)}, u32[]{:S(2)}, u32[]{:S(2)}) collective-permute-start(bf16[2,16,5120]{2,1,0:T(8,128)(2,1)S(1)} %pad_maximum_fusion), channel_id=1, source_target_pairs={{0,2},{2,0},{1,3},{3,1},{4,6},{6,4},{5,7},{7,5},{8,10},{10,8},{9,1... | collective-permute-start | bytes 983048 | tf_op jit(solution)/shard_map/ppermute | solution.py:320
  12.0 0.7 add_bitcast_fusion
  12.7 3.8 %collective-permute-start = (s32[1,20]{1,0:T(1,128)S(1)}, s32[1,20]{1,0:T(1,128)S(1)}, u32[]{:S(2)}, u32[]{:S(2)}) collective-permute-start(s32[1,20]{1,0:T(1,128)S(1)} %add_bitcast_fusion), channel_id=1, source_target_pairs={{0,2},{2,0},{1,3},{3,1},{4,6},{6,4},{5,7},{7,5},{8,10},{10,8},{9,1... | collective-permute-start | bytes 248 | tf_op jit(solution)/shard_map/ppermute | solution.py:320
  16.5 2.3 %pack.2 = bf16[32,32,384]{2,1,0:T(8,128)(2,1)} custom-call(s32[1]{0:T(128)} %bitcast.2.me_ref, s32[4]{0:T(128)} %bitcast.22, s32[1,16]{1,0:T(1,128)} %bitcast.24, bf16[16,5120]{1,0:T(8,128)(2,1)} %bitcast.18, bf16[16,5120]{1,0:T(8,128)(2,1)} %bitcast.19), custom_call_target="tpu_custom_call" | custom-call | tf_op jit(solution)/shard_map/pack/pallas_call | solution.py:62
  18.8 7.5 %all-to-all-start = ((bf16[32,32,384]{2,1,0:T(8,128)(2,1)}), bf16[32,32,384]{2,1,0:T(8,128)(2,1)S(1)}, u32[]{:S(2)}, u32[]{:S(2)}) async-start(bf16[32,32,384]{2,1,0:T(8,128)(2,1)} %pack.2), calls=%async_computation | async-start | bytes 1572864 | tf_op jit(solution)/shard_map/all_to_all | solution.py:308
  26.3 0.0 collective-permute-done
  26.3 0.6 slice.13.dest_ref
  26.9 0.6 slice_bitcast_fusion.2.counts_ref
  27.5 0.0 copy-start.4
  27.5 0.0 collective-permute-done.1
  27.5 0.7 slice_bitcast_fusion
  28.2 2.2 %pack.3 = bf16[32,32,384]{2,1,0:T(8,128)(2,1)} custom-call(s32[1]{0:T(128)} %bitcast.2.me_ref, s32[4]{0:T(128)} %slice_bitcast_fusion.2.counts_ref, s32[1,16]{1,0:T(1,128)} %slice.13.dest_ref, bf16[16,5120]{1,0:T(8,128)(2,1)} %get-tuple-element.21.tok_ref, bf16[16,5120]{1,0:T(8,128)(2,1)} %get-tuple-element.20.cot_ref), custom_call_target="tpu_custom_call" | custom-call | tf_op jit(solution)/shard_map/pack/pallas_call | solution.py:62
  30.5 7.5 %all-to-all-done.own_ref = bf16[32,32,384]{2,1,0:T(8,128)(2,1)S(1)} async-done(((bf16[32,32,384]{2,1,0:T(8,128)(2,1)}), bf16[32,32,384]{2,1,0:T(8,128)(2,1)S(1)}, u32[]{:S(2)}, u32[]{:S(2)}) %all-to-all-start) | async-done | bytes 786464 | tf_op jit(solution)/shard_map/all_to_all | solution.py:308
  38.0 6.8 %all-to-all-start.1 = ((bf16[32,32,384]{2,1,0:T(8,128)(2,1)}), bf16[32,32,384]{2,1,0:T(8,128)(2,1)S(1)}, u32[]{:S(2)}, u32[]{:S(2)}) async-start(bf16[32,32,384]{2,1,0:T(8,128)(2,1)} %pack.3), calls=%async_computation.1 | async-start | bytes 1572864 | tf_op jit(solution)/shard_map/all_to_all | solution.py:308
  44.7 0.0 reduce-scatter.2.cloned.1.call-start
  44.8 0.0 copy-done.4
  44.8 0.1 reshape.17
  44.9 0.2 dynamic-slice_reduce_fusion
  45.1 11.3 %all-to-all-done.1.other_ref = bf16[32,32,384]{2,1,0:T(8,128)(2,1)S(1)} async-done(((bf16[32,32,384]{2,1,0:T(8,128)(2,1)}), bf16[32,32,384]{2,1,0:T(8,128)(2,1)S(1)}, u32[]{:S(2)}, u32[]{:S(2)}) %all-to-all-start.1) | async-done | bytes 786464 | tf_op jit(solution)/shard_map/all_to_all | solution.py:308
  56.4 0.8 prepare.1
  57.2 0.0 copy-start.1
  57.3 1.1 copy-done.1
  58.3 18.7 %all-gather.2.cloned.1.call-done.weight_ref = bf16[8,3,320,128]{3,2,1,0:T(8,128)(2,1)} async-done(((bf16[1,3,320,128]{3,2,1,0:T(8,128)(2,1)}), bf16[8,3,320,128]{3,2,1,0:T(8,128)(2,1)}) %all-gather.2.cloned.1.call-update) | async-done | bytes 1966096 | tf_op jit(solution)/shard_map/all_gather | solution.py:312
  77.0 0.0 copy-start
  77.0 2.6 %first.3 = bf16[8,128,384]{2,1,0:T(8,128)(2,1)S(1)} custom-call(s32[8]{0:T(128)S(1)} %and_select_fusion.expert_ref, s32[1]{0:T(128)S(6)} %sub.8.half_ref, bf16[2,4,256,320]{3,2,1,0:T(8,128)(2,1)S(1)} %get-tuple-element.12.x_ref, bf16[8,3,320,128]{3,2,1,0:T(8,128)(2,1)} %all-gather.2.cloned.1.call-done.weight_ref), custom_call_target="tpu_custom_call" | custom-call | tf_op jit(solution)/shard_map/first/pallas_call | solution.py:112
  79.6 1.9 collective-permute-start.2
  81.6 0.0 copy-done
  81.6 1.5 first.2.keep_ref
  83.1 0.7 collective-permute-done.2.got_ref
  83.8 0.1 add_cores.1
  84.0 15.1 %all_to_all.30.part_ref = bf16[8,128,384]{2,1,0:T(8,128)(2,1)S(1)} all-to-all(bf16[8,128,384]{2,1,0:T(8,128)(2,1)S(1)} %add_cores.1), channel_id=1, replica_groups=mesh['y_lo'=2,'x'=4,'core'=2,'z_hi'=8,'z_lo'=2,'y_hi'=2] {'y_lo','x'}, dimensions={0} | all-to-all | bytes 1572864 | tf_op jit(solution)/shard_map/all_to_all | solution.py:308
  99.1 0.0 copy-start.2
  99.1 0.4 middle.1
  99.5 15.0 %all_to_all.31.mine_ref = bf16[8,128,384]{2,1,0:T(8,128)(2,1)S(1)} all-to-all(bf16[8,128,384]{2,1,0:T(8,128)(2,1)S(1)} %middle.1), channel_id=1, replica_groups=mesh['y_lo'=2,'x'=4,'core'=2,'z_hi'=8,'z_lo'=2,'y_hi'=2] {'y_lo','x'}, dimensions={0} | all-to-all | bytes 1572864 | tf_op jit(solution)/shard_map/all_to_all | solution.py:308
  114.5 1.9 collective-permute-start.3
  116.4 2.3 %collective-permute-done.3.far_ref.other_ref = bf16[8,128,384]{2,1,0:T(8,128)(2,1)S(1)} collective-permute-done((bf16[8,128,384]{2,1,0:T(8,128)(2,1)S(1)}, bf16[8,128,384]{2,1,0:T(8,128)(2,1)S(1)}, u32[]{:S(2)}, u32[]{:S(2)}) %collective-permute-start.3) | collective-permute-done | bytes 786464 | tf_op jit(solution)/shard_map/ppermute | solution.py:320
  118.7 0.0 copy-done.2
  118.7 2.6 %weigh.1 = bf16[8,3,320,128]{3,2,1,0:T(8,128)(2,1)} custom-call(s32[8]{0:T(128)S(1)} %and_select_fusion.expert_ref, s32[1]{0:T(128)} %bitcast.half_ref.core_ref, bf16[2,4,320,256]{3,2,1,0:T(8,128)(2,1)S(1)} %copy-done.2, bf16[8,128,384]{2,1,0:T(8,128)(2,1)S(1)} %all_to_all.31.mine_ref, bf16[8,128,384]{2,1,0:T(8,128)(2,1)S(1)} %collective-permute-done.3.far_ref.other_ref), custom_call_target="tpu_custom_call" | custom-call | tf_op jit(solution)/shard_map/weigh/pallas_call | solution.py:193
  121.2 0.0 reduce-scatter.2.cloned.1.call-update
  121.3 3.7 %last.1 = (bf16[32,32,384]{2,1,0:T(8,128)(2,1)S(1)}, bf16[32,32,384]{2,1,0:T(8,128)(2,1)S(1)}) custom-call(s32[8]{0:T(128)S(1)} %and_select_fusion.expert_ref, s32[1]{0:T(128)} %bitcast.half_ref.core_ref, bf16[8,3,320,128]{3,2,1,0:T(8,128)(2,1)S(1)} %copy-done, bf16[8,128,384]{2,1,0:T(8,128)(2,1)S(1)} %all_to_all.31.mine_ref, ...), custom_call_target="tpu_custom_call" | custom-call | tf_op jit(solution)/shard_map/last/pallas_call | solution.py:234
  125.0 0.0 copy-start.3
  125.0 19.1 %all_to_all.32.recv_ref = bf16[32,32,384]{2,1,0:T(8,128)(2,1)S(1)} all-to-all(bf16[32,32,384]{2,1,0:T(8,128)(2,1)S(1)} %get-tuple-element.14), channel_id=1, replica_groups=mesh['y_lo'=2,'x'=4,'core'=2,'z_hi'=8,'z_lo'=2,'y_hi'=2] {'y_hi','y_lo',..., dimensions={0} | all-to-all | bytes 1572864 | tf_op jit(solution)/shard_map/all_to_all | solution.py:308
  144.0 0.0 copy-done.3
  144.1 6.8 %all-to-all-start.4 = ((bf16[32,32,384]{2,1,0:T(8,128)(2,1)}), bf16[32,32,384]{2,1,0:T(8,128)(2,1)S(1)}, u32[]{:S(2)}, u32[]{:S(2)}) async-start(bf16[32,32,384]{2,1,0:T(8,128)(2,1)} %copy-done.3), calls=%async_computation.4 | async-start | bytes 1572864 | tf_op jit(solution)/shard_map/all_to_all | solution.py:308
  150.8 0.1 unpack_other.1
  151.0 2.8 %collective-permute-start.4 = (bf16[2,16,5120]{2,1,0:T(8,128)(2,1)S(1)}, bf16[2,16,5120]{2,1,0:T(8,128)(2,1)S(1)}, u32[]{:S(2)}, u32[]{:S(2)}) collective-permute-start(bf16[2,16,5120]{2,1,0:T(8,128)(2,1)S(1)} %unpack_other.1), channel_id=1, source_target_pairs={{0,2},{2,0},{1,3},{3,1},{4,6},{6,4},{5,7},{7,5},{8,10},{10,8},{9,1... | collective-permute-start | bytes 983048 | tf_op jit(solution)/shard_map/ppermute | solution.py:320
  153.8 8.7 %all-to-all-done.4.recv_ref = bf16[32,32,384]{2,1,0:T(8,128)(2,1)S(1)} async-done(((bf16[32,32,384]{2,1,0:T(8,128)(2,1)}), bf16[32,32,384]{2,1,0:T(8,128)(2,1)S(1)}, u32[]{:S(2)}, u32[]{:S(2)}) %all-to-all-start.4) | async-done | bytes 786464 | tf_op jit(solution)/shard_map/all_to_all | solution.py:308
  162.5 15.1 %collective-permute-done.4.add_ref = bf16[2,16,5120]{2,1,0:T(8,128)(2,1)S(1)} collective-permute-done((bf16[2,16,5120]{2,1,0:T(8,128)(2,1)S(1)}, bf16[2,16,5120]{2,1,0:T(8,128)(2,1)S(1)}, u32[]{:S(2)}, u32[]{:S(2)}) %collective-permute-start.4) | collective-permute-done | bytes 327712 | tf_op jit(solution)/shard_map/ppermute | solution.py:320
  177.6 0.9 unpack_own.1
  178.4 8.9 %reduce-scatter.2.cloned.1.call-done.own_ref = bf16[1,3,320,128]{3,2,1,0:T(8,128)(2,1)} async-done(((bf16[8,3,320,128]{3,2,1,0:T(8,128)(2,1)}), bf16[1,3,320,128]{3,2,1,0:T(8,128)(2,1)}) %reduce-scatter.2.cloned.1.call-update) | async-done | bytes 245776 | tf_op jit(solution)/shard_map/reduce_scatter | solution.py:316
  187.3 1.7 widen.1
  (1 shorter events, 0.0 us)
Async XLA Ops:
  7.2 69.8 %all-gather.2.cloned.1.call-start = ((), (), s32[]{:S(2)}) async-start(), calls=%async_computation.7 | async-start | bytes 2211840 | tf_op jit(solution)/shard_map/all_gather | solution.py:312
  9.9 17.6 %collective-permute-start.1 = (bf16[2,16,5120]{2,1,0:T(8,128)(2,1)S(1)}, bf16[2,16,5120]{2,1,0:T(8,128)(2,1)S(1)}, u32[]{:S(2)}, u32[]{:S(2)}) collective-permute-start(bf16[2,16,5120]{2,1,0:T(8,128)(2,1)S(1)} %pad_maximum_fusion), channel_id=1, source_target_pairs={{0,2},{2,0},{1,3},{3,1},{4,6},{6,4},{5,7},{7,5},{8,10},{10,8},{9,1... | collective-permute-start | bytes 983048 | tf_op jit(solution)/shard_map/ppermute | solution.py:320
  12.7 13.6 %collective-permute-start = (s32[1,20]{1,0:T(1,128)S(1)}, s32[1,20]{1,0:T(1,128)S(1)}, u32[]{:S(2)}, u32[]{:S(2)}) collective-permute-start(s32[1,20]{1,0:T(1,128)S(1)} %add_bitcast_fusion), channel_id=1, source_target_pairs={{0,2},{2,0},{1,3},{3,1},{4,6},{6,4},{5,7},{7,5},{8,10},{10,8},{9,1... | collective-permute-start | bytes 248 | tf_op jit(solution)/shard_map/ppermute | solution.py:320
  18.8 19.1 %all-to-all-start = ((bf16[32,32,384]{2,1,0:T(8,128)(2,1)}), bf16[32,32,384]{2,1,0:T(8,128)(2,1)S(1)}, u32[]{:S(2)}, u32[]{:S(2)}) async-start(bf16[32,32,384]{2,1,0:T(8,128)(2,1)} %pack.2), calls=%async_computation | async-start | bytes 1572864 | tf_op jit(solution)/shard_map/all_to_all | solution.py:308
  27.5 17.3 %copy-start.4 = (s32[32]{0:T(128)S(1)}, s32[32]{0:T(128)}, u32[]{:S(2)}) copy-start(s32[32]{0:T(128)} %param.11) | copy-start | bytes 388
  38.0 18.4 %all-to-all-start.1 = ((bf16[32,32,384]{2,1,0:T(8,128)(2,1)}), bf16[32,32,384]{2,1,0:T(8,128)(2,1)S(1)}, u32[]{:S(2)}, u32[]{:S(2)}) async-start(bf16[32,32,384]{2,1,0:T(8,128)(2,1)} %pack.3), calls=%async_computation.1 | async-start | bytes 1572864 | tf_op jit(solution)/shard_map/all_to_all | solution.py:308
  44.7 142.6 %reduce-scatter.2.cloned.1.call-start = ((), (), s32[]{:S(2)}) async-start(), calls=%async_computation.8 | async-start | bytes 2211840 | tf_op jit(solution)/shard_map/reduce_scatter | solution.py:316
  57.2 1.1 copy-start.1
  77.0 4.6 %copy-start = (bf16[8,3,320,128]{3,2,1,0:T(8,128)(2,1)S(1)}, bf16[8,3,320,128]{3,2,1,0:T(8,128)(2,1)}, u32[]{:S(2)}) copy-start(bf16[8,3,320,128]{3,2,1,0:T(8,128)(2,1)} %all-gather.2.cloned.1.call-done.weight_ref) | copy-start | bytes 5898244
  79.6 4.2 %collective-permute-start.2 = (bf16[8,128,384]{2,1,0:T(8,128)(2,1)S(1)}, bf16[8,128,384]{2,1,0:T(8,128)(2,1)S(1)}, u32[]{:S(2)}, u32[]{:S(2)}) collective-permute-start(bf16[8,128,384]{2,1,0:T(8,128)(2,1)S(1)} %first.3), channel_id=1, source_target_pairs={{0,32},{32,0},{1,33},{33,1},{2,34},{34,2},{3,35},{35,3},{4,36},{36... | collective-permute-start | bytes 2359304 | tf_op jit(solution)/shard_map/ppermute | solution.py:320
  99.1 19.6 %copy-start.2 = (bf16[2,4,320,256]{3,2,1,0:T(8,128)(2,1)S(1)}, bf16[2,4,320,256]{3,2,1,0:T(8,128)(2,1)}, u32[]{:S(2)}) copy-start(bf16[2,4,320,256]{3,2,1,0:T(8,128)(2,1)} %copy-done.1) | copy-start | bytes 3932164
  114.5 4.2 %collective-permute-start.3 = (bf16[8,128,384]{2,1,0:T(8,128)(2,1)S(1)}, bf16[8,128,384]{2,1,0:T(8,128)(2,1)S(1)}, u32[]{:S(2)}, u32[]{:S(2)}) collective-permute-start(bf16[8,128,384]{2,1,0:T(8,128)(2,1)S(1)} %all_to_all.31.mine_ref), channel_id=1, source_target_pairs={{0,32},{32,0},{1,33},{33,1},{2,34},{34,2},{3,35},{35,3},{4,36},{36... | collective-permute-start | bytes 2359304 | tf_op jit(solution)/shard_map/ppermute | solution.py:320
  125.0 19.1 %copy-start.3 = (bf16[32,32,384]{2,1,0:T(8,128)(2,1)}, bf16[32,32,384]{2,1,0:T(8,128)(2,1)S(1)}, u32[]{:S(2)}) copy-start(bf16[32,32,384]{2,1,0:T(8,128)(2,1)S(1)} %get-tuple-element.13) | copy-start | bytes 2359300
  144.1 18.4 %all-to-all-start.4 = ((bf16[32,32,384]{2,1,0:T(8,128)(2,1)}), bf16[32,32,384]{2,1,0:T(8,128)(2,1)S(1)}, u32[]{:S(2)}, u32[]{:S(2)}) async-start(bf16[32,32,384]{2,1,0:T(8,128)(2,1)} %copy-done.3), calls=%async_computation.4 | async-start | bytes 1572864 | tf_op jit(solution)/shard_map/all_to_all | solution.py:308
  151.0 26.6 %collective-permute-start.4 = (bf16[2,16,5120]{2,1,0:T(8,128)(2,1)S(1)}, bf16[2,16,5120]{2,1,0:T(8,128)(2,1)S(1)}, u32[]{:S(2)}, u32[]{:S(2)}) collective-permute-start(bf16[2,16,5120]{2,1,0:T(8,128)(2,1)S(1)} %unpack_other.1), channel_id=1, source_target_pairs={{0,2},{2,0},{1,3},{3,1},{4,6},{6,4},{5,7},{7,5},{8,10},{10,8},{9,1... | collective-permute-start | bytes 983048 | tf_op jit(solution)/shard_map/ppermute | solution.py:320
Sparse Core Ops, SparseCore 0:
  10.6 66.3 all-gather.1
  121.4 65.8 reduce-scatter.1

commit v8 on v7

--- a/solution.py
+++ b/solution.py
@@ -101,26 +101,21 @@
 
 
 def first_kernel(expert_ref, half_ref, x_ref, weight_ref, out_ref):
+    rows = pl.ds(pl.multiple_of(half_ref[0] * H, H), H)
     for i in range(Z // 2):
         e = expert_ref[Z // 2 * pl.program_id(0) + i]
         both = jnp.concatenate([weight_ref[i, 0], weight_ref[i, 1]], axis=1)
-        out_ref[i, :, 0 : 2 * S] = dot(x_ref[0, e], both).astype(out_ref.dtype)
-        out_ref[i, :, 2 * S : 3 * S] = dot(x_ref[1, e], weight_ref[i, 2]).astype(out_ref.dtype)
+        out_ref[i, :, 0 : 2 * S] = dot(x_ref[0, e, rows, :], both).astype(out_ref.dtype)
+        out_ref[i, :, 2 * S : 3 * S] = dot(x_ref[1, e, rows, :], weight_ref[i, 2]).astype(out_ref.dtype)
 
 
 def first(expert, half, x, weight, dtype):
     return pl.pallas_call(
         first_kernel,
         out_shape=jax.ShapeDtypeStruct((Z, H, 3 * S), dtype),
-        grid_spec=pltpu.PrefetchScalarGridSpec(
-            num_scalar_prefetch=2,
-            grid=(2,),
-            in_specs=[
-                pl.BlockSpec((2, E, H, W), lambda i, expert, half: (0, 0, half[0], 0)),
-                pl.BlockSpec((Z // 2, 3, W, S), lambda i, expert, half: (i, 0, 0, 0)),
-            ],
-            out_specs=pl.BlockSpec((Z // 2, H, 3 * S), lambda i, expert, half: (i, 0, 0)),
-        ),
+        grid=(2,),
+        in_specs=[SMEM, SMEM, VMEM, pl.BlockSpec((Z // 2, 3, W, S), lambda i: (i, 0, 0, 0))],
+        out_specs=pl.BlockSpec((Z // 2, H, 3 * S), lambda i: (i, 0, 0)),
         compiler_params=pltpu.CompilerParams(vmem_limit_bytes=LIMIT),
         name="first",
     )(expert, half, x, weight)
@@ -178,24 +173,27 @@
     return jnp.concatenate([jnp.where(low, mine, other), jnp.where(low, other, mine)], axis=0)
 
 
-def weigh_kernel(expert_ref, core_ref, xt_ref, mine_ref, other_ref, out_ref):
-    for i in range(Z // 2):
-        e = expert_ref[Z // 2 * pl.program_id(0) + i]
-        act = in_order(core_ref[0], mine_ref[i], other_ref[i])
+def weigh_kernel(expert_ref, core_ref, xt_ref, mine_ref, other_ref, out_ref, held_ref, sems):
+    copies = [pltpu.make_async_copy(held_ref.at[z], out_ref.at[z], sems.at[z]) for z in range(Z)]
+    for z in range(Z):
+        e = expert_ref[z]
+        act = in_order(core_ref[0], mine_ref[z], other_ref[z])
         both = dot(xt_ref[0, e], act[:, S : 3 * S])
-        out_ref[i, 0] = both[:, 0:S].astype(BF)
-        out_ref[i, 1] = both[:, S : 2 * S].astype(BF)
-        out_ref[i, 2] = dot(xt_ref[1, e], act[:, 0:S]).astype(BF)
+        held_ref[z, 0] = both[:, 0:S].astype(BF)
+        held_ref[z, 1] = both[:, S : 2 * S].astype(BF)
+        held_ref[z, 2] = dot(xt_ref[1, e], act[:, 0:S]).astype(BF)
+        copies[z].start()
+    for copy in copies:
+        copy.wait()
 
 
 def weigh(expert, core, xt, mine, other):
-    rows = pl.BlockSpec((Z // 2, H, 3 * S), lambda i: (i, 0, 0))
     return pl.pallas_call(
         weigh_kernel,
-        grid=(2,),
         out_shape=pltpu.HBM((Z, 3, W, S), BF),
-        in_specs=[SMEM, SMEM, pl.BlockSpec((2, E, W, R), lambda i: (0, 0, 0, 0)), rows, rows],
-        out_specs=pl.BlockSpec((Z // 2, 3, W, S), lambda i: (i, 0, 0, 0)),
+        in_specs=[SMEM, SMEM, VMEM, VMEM, VMEM],
+        out_specs=pl.BlockSpec(memory_space=pl.ANY),
+        scratch_shapes=[pltpu.VMEM((Z, 3, W, S), BF), pltpu.SemaphoreType.DMA((Z,))],
         compiler_params=pltpu.CompilerParams(vmem_limit_bytes=LIMIT),
         name="weigh",
     )(expert, core, xt, mine, other)

time: 197 us -> 196 us (level)
  the two profiles are of different devices: /device:TPU:44 before, /device:TPU:1 now
where the time goes in v8:
time: 196 us; the launch traced here: 195 us
  waiting for transfers between devices  69.5 us (35%)
  blocking collectives  50.2 us (26%)
  starting transfers between devices  36.2 us (18%)
  Pallas kernels  18.1 us (9%)
  between operations  14.2 us (7%)
  other arithmetic  3.46 us (2%)
  local copies, waits for them, and re-layouts  3.27 us (2%)
    all_to_all x3, blocking collectives, exchange(): return lax.all_to_all(x, axes, split_axis=0, concat_axis=0, tiled=True)  50.2 us
    all_to_all x3, waiting for transfers between devices, exchange(): return lax.all_to_all(x, axes, split_axis=0, concat_axis=0, tiled=True)  35.6 us
    all_to_all x3, starting transfers between devices, exchange(): return lax.all_to_all(x, axes, split_axis=0, concat_axis=0, tiled=True)  18.1 us
    ppermute x5, starting transfers between devices, swap(): return [lax.ppermute(x, axis, ((0, 1), (1, 0))) for x in xs]  18 us
    ppermute x5, waiting for transfers between devices, swap(): return [lax.ppermute(x, axis, ((0, 1), (1, 0))) for x in xs]  14.2 us
    all_gather x1, waiting for transfers between devices, gather(): return lax.all_gather(x, 'z_hi', axis=0, tiled=True)  12.2 us
    reduce_scatter x1, waiting for transfers between devices, scatter(): return lax.psum_scatter(x, 'z_hi', scatter_dimension=0, tiled=True)  7.45 us
    pallas_call x2, Pallas kernels, pack(): pl.pallas_call(pack_kernel, out_shape=jax.ShapeDtypeStruct((Y * G, 2 * G,...  4.49 us
  transfers between devices with their start and end apart: 10, of which 8 were waited for; matrix products, arithmetic and copies ran while one was open for 2% of the time, Pallas kernels for 6%

profile of v8, /device:TPU:1, one launch (start us, length us, event | category | flops | bytes accessed | tf_op | source)
XLA Modules:
  0.0 194.9 jit_solution(10832169075945514836)
XLA Ops:
  7.2 0.0 all-gather.2.cloned.1.call-start
  7.2 1.7 pad_maximum_fusion.1
  8.9 0.0 all-gather.2.cloned.1.call-update
  8.9 1.0 pad_maximum_fusion
  9.9 4.4 %collective-permute-start.1 = (bf16[2,16,5120]{2,1,0:T(8,128)(2,1)S(1)}, bf16[2,16,5120]{2,1,0:T(8,128)(2,1)S(1)}, u32[]{:S(2)}, u32[]{:S(2)}) collective-permute-start(bf16[2,16,5120]{2,1,0:T(8,128)(2,1)S(1)} %pad_maximum_fusion), channel_id=1, source_target_pairs={{0,2},{2,0},{1,3},{3,1},{4,6},{6,4},{5,7},{7,5},{8,10},{10,8},{9,1... | collective-permute-start | bytes 983048 | tf_op jit(solution)/shard_map/ppermute | solution.py:318
  14.3 0.7 add_bitcast_fusion
  15.1 1.9 collective-permute-start
  17.0 2.3 %pack.2 = bf16[32,32,384]{2,1,0:T(8,128)(2,1)} custom-call(s32[1]{0:T(128)} %bitcast.2.me_ref, s32[4]{0:T(128)} %bitcast.22, s32[1,16]{1,0:T(1,128)} %bitcast.24, bf16[16,5120]{1,0:T(8,128)(2,1)} %bitcast.18, bf16[16,5120]{1,0:T(8,128)(2,1)} %bitcast.19), custom_call_target="tpu_custom_call" | custom-call | tf_op jit(solution)/shard_map/pack/pallas_call | solution.py:62
  19.2 10.0 %all-to-all-start = ((bf16[32,32,384]{2,1,0:T(8,128)(2,1)}), bf16[32,32,384]{2,1,0:T(8,128)(2,1)S(1)}, u32[]{:S(2)}, u32[]{:S(2)}) async-start(bf16[32,32,384]{2,1,0:T(8,128)(2,1)} %pack.2), calls=%async_computation | async-start | bytes 1572864 | tf_op jit(solution)/shard_map/all_to_all | solution.py:306
  29.2 0.0 collective-permute-done
  29.2 0.6 slice.13.dest_ref
  29.8 0.6 slice_bitcast_fusion.2.counts_ref
  30.4 0.0 copy-start.4
  30.4 0.0 collective-permute-done.1
  30.4 0.7 slice_bitcast_fusion
  31.2 2.2 %pack.3 = bf16[32,32,384]{2,1,0:T(8,128)(2,1)} custom-call(s32[1]{0:T(128)} %bitcast.2.me_ref, s32[4]{0:T(128)} %slice_bitcast_fusion.2.counts_ref, s32[1,16]{1,0:T(1,128)} %slice.13.dest_ref, bf16[16,5120]{1,0:T(8,128)(2,1)} %get-tuple-element.21.tok_ref, bf16[16,5120]{1,0:T(8,128)(2,1)} %get-tuple-element.20.cot_ref), custom_call_target="tpu_custom_call" | custom-call | tf_op jit(solution)/shard_map/pack/pallas_call | solution.py:62
  33.4 10.2 %all-to-all-done.own_ref = bf16[32,32,384]{2,1,0:T(8,128)(2,1)S(1)} async-done(((bf16[32,32,384]{2,1,0:T(8,128)(2,1)}), bf16[32,32,384]{2,1,0:T(8,128)(2,1)S(1)}, u32[]{:S(2)}, u32[]{:S(2)}) %all-to-all-start) | async-done | bytes 786464 | tf_op jit(solution)/shard_map/all_to_all | solution.py:306
  43.6 4.1 %all-to-all-start.1 = ((bf16[32,32,384]{2,1,0:T(8,128)(2,1)}), bf16[32,32,384]{2,1,0:T(8,128)(2,1)S(1)}, u32[]{:S(2)}, u32[]{:S(2)}) async-start(bf16[32,32,384]{2,1,0:T(8,128)(2,1)} %pack.3), calls=%async_computation.1 | async-start | bytes 1572864 | tf_op jit(solution)/shard_map/all_to_all | solution.py:306
  47.7 0.0 reduce-scatter.2.cloned.1.call-start
  47.7 0.0 copy-done.4
  47.7 0.1 reshape.17
  47.8 0.2 dynamic-slice_reduce_fusion
  48.0 14.0 %all-to-all-done.1.other_ref = bf16[32,32,384]{2,1,0:T(8,128)(2,1)S(1)} async-done(((bf16[32,32,384]{2,1,0:T(8,128)(2,1)}), bf16[32,32,384]{2,1,0:T(8,128)(2,1)S(1)}, u32[]{:S(2)}, u32[]{:S(2)}) %all-to-all-start.1) | async-done | bytes 786464 | tf_op jit(solution)/shard_map/all_to_all | solution.py:306
  62.0 0.8 prepare.1
  62.9 0.0 copy-start.1
  62.9 1.1 copy-done.1
  63.9 12.2 %all-gather.2.cloned.1.call-done.weight_ref = bf16[8,3,320,128]{3,2,1,0:T(8,128)(2,1)} async-done(((bf16[1,3,320,128]{3,2,1,0:T(8,128)(2,1)}), bf16[8,3,320,128]{3,2,1,0:T(8,128)(2,1)}) %all-gather.2.cloned.1.call-update) | async-done | bytes 1966096 | tf_op jit(solution)/shard_map/all_gather | solution.py:310
  76.1 0.0 copy-start
  76.1 2.2 %first.3 = bf16[8,128,384]{2,1,0:T(8,128)(2,1)S(1)} custom-call(s32[8]{0:T(128)S(1)} %and_select_fusion.expert_ref, s32[1]{0:T(128)S(6)} %sub.8.half_ref, bf16[2,4,256,320]{3,2,1,0:T(8,128)(2,1)S(1)} %get-tuple-element.12.x_ref, bf16[8,3,320,128]{3,2,1,0:T(8,128)(2,1)} %all-gather.2.cloned.1.call-done.weight_ref), custom_call_target="tpu_custom_call" | custom-call | tf_op jit(solution)/shard_map/first/pallas_call | solution.py:113
  78.3 5.0 %collective-permute-start.2 = (bf16[8,128,384]{2,1,0:T(8,128)(2,1)S(1)}, bf16[8,128,384]{2,1,0:T(8,128)(2,1)S(1)}, u32[]{:S(2)}, u32[]{:S(2)}) collective-permute-start(bf16[8,128,384]{2,1,0:T(8,128)(2,1)S(1)} %first.3), channel_id=1, source_target_pairs={{0,32},{32,0},{1,33},{33,1},{2,34},{34,2},{3,35},{35,3},{4,36},{36... | collective-permute-start | bytes 2359304 | tf_op jit(solution)/shard_map/ppermute | solution.py:318
  83.3 0.0 copy-done
  83.3 1.4 first.2.keep_ref
  84.7 0.5 collective-permute-done.2.got_ref
  85.2 0.1 add_cores.1
  85.3 17.2 %all_to_all.30.part_ref = bf16[8,128,384]{2,1,0:T(8,128)(2,1)S(1)} all-to-all(bf16[8,128,384]{2,1,0:T(8,128)(2,1)S(1)} %add_cores.1), channel_id=1, replica_groups=mesh['y_lo'=2,'x'=4,'core'=2,'z_hi'=8,'z_lo'=2,'y_hi'=2] {'y_lo','x'}, dimensions={0} | all-to-all | bytes 1572864 | tf_op jit(solution)/shard_map/all_to_all | solution.py:306
  102.5 0.0 copy-start.2
  102.5 0.4 middle.1
  102.9 14.2 %all_to_all.31.mine_ref = bf16[8,128,384]{2,1,0:T(8,128)(2,1)S(1)} all-to-all(bf16[8,128,384]{2,1,0:T(8,128)(2,1)S(1)} %middle.1), channel_id=1, replica_groups=mesh['y_lo'=2,'x'=4,'core'=2,'z_hi'=8,'z_lo'=2,'y_hi'=2] {'y_lo','x'}, dimensions={0} | all-to-all | bytes 1572864 | tf_op jit(solution)/shard_map/all_to_all | solution.py:306
  117.1 4.0 %collective-permute-start.3 = (bf16[8,128,384]{2,1,0:T(8,128)(2,1)S(1)}, bf16[8,128,384]{2,1,0:T(8,128)(2,1)S(1)}, u32[]{:S(2)}, u32[]{:S(2)}) collective-permute-start(bf16[8,128,384]{2,1,0:T(8,128)(2,1)S(1)} %all_to_all.31.mine_ref), channel_id=1, source_target_pairs={{0,32},{32,0},{1,33},{33,1},{2,34},{34,2},{3,35},{35,3},{4,36},{36... | collective-permute-start | bytes 2359304 | tf_op jit(solution)/shard_map/ppermute | solution.py:318
  121.1 1.9 collective-permute-done.3.far_ref.other_ref
  123.0 0.0 copy-done.2
  123.0 2.2 %weigh.1 = bf16[8,3,320,128]{3,2,1,0:T(8,128)(2,1)} custom-call(s32[8]{0:T(128)S(1)} %and_select_fusion.expert_ref, s32[1]{0:T(128)} %bitcast.half_ref.core_ref, bf16[2,4,320,256]{3,2,1,0:T(8,128)(2,1)S(1)} %copy-done.2, bf16[8,128,384]{2,1,0:T(8,128)(2,1)S(1)} %all_to_all.31.mine_ref, bf16[8,128,384]{2,1,0:T(8,128)(2,1)S(1)} %collective-permute-done.3.far_ref.other_ref), custom_call_target="tpu_custom_call" | custom-call | tf_op jit(solution)/shard_map/weigh/pallas_call | solution.py:191
  125.2 0.0 reduce-scatter.2.cloned.1.call-update
  125.2 3.7 %last.1 = (bf16[32,32,384]{2,1,0:T(8,128)(2,1)S(1)}, bf16[32,32,384]{2,1,0:T(8,128)(2,1)S(1)}) custom-call(s32[8]{0:T(128)S(1)} %and_select_fusion.expert_ref, s32[1]{0:T(128)} %bitcast.half_ref.core_ref, bf16[8,3,320,128]{3,2,1,0:T(8,128)(2,1)S(1)} %copy-done, bf16[8,128,384]{2,1,0:T(8,128)(2,1)S(1)} %all_to_all.31.mine_ref, ...), custom_call_target="tpu_custom_call" | custom-call | tf_op jit(solution)/shard_map/last/pallas_call | solution.py:232
  128.9 0.0 copy-start.3
  128.9 18.8 %all_to_all.32.recv_ref = bf16[32,32,384]{2,1,0:T(8,128)(2,1)S(1)} all-to-all(bf16[32,32,384]{2,1,0:T(8,128)(2,1)S(1)} %get-tuple-element.14), channel_id=1, replica_groups=mesh['y_lo'=2,'x'=4,'core'=2,'z_hi'=8,'z_lo'=2,'y_hi'=2] {'y_hi','y_lo',..., dimensions={0} | all-to-all | bytes 1572864 | tf_op jit(solution)/shard_map/all_to_all | solution.py:306
  147.8 0.0 copy-done.3
  147.8 4.1 %all-to-all-start.4 = ((bf16[32,32,384]{2,1,0:T(8,128)(2,1)}), bf16[32,32,384]{2,1,0:T(8,128)(2,1)S(1)}, u32[]{:S(2)}, u32[]{:S(2)}) async-start(bf16[32,32,384]{2,1,0:T(8,128)(2,1)} %copy-done.3), calls=%async_computation.4 | async-start | bytes 1572864 | tf_op jit(solution)/shard_map/all_to_all | solution.py:306
  151.8 0.1 unpack_other.1
  152.0 2.7 %collective-permute-start.4 = (bf16[2,16,5120]{2,1,0:T(8,128)(2,1)S(1)}, bf16[2,16,5120]{2,1,0:T(8,128)(2,1)S(1)}, u32[]{:S(2)}, u32[]{:S(2)}) collective-permute-start(bf16[2,16,5120]{2,1,0:T(8,128)(2,1)S(1)} %unpack_other.1), channel_id=1, source_target_pairs={{0,2},{2,0},{1,3},{3,1},{4,6},{6,4},{5,7},{7,5},{8,10},{10,8},{9,1... | collective-permute-start | bytes 983048 | tf_op jit(solution)/shard_map/ppermute | solution.py:318
  154.7 11.5 %all-to-all-done.4.recv_ref = bf16[32,32,384]{2,1,0:T(8,128)(2,1)S(1)} async-done(((bf16[32,32,384]{2,1,0:T(8,128)(2,1)}), bf16[32,32,384]{2,1,0:T(8,128)(2,1)S(1)}, u32[]{:S(2)}, u32[]{:S(2)}) %all-to-all-start.4) | async-done | bytes 786464 | tf_op jit(solution)/shard_map/all_to_all | solution.py:306
  166.2 11.8 %collective-permute-done.4.add_ref = bf16[2,16,5120]{2,1,0:T(8,128)(2,1)S(1)} collective-permute-done((bf16[2,16,5120]{2,1,0:T(8,128)(2,1)S(1)}, bf16[2,16,5120]{2,1,0:T(8,128)(2,1)S(1)}, u32[]{:S(2)}, u32[]{:S(2)}) %collective-permute-start.4) | collective-permute-done | bytes 327712 | tf_op jit(solution)/shard_map/ppermute | solution.py:318
  178.0 0.9 unpack_own.1
  178.9 7.4 %reduce-scatter.2.cloned.1.call-done.own_ref = bf16[1,3,320,128]{3,2,1,0:T(8,128)(2,1)} async-done(((bf16[8,3,320,128]{3,2,1,0:T(8,128)(2,1)}), bf16[1,3,320,128]{3,2,1,0:T(8,128)(2,1)}) %reduce-scatter.2.cloned.1.call-update) | async-done | bytes 245776 | tf_op jit(solution)/shard_map/reduce_scatter | solution.py:314
  186.3 1.7 widen.1
  (1 shorter events, 0.0 us)
Async XLA Ops:
  7.2 68.9 %all-gather.2.cloned.1.call-start = ((), (), s32[]{:S(2)}) async-start(), calls=%async_computation.7 | async-start | bytes 2211840 | tf_op jit(solution)/shard_map/all_gather | solution.py:310
  9.9 20.5 %collective-permute-start.1 = (bf16[2,16,5120]{2,1,0:T(8,128)(2,1)S(1)}, bf16[2,16,5120]{2,1,0:T(8,128)(2,1)S(1)}, u32[]{:S(2)}, u32[]{:S(2)}) collective-permute-start(bf16[2,16,5120]{2,1,0:T(8,128)(2,1)S(1)} %pad_maximum_fusion), channel_id=1, source_target_pairs={{0,2},{2,0},{1,3},{3,1},{4,6},{6,4},{5,7},{7,5},{8,10},{10,8},{9,1... | collective-permute-start | bytes 983048 | tf_op jit(solution)/shard_map/ppermute | solution.py:318
  15.1 14.2 %collective-permute-start = (s32[1,20]{1,0:T(1,128)S(1)}, s32[1,20]{1,0:T(1,128)S(1)}, u32[]{:S(2)}, u32[]{:S(2)}) collective-permute-start(s32[1,20]{1,0:T(1,128)S(1)} %add_bitcast_fusion), channel_id=1, source_target_pairs={{0,2},{2,0},{1,3},{3,1},{4,6},{6,4},{5,7},{7,5},{8,10},{10,8},{9,1... | collective-permute-start | bytes 248 | tf_op jit(solution)/shard_map/ppermute | solution.py:318
  19.2 24.3 %all-to-all-start = ((bf16[32,32,384]{2,1,0:T(8,128)(2,1)}), bf16[32,32,384]{2,1,0:T(8,128)(2,1)S(1)}, u32[]{:S(2)}, u32[]{:S(2)}) async-start(bf16[32,32,384]{2,1,0:T(8,128)(2,1)} %pack.2), calls=%async_computation | async-start | bytes 1572864 | tf_op jit(solution)/shard_map/all_to_all | solution.py:306
  30.4 17.3 %copy-start.4 = (s32[32]{0:T(128)S(1)}, s32[32]{0:T(128)}, u32[]{:S(2)}) copy-start(s32[32]{0:T(128)} %param.11) | copy-start | bytes 388
  43.6 18.4 %all-to-all-start.1 = ((bf16[32,32,384]{2,1,0:T(8,128)(2,1)}), bf16[32,32,384]{2,1,0:T(8,128)(2,1)S(1)}, u32[]{:S(2)}, u32[]{:S(2)}) async-start(bf16[32,32,384]{2,1,0:T(8,128)(2,1)} %pack.3), calls=%async_computation.1 | async-start | bytes 1572864 | tf_op jit(solution)/shard_map/all_to_all | solution.py:306
  47.7 138.7 %reduce-scatter.2.cloned.1.call-start = ((), (), s32[]{:S(2)}) async-start(), calls=%async_computation.8 | async-start | bytes 2211840 | tf_op jit(solution)/shard_map/reduce_scatter | solution.py:314
  62.9 1.1 copy-start.1
  76.1 7.2 %copy-start = (bf16[8,3,320,128]{3,2,1,0:T(8,128)(2,1)S(1)}, bf16[8,3,320,128]{3,2,1,0:T(8,128)(2,1)}, u32[]{:S(2)}) copy-start(bf16[8,3,320,128]{3,2,1,0:T(8,128)(2,1)} %all-gather.2.cloned.1.call-done.weight_ref) | copy-start | bytes 5898244
  78.3 6.9 %collective-permute-start.2 = (bf16[8,128,384]{2,1,0:T(8,128)(2,1)S(1)}, bf16[8,128,384]{2,1,0:T(8,128)(2,1)S(1)}, u32[]{:S(2)}, u32[]{:S(2)}) collective-permute-start(bf16[8,128,384]{2,1,0:T(8,128)(2,1)S(1)} %first.3), channel_id=1, source_target_pairs={{0,32},{32,0},{1,33},{33,1},{2,34},{34,2},{3,35},{35,3},{4,36},{36... | collective-permute-start | bytes 2359304 | tf_op jit(solution)/shard_map/ppermute | solution.py:318
  102.5 20.5 %copy-start.2 = (bf16[2,4,320,256]{3,2,1,0:T(8,128)(2,1)S(1)}, bf16[2,4,320,256]{3,2,1,0:T(8,128)(2,1)}, u32[]{:S(2)}) copy-start(bf16[2,4,320,256]{3,2,1,0:T(8,128)(2,1)} %copy-done.1) | copy-start | bytes 3932164
  117.1 5.9 %collective-permute-start.3 = (bf16[8,128,384]{2,1,0:T(8,128)(2,1)S(1)}, bf16[8,128,384]{2,1,0:T(8,128)(2,1)S(1)}, u32[]{:S(2)}, u32[]{:S(2)}) collective-permute-start(bf16[8,128,384]{2,1,0:T(8,128)(2,1)S(1)} %all_to_all.31.mine_ref), channel_id=1, source_target_pairs={{0,32},{32,0},{1,33},{33,1},{2,34},{34,2},{3,35},{35,3},{4,36},{36... | collective-permute-start | bytes 2359304 | tf_op jit(solution)/shard_map/ppermute | solution.py:318
  128.9 18.8 %copy-start.3 = (bf16[32,32,384]{2,1,0:T(8,128)(2,1)}, bf16[32,32,384]{2,1,0:T(8,128)(2,1)S(1)}, u32[]{:S(2)}) copy-start(bf16[32,32,384]{2,1,0:T(8,128)(2,1)S(1)} %get-tuple-element.13) | copy-start | bytes 2359300
  147.8 18.4 %all-to-all-start.4 = ((bf16[32,32,384]{2,1,0:T(8,128)(2,1)}), bf16[32,32,384]{2,1,0:T(8,128)(2,1)S(1)}, u32[]{:S(2)}, u32[]{:S(2)}) async-start(bf16[32,32,384]{2,1,0:T(8,128)(2,1)} %copy-done.3), calls=%async_computation.4 | async-start | bytes 1572864 | tf_op jit(solution)/shard_map/all_to_all | solution.py:306
  152.0 26.0 %collective-permute-start.4 = (bf16[2,16,5120]{2,1,0:T(8,128)(2,1)S(1)}, bf16[2,16,5120]{2,1,0:T(8,128)(2,1)S(1)}, u32[]{:S(2)}, u32[]{:S(2)}) collective-permute-start(bf16[2,16,5120]{2,1,0:T(8,128)(2,1)S(1)} %unpack_other.1), channel_id=1, source_target_pairs={{0,2},{2,0},{1,3},{3,1},{4,6},{6,4},{5,7},{7,5},{8,10},{10,8},{9,1... | collective-permute-start | bytes 983048 | tf_op jit(solution)/shard_map/ppermute | solution.py:318
Sparse Core Ops, SparseCore 0:
  10.6 65.4 all-gather.1
  125.3 60.9 reduce-scatter.1

commit v9 on v8

--- a/solution.py
+++ b/solution.py
@@ -307,11 +307,12 @@
 
 
 def gather(x):
-    return lax.all_gather(x, "z_hi", axis=0, tiled=True)
+    return lax.all_gather(x.reshape(3 * W, S), "z_hi", axis=0, tiled=True).reshape(Z, 3, W, S)
 
 
 def scatter(x):
-    return lax.psum_scatter(x, "z_hi", scatter_dimension=0, tiled=True)
+    flat = x.reshape(Z * 3 * W, S)
+    return lax.psum_scatter(flat, "z_hi", scatter_dimension=0, tiled=True).reshape(1, 3, W, S)
 
 
 def swap(*xs, axis="z_lo"):

time: 196 us -> 195 us (level)
  the two profiles are of different devices: /device:TPU:1 before, /device:TPU:48 now
where the time goes in v9:
time: 195 us
  waiting for transfers between devices  71 us (36%)
  blocking collectives  50.8 us (26%)
  starting transfers between devices  33.8 us (17%)
  Pallas kernels  18.1 us (9%)
  between operations  14.2 us (7%)
  other arithmetic  3.46 us (2%)
  local copies, waits for them, and re-layouts  3.27 us (2%)
    all_to_all x3, blocking collectives, exchange(): return lax.all_to_all(x, axes, split_axis=0, concat_axis=0, tiled=True)  50.8 us
    all_to_all x3, waiting for transfers between devices, exchange(): return lax.all_to_all(x, axes, split_axis=0, concat_axis=0, tiled=True)  27.4 us
    all_to_all x3, starting transfers between devices, exchange(): return lax.all_to_all(x, axes, split_axis=0, concat_axis=0, tiled=True)  20.5 us
    ppermute x5, waiting for transfers between devices, swap(): return [lax.ppermute(x, axis, ((0, 1), (1, 0))) for x in xs]  18.7 us
    all_gather x1, waiting for transfers between devices, gather(): lax.all_gather(x.reshape(3 * W, S), 'z_hi', axis=0, tiled=True)  16.9 us
    ppermute x5, starting transfers between devices, swap(): return [lax.ppermute(x, axis, ((0, 1), (1, 0))) for x in xs]  13.2 us
    reduce_scatter x1, waiting for transfers between devices, scatter(): lax.psum_scatter(flat, 'z_hi', scatter_dimension=0, tiled=True)  7.94 us
    pallas_call x2, Pallas kernels, pack(): pl.pallas_call(pack_kernel, out_shape=jax.ShapeDtypeStruct((Y * G, 2 * G,...  4.49 us
  transfers between devices with their start and end apart: 10, of which 8 were waited for; matrix products, arithmetic and copies ran while one was open for 2% of the time, Pallas kernels for 6%

profile of v9, /device:TPU:48, one launch (start us, length us, event | category | flops | bytes accessed | tf_op | source)
XLA Modules:
  0.0 194.7 jit_solution(14655717858472533730)
XLA Ops:
  7.2 0.0 all-gather.2.cloned.1.call-start
  7.2 1.7 pad_maximum_fusion.1
  8.9 0.0 all-gather.2.cloned.1.call-update
  8.9 1.0 pad_maximum_fusion
  9.9 2.0 %collective-permute-start.1 = (bf16[2,16,5120]{2,1,0:T(8,128)(2,1)S(1)}, bf16[2,16,5120]{2,1,0:T(8,128)(2,1)S(1)}, u32[]{:S(2)}, u32[]{:S(2)}) collective-permute-start(bf16[2,16,5120]{2,1,0:T(8,128)(2,1)S(1)} %pad_maximum_fusion), channel_id=1, source_target_pairs={{0,2},{2,0},{1,3},{3,1},{4,6},{6,4},{5,7},{7,5},{8,10},{10,8},{9,1... | collective-permute-start | bytes 983048 | tf_op jit(solution)/shard_map/ppermute | solution.py:319
  12.0 0.7 add_bitcast_fusion
  12.7 3.8 %collective-permute-start = (s32[1,20]{1,0:T(1,128)S(1)}, s32[1,20]{1,0:T(1,128)S(1)}, u32[]{:S(2)}, u32[]{:S(2)}) collective-permute-start(s32[1,20]{1,0:T(1,128)S(1)} %add_bitcast_fusion), channel_id=1, source_target_pairs={{0,2},{2,0},{1,3},{3,1},{4,6},{6,4},{5,7},{7,5},{8,10},{10,8},{9,1... | collective-permute-start | bytes 248 | tf_op jit(solution)/shard_map/ppermute | solution.py:319
  16.5 2.3 %pack.2 = bf16[32,32,384]{2,1,0:T(8,128)(2,1)} custom-call(s32[1]{0:T(128)} %bitcast.4.me_ref, s32[4]{0:T(128)} %bitcast.32, s32[1,16]{1,0:T(1,128)} %bitcast.34, bf16[16,5120]{1,0:T(8,128)(2,1)} %bitcast.27, bf16[16,5120]{1,0:T(8,128)(2,1)} %bitcast.28), custom_call_target="tpu_custom_call" | custom-call | tf_op jit(solution)/shard_map/pack/pallas_call | solution.py:62
  18.8 7.4 %all-to-all-start = ((bf16[32,32,384]{2,1,0:T(8,128)(2,1)}), bf16[32,32,384]{2,1,0:T(8,128)(2,1)S(1)}, u32[]{:S(2)}, u32[]{:S(2)}) async-start(bf16[32,32,384]{2,1,0:T(8,128)(2,1)} %pack.2), calls=%async_computation | async-start | bytes 1572864 | tf_op jit(solution)/shard_map/all_to_all | solution.py:306
  26.3 0.0 collective-permute-done
  26.3 0.6 slice.13.dest_ref
  26.9 0.6 slice_bitcast_fusion.2.counts_ref
  27.5 0.0 copy-start.4
  27.5 0.0 collective-permute-done.1
  27.5 0.7 slice_bitcast_fusion
  28.2 2.2 %pack.3 = bf16[32,32,384]{2,1,0:T(8,128)(2,1)} custom-call(s32[1]{0:T(128)} %bitcast.4.me_ref, s32[4]{0:T(128)} %slice_bitcast_fusion.2.counts_ref, s32[1,16]{1,0:T(1,128)} %slice.13.dest_ref, bf16[16,5120]{1,0:T(8,128)(2,1)} %get-tuple-element.21.tok_ref, bf16[16,5120]{1,0:T(8,128)(2,1)} %get-tuple-element.20.cot_ref), custom_call_target="tpu_custom_call" | custom-call | tf_op jit(solution)/shard_map/pack/pallas_call | solution.py:62
  30.4 7.7 %all-to-all-done.own_ref = bf16[32,32,384]{2,1,0:T(8,128)(2,1)S(1)} async-done(((bf16[32,32,384]{2,1,0:T(8,128)(2,1)}), bf16[32,32,384]{2,1,0:T(8,128)(2,1)S(1)}, u32[]{:S(2)}, u32[]{:S(2)}) %all-to-all-start) | async-done | bytes 786464 | tf_op jit(solution)/shard_map/all_to_all | solution.py:306
  38.1 6.6 %all-to-all-start.1 = ((bf16[32,32,384]{2,1,0:T(8,128)(2,1)}), bf16[32,32,384]{2,1,0:T(8,128)(2,1)S(1)}, u32[]{:S(2)}, u32[]{:S(2)}) async-start(bf16[32,32,384]{2,1,0:T(8,128)(2,1)} %pack.3), calls=%async_computation.1 | async-start | bytes 1572864 | tf_op jit(solution)/shard_map/all_to_all | solution.py:306
  44.7 0.0 reduce-scatter.2.cloned.1.call-start
  44.7 0.0 copy-done.4
  44.8 0.1 reshape.29
  44.8 0.2 dynamic-slice_reduce_fusion
  45.0 11.5 %all-to-all-done.1.other_ref = bf16[32,32,384]{2,1,0:T(8,128)(2,1)S(1)} async-done(((bf16[32,32,384]{2,1,0:T(8,128)(2,1)}), bf16[32,32,384]{2,1,0:T(8,128)(2,1)S(1)}, u32[]{:S(2)}, u32[]{:S(2)}) %all-to-all-start.1) | async-done | bytes 786464 | tf_op jit(solution)/shard_map/all_to_all | solution.py:306
  56.6 0.9 prepare.1
  57.4 0.0 copy-start.1
  57.4 1.1 copy-done.1
  58.5 16.9 %all-gather.2.cloned.1.call-done = bf16[7680,128]{1,0:T(8,128)(2,1)} async-done(((bf16[960,128]{1,0:T(8,128)(2,1)}), bf16[7680,128]{1,0:T(8,128)(2,1)}) %all-gather.2.cloned.1.call-update) | async-done | bytes 1966096 | tf_op jit(solution)/shard_map/all_gather | solution.py:310
  75.3 0.0 copy-start
  75.3 2.2 %first.3 = bf16[8,128,384]{2,1,0:T(8,128)(2,1)S(1)} custom-call(s32[8]{0:T(128)S(1)} %and_select_fusion.expert_ref, s32[1]{0:T(128)S(6)} %sub.8.half_ref, bf16[2,4,256,320]{3,2,1,0:T(8,128)(2,1)S(1)} %get-tuple-element.12.x_ref, bf16[8,3,320,128]{3,2,1,0:T(8,128)(2,1)} %bitcast.22), custom_call_target="tpu_custom_call" | custom-call | tf_op jit(solution)/shard_map/first/pallas_call | solution.py:113
  77.5 1.9 collective-permute-start.2
  79.5 0.0 copy-done
  79.5 1.4 first.2.keep_ref
  80.9 0.8 collective-permute-done.2.got_ref
  81.7 0.1 add_cores.1
  81.9 18.6 %all_to_all.30.part_ref = bf16[8,128,384]{2,1,0:T(8,128)(2,1)S(1)} all-to-all(bf16[8,128,384]{2,1,0:T(8,128)(2,1)S(1)} %add_cores.1), channel_id=1, replica_groups=mesh['y_lo'=2,'x'=4,'core'=2,'z_hi'=8,'z_lo'=2,'y_hi'=2] {'y_lo','x'}, dimensions={0} | all-to-all | bytes 1572864 | tf_op jit(solution)/shard_map/all_to_all | solution.py:306
  100.5 0.0 copy-start.2
  100.5 0.4 middle.1
  100.9 15.0 %all_to_all.31.mine_ref = bf16[8,128,384]{2,1,0:T(8,128)(2,1)S(1)} all-to-all(bf16[8,128,384]{2,1,0:T(8,128)(2,1)S(1)} %middle.1), channel_id=1, replica_groups=mesh['y_lo'=2,'x'=4,'core'=2,'z_hi'=8,'z_lo'=2,'y_hi'=2] {'y_lo','x'}, dimensions={0} | all-to-all | bytes 1572864 | tf_op jit(solution)/shard_map/all_to_all | solution.py:306
  115.9 1.9 collective-permute-start.3
  117.8 2.3 %collective-permute-done.3.far_ref.other_ref = bf16[8,128,384]{2,1,0:T(8,128)(2,1)S(1)} collective-permute-done((bf16[8,128,384]{2,1,0:T(8,128)(2,1)S(1)}, bf16[8,128,384]{2,1,0:T(8,128)(2,1)S(1)}, u32[]{:S(2)}, u32[]{:S(2)}) %collective-permute-start.3) | collective-permute-done | bytes 786464 | tf_op jit(solution)/shard_map/ppermute | solution.py:319
  120.1 0.0 copy-done.2
  120.1 2.2 %weigh.1 = bf16[8,3,320,128]{3,2,1,0:T(8,128)(2,1)} custom-call(s32[8]{0:T(128)S(1)} %and_select_fusion.expert_ref, s32[1]{0:T(128)} %bitcast.half_ref.core_ref, bf16[2,4,320,256]{3,2,1,0:T(8,128)(2,1)S(1)} %copy-done.2, bf16[8,128,384]{2,1,0:T(8,128)(2,1)S(1)} %all_to_all.31.mine_ref, bf16[8,128,384]{2,1,0:T(8,128)(2,1)S(1)} %collective-permute-done.3.far_ref.other_ref), custom_call_target="tpu_custom_call" | custom-call | tf_op jit(solution)/shard_map/weigh/pallas_call | solution.py:191
  122.3 0.0 reduce-scatter.2.cloned.1.call-update
  122.3 3.7 %last.1 = (bf16[32,32,384]{2,1,0:T(8,128)(2,1)S(1)}, bf16[32,32,384]{2,1,0:T(8,128)(2,1)S(1)}) custom-call(s32[8]{0:T(128)S(1)} %and_select_fusion.expert_ref, s32[1]{0:T(128)} %bitcast.half_ref.core_ref, bf16[8,3,320,128]{3,2,1,0:T(8,128)(2,1)S(1)} %bitcast.24, bf16[8,128,384]{2,1,0:T(8,128)(2,1)S(1)} %all_to_all.31.mine_ref, ...), custom_call_target="tpu_custom_call" | custom-call | tf_op jit(solution)/shard_map/last/pallas_call | solution.py:232
  126.0 0.0 copy-start.3
  126.0 17.2 %all_to_all.32.recv_ref = bf16[32,32,384]{2,1,0:T(8,128)(2,1)S(1)} all-to-all(bf16[32,32,384]{2,1,0:T(8,128)(2,1)S(1)} %get-tuple-element.14), channel_id=1, replica_groups=mesh['y_lo'=2,'x'=4,'core'=2,'z_hi'=8,'z_lo'=2,'y_hi'=2] {'y_hi','y_lo',..., dimensions={0} | all-to-all | bytes 1572864 | tf_op jit(solution)/shard_map/all_to_all | solution.py:306
  143.2 0.0 copy-done.3
  143.2 6.5 %all-to-all-start.4 = ((bf16[32,32,384]{2,1,0:T(8,128)(2,1)}), bf16[32,32,384]{2,1,0:T(8,128)(2,1)S(1)}, u32[]{:S(2)}, u32[]{:S(2)}) async-start(bf16[32,32,384]{2,1,0:T(8,128)(2,1)} %copy-done.3), calls=%async_computation.4 | async-start | bytes 1572864 | tf_op jit(solution)/shard_map/all_to_all | solution.py:306
  149.7 0.1 unpack_other.1
  149.9 3.5 %collective-permute-start.4 = (bf16[2,16,5120]{2,1,0:T(8,128)(2,1)S(1)}, bf16[2,16,5120]{2,1,0:T(8,128)(2,1)S(1)}, u32[]{:S(2)}, u32[]{:S(2)}) collective-permute-start(bf16[2,16,5120]{2,1,0:T(8,128)(2,1)S(1)} %unpack_other.1), channel_id=1, source_target_pairs={{0,2},{2,0},{1,3},{3,1},{4,6},{6,4},{5,7},{7,5},{8,10},{10,8},{9,1... | collective-permute-start | bytes 983048 | tf_op jit(solution)/shard_map/ppermute | solution.py:319
  153.4 8.2 %all-to-all-done.4.recv_ref = bf16[32,32,384]{2,1,0:T(8,128)(2,1)S(1)} async-done(((bf16[32,32,384]{2,1,0:T(8,128)(2,1)}), bf16[32,32,384]{2,1,0:T(8,128)(2,1)S(1)}, u32[]{:S(2)}, u32[]{:S(2)}) %all-to-all-start.4) | async-done | bytes 786464 | tf_op jit(solution)/shard_map/all_to_all | solution.py:306
  161.6 15.7 %collective-permute-done.4.add_ref = bf16[2,16,5120]{2,1,0:T(8,128)(2,1)S(1)} collective-permute-done((bf16[2,16,5120]{2,1,0:T(8,128)(2,1)S(1)}, bf16[2,16,5120]{2,1,0:T(8,128)(2,1)S(1)}, u32[]{:S(2)}, u32[]{:S(2)}) %collective-permute-start.4) | collective-permute-done | bytes 327712 | tf_op jit(solution)/shard_map/ppermute | solution.py:319
  177.3 0.9 unpack_own.1
  178.1 7.9 %reduce-scatter.2.cloned.1.call-done = bf16[960,128]{1,0:T(8,128)(2,1)} async-done(((bf16[7680,128]{1,0:T(8,128)(2,1)}), bf16[960,128]{1,0:T(8,128)(2,1)}) %reduce-scatter.2.cloned.1.call-update) | async-done | bytes 245776 | tf_op jit(solution)/shard_map/reduce_scatter | solution.py:315
  186.1 1.7 widen.1
  (1 shorter events, 0.0 us)
Async XLA Ops:
  7.2 68.2 %all-gather.2.cloned.1.call-start = ((), (), s32[]{:S(2)}) async-start(), calls=%async_computation.7 | async-start | bytes 2211840 | tf_op jit(solution)/shard_map/all_gather | solution.py:310
  9.9 17.5 %collective-permute-start.1 = (bf16[2,16,5120]{2,1,0:T(8,128)(2,1)S(1)}, bf16[2,16,5120]{2,1,0:T(8,128)(2,1)S(1)}, u32[]{:S(2)}, u32[]{:S(2)}) collective-permute-start(bf16[2,16,5120]{2,1,0:T(8,128)(2,1)S(1)} %pad_maximum_fusion), channel_id=1, source_target_pairs={{0,2},{2,0},{1,3},{3,1},{4,6},{6,4},{5,7},{7,5},{8,10},{10,8},{9,1... | collective-permute-start | bytes 983048 | tf_op jit(solution)/shard_map/ppermute | solution.py:319
  12.7 13.5 %collective-permute-start = (s32[1,20]{1,0:T(1,128)S(1)}, s32[1,20]{1,0:T(1,128)S(1)}, u32[]{:S(2)}, u32[]{:S(2)}) collective-permute-start(s32[1,20]{1,0:T(1,128)S(1)} %add_bitcast_fusion), channel_id=1, source_target_pairs={{0,2},{2,0},{1,3},{3,1},{4,6},{6,4},{5,7},{7,5},{8,10},{10,8},{9,1... | collective-permute-start | bytes 248 | tf_op jit(solution)/shard_map/ppermute | solution.py:319
  18.8 19.3 %all-to-all-start = ((bf16[32,32,384]{2,1,0:T(8,128)(2,1)}), bf16[32,32,384]{2,1,0:T(8,128)(2,1)S(1)}, u32[]{:S(2)}, u32[]{:S(2)}) async-start(bf16[32,32,384]{2,1,0:T(8,128)(2,1)} %pack.2), calls=%async_computation | async-start | bytes 1572864 | tf_op jit(solution)/shard_map/all_to_all | solution.py:306
  27.5 17.3 %copy-start.4 = (s32[32]{0:T(128)S(1)}, s32[32]{0:T(128)}, u32[]{:S(2)}) copy-start(s32[32]{0:T(128)} %param.11) | copy-start | bytes 388
  38.1 18.4 %all-to-all-start.1 = ((bf16[32,32,384]{2,1,0:T(8,128)(2,1)}), bf16[32,32,384]{2,1,0:T(8,128)(2,1)S(1)}, u32[]{:S(2)}, u32[]{:S(2)}) async-start(bf16[32,32,384]{2,1,0:T(8,128)(2,1)} %pack.3), calls=%async_computation.1 | async-start | bytes 1572864 | tf_op jit(solution)/shard_map/all_to_all | solution.py:306
  44.7 141.4 %reduce-scatter.2.cloned.1.call-start = ((), (), s32[]{:S(2)}) async-start(), calls=%async_computation.8 | async-start | bytes 2211840 | tf_op jit(solution)/shard_map/reduce_scatter | solution.py:315
  57.4 1.1 copy-start.1
  75.3 4.1 %copy-start = (bf16[7680,128]{1,0:T(8,128)(2,1)S(1)}, bf16[7680,128]{1,0:T(8,128)(2,1)}, u32[]{:S(2)}) copy-start(bf16[7680,128]{1,0:T(8,128)(2,1)} %all-gather.2.cloned.1.call-done) | copy-start | bytes 5898244
  77.5 4.2 %collective-permute-start.2 = (bf16[8,128,384]{2,1,0:T(8,128)(2,1)S(1)}, bf16[8,128,384]{2,1,0:T(8,128)(2,1)S(1)}, u32[]{:S(2)}, u32[]{:S(2)}) collective-permute-start(bf16[8,128,384]{2,1,0:T(8,128)(2,1)S(1)} %first.3), channel_id=1, source_target_pairs={{0,32},{32,0},{1,33},{33,1},{2,34},{34,2},{3,35},{35,3},{4,36},{36... | collective-permute-start | bytes 2359304 | tf_op jit(solution)/shard_map/ppermute | solution.py:319
  100.5 19.6 %copy-start.2 = (bf16[2,4,320,256]{3,2,1,0:T(8,128)(2,1)S(1)}, bf16[2,4,320,256]{3,2,1,0:T(8,128)(2,1)}, u32[]{:S(2)}) copy-start(bf16[2,4,320,256]{3,2,1,0:T(8,128)(2,1)} %copy-done.1) | copy-start | bytes 3932164
  115.9 4.2 %collective-permute-start.3 = (bf16[8,128,384]{2,1,0:T(8,128)(2,1)S(1)}, bf16[8,128,384]{2,1,0:T(8,128)(2,1)S(1)}, u32[]{:S(2)}, u32[]{:S(2)}) collective-permute-start(bf16[8,128,384]{2,1,0:T(8,128)(2,1)S(1)} %all_to_all.31.mine_ref), channel_id=1, source_target_pairs={{0,32},{32,0},{1,33},{33,1},{2,34},{34,2},{3,35},{35,3},{4,36},{36... | collective-permute-start | bytes 2359304 | tf_op jit(solution)/shard_map/ppermute | solution.py:319
  126.0 17.2 %copy-start.3 = (bf16[32,32,384]{2,1,0:T(8,128)(2,1)}, bf16[32,32,384]{2,1,0:T(8,128)(2,1)S(1)}, u32[]{:S(2)}) copy-start(bf16[32,32,384]{2,1,0:T(8,128)(2,1)S(1)} %get-tuple-element.13) | copy-start | bytes 2359300
  143.2 18.4 %all-to-all-start.4 = ((bf16[32,32,384]{2,1,0:T(8,128)(2,1)}), bf16[32,32,384]{2,1,0:T(8,128)(2,1)S(1)}, u32[]{:S(2)}, u32[]{:S(2)}) async-start(bf16[32,32,384]{2,1,0:T(8,128)(2,1)} %copy-done.3), calls=%async_computation.4 | async-start | bytes 1572864 | tf_op jit(solution)/shard_map/all_to_all | solution.py:306
  149.9 27.4 %collective-permute-start.4 = (bf16[2,16,5120]{2,1,0:T(8,128)(2,1)S(1)}, bf16[2,16,5120]{2,1,0:T(8,128)(2,1)S(1)}, u32[]{:S(2)}, u32[]{:S(2)}) collective-permute-start(bf16[2,16,5120]{2,1,0:T(8,128)(2,1)S(1)} %unpack_other.1), channel_id=1, source_target_pairs={{0,2},{2,0},{1,3},{3,1},{4,6},{6,4},{5,7},{7,5},{8,10},{10,8},{9,1... | collective-permute-start | bytes 983048 | tf_op jit(solution)/shard_map/ppermute | solution.py:319
Sparse Core Ops, SparseCore 0:
  10.6 64.6 all-gather.1
  122.4 63.6 reduce-scatter.1
